TPU v7x, 32 devices: a whole 2x2x4 slice. The times are simulated.
32 devices in a mesh: clips: 2 (over x), tile: 4 (over y, core), tm: 4 (over z).
Axes of the slice: x: 2, y: 2, z: 4, core: 2. Of those that a mesh axis runs over, the one named last changes fastest.
Arguments:
- clip_frames: bfloat16 [16, 16, 128, 256], P(('clips', 'tm'), 'tile'), parts along dimension 0, may hold values from -6 to 6
- weight_first: bfloat16 [3, 3, 3, 256, 256], replicated, may hold values from -0.078125 to 0.078125
- bias_first: float32 [256], replicated, may hold values from -3 to 3
- weight_second: bfloat16 [3, 3, 3, 256, 256], replicated, may hold values from -0.078125 to 0.078125
- bias_second: float32 [256], replicated, may hold values from -3 to 3
Outputs:
- pooled_frames: bfloat16 [8, 16, 128, 256], P(('clips', 'tm'), 'tile'), parts along dimension 0
There are 2 independent parts, one for each index of `clips`. A program takes and returns all parts, laid end to end along the dimension named above; an argument that names none is the same for every part. Nothing has to cross between parts.
All inputs are finite; a program needn't handle non-finite values.
Results may differ from a plain program's by a relative error of at most 0.0029.
Values may be sent and summed in bfloat16 or wider, within the bound.
No kernel may reach another device: no remote copies, remote signals or barrier semaphores. Data moves between devices by JAX's collectives and lax.ppermute only.
A program may use at most 128 MiB of HBM per device.

v0:
```python
import functools

import jax
import jax.numpy as jnp
from jax import lax
from jax.experimental import pallas as pl
from jax.experimental.pallas import tpu as pltpu
from jax.sharding import PartitionSpec as P


VMEM = pl.BlockSpec(memory_space=pltpu.VMEM)
HBM = pl.BlockSpec(memory_space=pltpu.HBM)


def call(body, outs, args, flops, in_specs=None, scratch=()):
    return pl.pallas_call(
        body,
        out_shape=outs,
        in_specs=in_specs or [VMEM] * len(args),
        out_specs=[VMEM] * len(outs),
        scratch_shapes=scratch,
        compiler_params=pltpu.CompilerParams(vmem_limit_bytes=16 << 20),
        cost_estimate=pl.CostEstimate(flops=flops, bytes_accessed=0, transcendentals=0),
    )(*args)


def flat(value):
    return value.reshape(-1, value.shape[-1])


def row_taps(slab, rows):
    return [flat(slab[p : p + rows]) for p in range(3)]


def convolved(lhs, weights, rows, cols):
    stacked = jnp.concatenate(lhs, axis=1)
    total = None
    for q in range(3):
        taps = jnp.concatenate([w[q] for w in weights], axis=0)
        part = jnp.dot(stacked, taps, preferred_element_type=jnp.float32)
        part = part.reshape(rows, cols, part.shape[-1])
        if q != 1:
            col = lax.broadcasted_iota(jnp.int32, part.shape, 1)
            edge = 0 if q == 0 else cols - 1
            part = jnp.where(col == edge, 0.0, pltpu.roll(part, 1 if q == 0 else cols - 1, 1))
        total = part if total is None else total + part
    return total


def parity():
    return lax.rem(lax.axis_index("tile"), 2)


def either(first, second):
    even = parity() == 0
    return jnp.concatenate([jnp.where(even, a, b) for a, b in zip(first, second)], axis=0)


def own_edge(own, side):
    odd = parity()
    last = own.shape[0] - 2
    return own[pl.ds((odd if side == 0 else 1 - odd) * last, 2)]


def outer_slab(outer, own, tiles):
    tile = lax.axis_index("tile")
    beyond = (tile == 0) | ((tile == tiles - 1) & (parity() == 1))
    outer = jnp.where(beyond, jnp.zeros_like(outer), outer)
    edge = own_edge(own, 0)
    return either([outer, edge], [edge, outer])


def inner_slab(inner, own):
    edge = own_edge(own, 1)
    return either([edge, inner], [inner, edge])


def places(rows):
    odd = parity()
    return pl.ds(2, rows - 2), pl.ds((1 - odd) * rows, 2), pl.ds(odd * rows, 2)


def weight_rows(w_ref, a):
    return [[w_ref[a, p, q] for q in range(3)] for p in range(3)]


def silu_rows(value, start, rows, tiles):
    hidden = (value / (1.0 + jnp.exp(-value))).astype(jnp.bfloat16)
    row = lax.broadcasted_iota(jnp.int32, hidden.shape, 0) + start
    row = row + lax.axis_index("tile") * rows - 1
    inside = (row >= 0) & (row < tiles * rows)
    return jnp.where(inside, hidden, jnp.zeros_like(hidden))


def edges_body(x_ref, own_ref, outer_ref, inner_ref, sem):
    copy = pltpu.make_async_copy(x_ref, own_ref, sem)
    copy.start()
    copy.wait()
    for f in range(2):
        outer_ref[f] = own_edge(own_ref.at[f], 0)
        inner_ref[f] = own_edge(own_ref.at[f], 1)


def turn_body(m_ref, inner_ref):
    for f in range(2):
        inner_ref[f] = own_edge(m_ref.at[f], 1)


def own_sums(slabs, w_ref, b_ref, acc0_ref, acc1_ref):
    rows, cols = acc0_ref.shape[:2]
    taps = [row_taps(slab, rows) for slab in slabs]
    acc0_ref[...] = b_ref[...] + convolved(taps[0], weight_rows(w_ref, 2), rows, cols)
    weights = weight_rows(w_ref, 1) + weight_rows(w_ref, 2)
    acc1_ref[...] = b_ref[...] + convolved(taps[0] + taps[1], weights, rows, cols)


def own_near_body(x_ref, inner_ref, w_ref, b_ref, acc0_ref, acc1_ref):
    even = parity() == 0
    slabs = []
    for f in range(2):
        below = jnp.concatenate([x_ref[f], inner_ref[f]], axis=0)
        above = jnp.concatenate([inner_ref[f], x_ref[f]], axis=0)
        slabs.append(jnp.where(even, below, above))
    own_sums(slabs, w_ref, b_ref, acc0_ref, acc1_ref)


def own_far_body(tiles, x_ref, outer_ref, w_ref, b_ref, acc0_ref, acc1_ref):
    slabs = [outer_slab(outer_ref[f], x_ref.at[f], tiles) for f in range(2)]
    own_sums(slabs, w_ref, b_ref, acc0_ref, acc1_ref)


def hidden(slab, bases, places_of, w_ref, tiles, whole, h0_ref, h1_ref, sum0_ref, sum1_ref):
    rows, cols = sum0_ref.shape[:2]
    started = lax.axis_index("tm") > 0

    @pl.when(started)
    def _():
        taps = [row_taps(slab(f), rows) for f in range(2)]
        weights = weight_rows(w_ref, 0) + weight_rows(w_ref, 1)
        sum0_ref[...] = bases[0]() + convolved(taps[0] + taps[1], weights, rows, cols)
        sum1_ref[...] = bases[1]() + convolved(taps[1], weight_rows(w_ref, 0), rows, cols)

    @pl.when(jnp.logical_not(started))
    def _():
        sum0_ref[...] = bases[0]()
        sum1_ref[...] = bases[1]()

    h0_ref[...] = silu_rows(sum0_ref[...], places_of.start, whole, tiles)
    h1_ref[...] = silu_rows(sum1_ref[...], places_of.start, whole, tiles)


def from_near(acc_ref, start, rows):
    return lambda: acc_ref[pl.ds(start, rows)]


def middle_body(tiles, m_ref, w_ref, _, acc0_ref, acc1_ref, h0_ref, h1_ref, sum0_ref, sum1_ref):
    rows = m_ref.shape[1]
    start = 2 * parity()
    bases = [from_near(acc_ref, start, rows - 2) for acc_ref in (acc0_ref, acc1_ref)]
    place = places(rows)[0]
    hidden(lambda f: m_ref[f], bases, place, w_ref, tiles, rows, h0_ref, h1_ref, sum0_ref, sum1_ref)


def partial_rows(times, h0, h1, v_ref, rows, cols, send_ref):
    has_next = lax.axis_index("tm") < times - 1

    @pl.when(has_next)
    def _():
        both = (h0.astype(jnp.float32) + h1.astype(jnp.float32)).astype(jnp.bfloat16)
        taps = row_taps(both, rows) + row_taps(h1, rows)
        part = convolved(taps, weight_rows(v_ref, 0) + weight_rows(v_ref, 1), rows, cols)
        send_ref[...] = part.astype(jnp.bfloat16)

    @pl.when(jnp.logical_not(has_next))
    def _():
        send_ref[...] = jnp.zeros_like(send_ref)


def near_body(
    tiles, times, m_ref, inner_ref, w_ref, v_ref, acc0_ref, acc1_ref, mid0_ref, mid1_ref,
    send_ref, h0_ref, h1_ref, sum0_ref, sum1_ref,
):
    rows, cols = m_ref.shape[1:3]
    odd = parity()
    start = (1 - odd) * (rows - 2)
    bases = [from_near(acc_ref, start, 2) for acc_ref in (acc0_ref, acc1_ref)]
    place = places(rows)[1]

    def slab(f):
        return inner_slab(inner_ref[f], m_ref.at[f])

    middle, near = pl.ds(2 * odd, rows - 2), pl.ds(start, 2)
    h0_ref[middle], h1_ref[middle] = mid0_ref[...], mid1_ref[...]
    hidden(
        slab, bases, place, w_ref, tiles, rows, h0_ref.at[near], h1_ref.at[near], sum0_ref,
        sum1_ref,
    )
    partial_rows(times, h0_ref[...], h1_ref[...], v_ref, rows - 2, cols, send_ref)


def far_body(
    tiles, times, m_ref, outer_ref, w_ref, v_ref, acc0_ref, acc1_ref, near0_ref, near1_ref,
    send_ref, h0_ref, h1_ref, sum0_ref, sum1_ref,
):
    rows, cols = m_ref.shape[1:3]
    odd = parity()
    far = places(rows)[2]
    near = pl.ds(2 * (1 - odd), rows)

    def slab(f):
        return outer_slab(outer_ref[f], m_ref.at[f], tiles)

    bases = [lambda: acc0_ref[...], lambda: acc1_ref[...]]
    h0_ref[near], h1_ref[near] = near0_ref[...], near1_ref[...]
    hidden(
        slab, bases, far, w_ref, tiles, rows, h0_ref.at[far], h1_ref.at[far], sum0_ref, sum1_ref
    )
    side = pl.ds(odd * (rows - 2), 4)
    partial_rows(times, h0_ref[side], h1_ref[side], v_ref, 2, cols, send_ref)


def rest_body(x_ref, h0_ref, h1_ref, v_ref, b_ref, out_ref):
    rows, cols = x_ref.shape[1:3]
    h0, h1 = h0_ref[...], h1_ref[...]
    both = (h0.astype(jnp.float32) + h1.astype(jnp.float32)).astype(jnp.bfloat16)
    taps = row_taps(h0, rows) + row_taps(both, rows)
    part = convolved(taps, weight_rows(v_ref, 1) + weight_rows(v_ref, 2), rows, cols)
    total = x_ref[0].astype(jnp.float32) + x_ref[1].astype(jnp.float32) + part
    out_ref[0] = total * 0.5 + b_ref[...]


def join_body(rest_ref, near_ref, far_ref, out_ref):
    rows = rest_ref.shape[1]
    odd = parity()
    first = lax.axis_index("tm") == 0
    for part_ref, start in ((near_ref, 2 * (1 - odd)), (far_ref, odd * (rows - 2))):
        part = part_ref[...].astype(jnp.float32)
        part = jnp.where(first, jnp.zeros_like(part), part)
        place = pl.ds(start, part.shape[0])
        out_ref[0, place] = (rest_ref[0, place] + 0.5 * part).astype(jnp.bfloat16)


def block(x, weight_first, bias_first, weight_second, bias_second):
    _, rows, cols, channels = x.shape
    tiles, times = lax.axis_size("tile"), lax.axis_size("tm")
    forward = [(i, i + 1) for i in range(times - 1)]
    ring = forward + [(times - 1, 0)]
    inner_pairs = [(i, i + 1) for i in range(0, tiles - 1, 2)]
    outer_pairs = [(i, i + 1) for i in range(1, tiles - 1, 2)]
    inner_pairs += [(j, i) for i, j in inner_pairs]
    outer_pairs += [(j, i) for i, j in outer_pairs]
    unpaired = [(0, tiles - 1), (tiles - 1, 0)] if tiles % 2 == 0 else []
    diagonal = [(i * times + s, j * times + t) for i, j in outer_pairs for s, t in forward]

    def frames(*lead, dtype=jnp.bfloat16):
        return jax.ShapeDtypeStruct((*lead, cols, channels), dtype)

    f32 = jnp.float32
    earlier = lax.ppermute(x, "tm", ring)
    x, outer_edge, inner_edge = call(
        edges_body,
        [frames(2, rows), frames(2, 2), frames(2, 2)],
        (pltpu.with_memory_space_constraint(x, pltpu.HBM),),
        10**10,
        in_specs=[HBM],
        scratch=[pltpu.SemaphoreType.DMA(())],
    )
    inner = lax.ppermute(inner_edge, "tile", inner_pairs)
    outer = lax.ppermute(outer_edge, "tile", outer_pairs + unpaired)
    corner = lax.ppermute(outer_edge, ("tile", "tm"), diagonal)

    bias_first = bias_first.reshape(1, 1, -1)
    bias_second = bias_second.reshape(1, 1, -1)
    unit = 2 * 9 * channels * channels * cols
    wide = rows + 2
    sums0, sums1 = call(
        own_near_body,
        [frames(rows, dtype=f32), frames(rows, dtype=f32)],
        (x, inner, weight_first, bias_first),
        3 * unit * rows,
    )
    far0, far1 = call(
        functools.partial(own_far_body, tiles),
        [frames(2, dtype=f32), frames(2, dtype=f32)],
        (x, outer, weight_first, bias_first),
        0,
    )
    (inner_edge,) = call(turn_body, [frames(2, 2)], (earlier,), 0)
    inner_corner = lax.ppermute(inner_edge, "tile", inner_pairs)

    def sums(count):
        return [pltpu.VMEM((count, cols, channels), f32)] * 2

    mid0, mid1 = call(
        functools.partial(middle_body, tiles),
        [frames(rows - 2), frames(rows - 2)],
        (earlier, weight_first, weight_second, sums0, sums1),
        0,
        scratch=sums(rows - 2),
    )
    near_send, near0, near1 = call(
        functools.partial(near_body, tiles, times),
        [frames(rows - 2), frames(rows), frames(rows)],
        (earlier, inner_corner, weight_first, weight_second, sums0, sums1, mid0, mid1),
        0,
        scratch=sums(2),
    )
    near_part = lax.ppermute(near_send, "tm", ring)
    far_send, h0, h1 = call(
        functools.partial(far_body, tiles, times),
        [frames(2), frames(wide), frames(wide)],
        (earlier, corner, weight_first, weight_second, far0, far1, near0, near1),
        0,
        scratch=sums(2),
    )
    far_part = lax.ppermute(far_send, "tm", ring)
    (rest,) = call(
        rest_body,
        [frames(1, rows, dtype=f32)],
        (x, h0, h1, weight_second, bias_second),
        2 * unit * rows,
    )
    (pooled,) = call(join_body, [frames(1, rows)], (rest, near_part, far_part), 0)
    return pooled


def solution(mesh):
    in_specs = (P(("clips", "tm"), "tile", None, None), P(), P(), P(), P())
    out_specs = P(("clips", "tm"), "tile", None, None)
    return jax.shard_map(block, mesh=mesh, in_specs=in_specs, out_specs=out_specs, check_vma=False)
```

profile of v0, /device:TPU:1, one launch (start us, length us, event | category | flops | bytes accessed | tf_op | source)
XLA Modules:
  0.0 36.1 jit_solution(10261815195564259491)
XLA Ops:
  0.0 0.0 copy-start.2
  0.0 0.0 copy-start
  0.0 2.1 %collective-permute-start = (bf16[2,4,128,256]{3,2,1,0:T(8,128)(2,1)}, bf16[2,4,128,256]{3,2,1,0:T(8,128)(2,1)S(1)}, u32[]{:S(2)}, u32[]{:S(2)}) collective-permute-start(bf16[2,4,128,256]{3,2,1,0:T(8,128)(2,1)} %x_ref.1), channel_id=1, source_target_pairs={{0,1},{1,2},{2,3},{3,0},{4,5},{5,6},{6,7},{7,4},{8,9},{9,10},{10,1... | collective-permute-start | bytes 1572872 | tf_op jit(solution)/shard_map/ppermute | solution.py:259
  2.1 1.1 %shard_map.55 = (bf16[2,4,128,256]{3,2,1,0:T(8,128)(2,1)S(1)}, bf16[2,2,128,256]{3,2,1,0:T(8,128)(2,1)S(1)}, bf16[2,2,128,256]{3,2,1,0:T(8,128)(2,1)S(1)}) custom-call(bf16[2,4,128,256]{3,2,1,0:T(8,128)(2,1)} %x_ref.1), custom_call_target="tpu_custom_call" | custom-call | flops 10000000000 | tf_op jit(solution)/shard_map/pallas_call | solution.py:16
  3.2 2.1 %collective-permute-start.2 = (bf16[2,2,128,256]{3,2,1,0:T(8,128)(2,1)S(1)}, bf16[2,2,128,256]{3,2,1,0:T(8,128)(2,1)S(1)}, u32[]{:S(2)}, u32[]{:S(2)}) collective-permute-start(bf16[2,2,128,256]{3,2,1,0:T(8,128)(2,1)S(1)} %get-tuple-element.21), channel_id=1, source_target_pairs={{4,8},{8,4},{0,12},{12,0},{5,9},{9,5},{1,13},{13,1},{6,10},{10,6},... | collective-permute-start | bytes 786440 | tf_op jit(solution)/shard_map/ppermute | solution.py:269
  5.4 0.0 collective-permute-start.4
  5.4 10.6 %collective-permute-done.m_ref = bf16[2,4,128,256]{3,2,1,0:T(8,128)(2,1)S(1)} collective-permute-done((bf16[2,4,128,256]{3,2,1,0:T(8,128)(2,1)}, bf16[2,4,128,256]{3,2,1,0:T(8,128)(2,1)S(1)}, u32[]{:S(2)}, u32[]{:S(2)}) %collective-permute-start) | collective-permute-done | bytes 524320 | tf_op jit(solution)/shard_map/ppermute | solution.py:259
  16.0 1.3 %collective-permute-start.3 = (bf16[2,2,128,256]{3,2,1,0:T(8,128)(2,1)S(1)}, bf16[2,2,128,256]{3,2,1,0:T(8,128)(2,1)S(1)}, u32[]{:S(2)}, u32[]{:S(2)}) collective-permute-start(bf16[2,2,128,256]{3,2,1,0:T(8,128)(2,1)S(1)} %shard_map.57), channel_id=1, source_target_pairs={{0,4},{8,12},{4,0},{12,8},{1,5},{9,13},{5,1},{13,9},{2,6},{10,14},... | collective-permute-start | bytes 786440 | tf_op jit(solution)/shard_map/ppermute | solution.py:289
  17.3 2.2 %collective-permute-start.1 = (bf16[2,2,128,256]{3,2,1,0:T(8,128)(2,1)S(1)}, bf16[2,2,128,256]{3,2,1,0:T(8,128)(2,1)S(1)}, u32[]{:S(2)}, u32[]{:S(2)}) collective-permute-start(bf16[2,2,128,256]{3,2,1,0:T(8,128)(2,1)S(1)} %get-tuple-element.21), channel_id=1, source_target_pairs={{4,9},{5,10},{6,11},{8,5},{9,6},{10,7},{20,25},{21,26},{22,27},{24... | collective-permute-start | bytes 786440 | tf_op jit(solution)/shard_map/ppermute | solution.py:270
  19.5 0.0 collective-permute-done.2.outer_ref
  19.5 0.0 copy-done.2
  19.6 0.0 copy-done
  19.6 1.1 %shard_map.56 = (f32[2,128,256]{2,1,0:T(8,128)S(1)}, f32[2,128,256]{2,1,0:T(8,128)S(1)}) custom-call(bf16[2,4,128,256]{3,2,1,0:T(8,128)(2,1)S(1)} %get-tuple-element.20.x_ref, bf16[2,2,128,256]{3,2,1,0:T(8,128)(2,1)S(1)} %collective-permute-done.2.outer_ref, bf16[3,3,3,256,256]{4,3,2,1,0:T(8,128)(2,1)S(1)} %copy-done, f32[1,1,256]{2,1,0:T(1,128)S(1)} %bitcast.2), custom_call_target="tpu_custom_call" | custom-call | tf_op jit(solution)/shard_map/pallas_call | solution.py:16
  20.7 0.0 copy-start.1
  20.7 0.0 collective-permute-done.4.inner_ref
  20.7 2.0 %shard_map.58 = (f32[4,128,256]{2,1,0:T(8,128)S(1)}, f32[4,128,256]{2,1,0:T(8,128)S(1)}) custom-call(bf16[2,4,128,256]{3,2,1,0:T(8,128)(2,1)S(1)} %get-tuple-element.20.x_ref, bf16[2,2,128,256]{3,2,1,0:T(8,128)(2,1)S(1)} %collective-permute-done.4.inner_ref, bf16[3,3,3,256,256]{4,3,2,1,0:T(8,128)(2,1)S(1)} %copy-done, f32[1,1,256]{2,1,0:T(1,128)S(1)} %bitcast.3), custom_call_target="tpu_custom_call" | custom-call | flops 1811939328 | tf_op jit(solution)/shard_map/pallas_call | solution.py:16
  22.7 0.0 copy-done.1
  22.7 0.2 shard_map.59
  22.9 0.0 collective-permute-done.3.inner_ref
  22.9 1.1 %shard_map.60 = (bf16[2,128,256]{2,1,0:T(8,128)(2,1)S(1)}, bf16[4,128,256]{2,1,0:T(8,128)(2,1)S(1)}, bf16[4,128,256]{2,1,0:T(8,128)(2,1)S(1)}) custom-call(bf16[2,4,128,256]{3,2,1,0:T(8,128)(2,1)S(1)} %collective-permute-done.m_ref, bf16[2,2,128,256]{3,2,1,0:T(8,128)(2,1)S(1)} %collective-permute-done.3.inner_ref, bf16[3,3,3,256,256]{4,3,2,1,0:T(8,128)(2,1)S(1)} %copy-done, ...), custom_call_target="tpu_custom_call" | custom-call | tf_op jit(solution)/shard_map/pallas_call | solution.py:16
  24.0 0.0 collective-permute-done.1.outer_ref
  24.0 0.0 copy-start.3
  24.0 1.1 %shard_map.61 = (bf16[2,128,256]{2,1,0:T(8,128)(2,1)S(1)}, bf16[6,128,256]{2,1,0:T(8,128)(2,1)S(1)}, bf16[6,128,256]{2,1,0:T(8,128)(2,1)S(1)}) custom-call(bf16[2,4,128,256]{3,2,1,0:T(8,128)(2,1)S(1)} %collective-permute-done.m_ref, bf16[2,2,128,256]{3,2,1,0:T(8,128)(2,1)S(1)} %collective-permute-done.1.outer_ref, bf16[3,3,3,256,256]{4,3,2,1,0:T(8,128)(2,1)S(1)} %copy-done, ...), custom_call_target="tpu_custom_call" | custom-call | tf_op jit(solution)/shard_map/pallas_call | solution.py:16
  25.2 4.5 %collective-permute-start.6 = (bf16[2,128,256]{2,1,0:T(8,128)(2,1)S(1)}, bf16[2,128,256]{2,1,0:T(8,128)(2,1)S(1)}, u32[]{:S(2)}, u32[]{:S(2)}) collective-permute-start(bf16[2,128,256]{2,1,0:T(8,128)(2,1)S(1)} %get-tuple-element.34), channel_id=1, source_target_pairs={{0,1},{1,2},{2,3},{3,0},{4,5},{5,6},{6,7},{7,4},{8,9},{9,10},{10,1... | collective-permute-start | bytes 393224 | tf_op jit(solution)/shard_map/ppermute | solution.py:316
  29.7 1.3 %collective-permute-start.5 = (bf16[2,128,256]{2,1,0:T(8,128)(2,1)S(1)}, bf16[2,128,256]{2,1,0:T(8,128)(2,1)S(1)}, u32[]{:S(2)}, u32[]{:S(2)}) collective-permute-start(bf16[2,128,256]{2,1,0:T(8,128)(2,1)S(1)} %get-tuple-element.33), channel_id=1, source_target_pairs={{0,1},{1,2},{2,3},{3,0},{4,5},{5,6},{6,7},{7,4},{8,9},{9,10},{10,1... | collective-permute-start | bytes 393224 | tf_op jit(solution)/shard_map/ppermute | solution.py:308
  31.0 0.0 copy-done.3
  31.0 1.4 %shard_map.62.rest_ref = f32[1,4,128,256]{3,2,1,0:T(8,128)S(1)} custom-call(bf16[2,4,128,256]{3,2,1,0:T(8,128)(2,1)S(1)} %get-tuple-element.20.x_ref, bf16[6,128,256]{2,1,0:T(8,128)(2,1)S(1)} %get-tuple-element.31.h0_ref, bf16[6,128,256]{2,1,0:T(8,128)(2,1)S(1)} %get-tuple-element.32.h1_ref, bf16[3,3,3,256,256]{4,3,2,1,0:T(8,128)(2,1)S(1)} %copy-done.1, ...), custom_call_target="tpu_custom_call" | custom-call | flops 1207959552 | tf_op jit(solution)/shard_map/pallas_call | solution.py:16
  32.4 0.0 collective-permute-done.6.far_ref
  32.4 2.9 %collective-permute-done.5.near_ref = bf16[2,128,256]{2,1,0:T(8,128)(2,1)S(1)} collective-permute-done((bf16[2,128,256]{2,1,0:T(8,128)(2,1)S(1)}, bf16[2,128,256]{2,1,0:T(8,128)(2,1)S(1)}, u32[]{:S(2)}, u32[]{:S(2)}) %collective-permute-start.5) | collective-permute-done | bytes 131104 | tf_op jit(solution)/shard_map/ppermute | solution.py:308
  35.3 0.8 %shard_map.63 = bf16[1,4,128,256]{3,2,1,0:T(8,128)(2,1)} custom-call(f32[1,4,128,256]{3,2,1,0:T(8,128)S(1)} %shard_map.62.rest_ref, bf16[2,128,256]{2,1,0:T(8,128)(2,1)S(1)} %collective-permute-done.5.near_ref, bf16[2,128,256]{2,1,0:T(8,128)(2,1)S(1)} %collective-permute-done.6.far_ref), custom_call_target="tpu_custom_call" | custom-call | tf_op jit(solution)/shard_map/pallas_call | solution.py:16
  (1 shorter events, 0.0 us)
Async XLA Ops:
  0.0 19.6 %copy-start.2 = (f32[256]{0:T(256)S(1)}, f32[256]{0:T(256)}, u32[]{:S(2)}) copy-start(f32[256]{0:T(256)} %param.7) | copy-start | bytes 3076
  0.0 19.6 %copy-start = (bf16[3,3,3,256,256]{4,3,2,1,0:T(8,128)(2,1)S(1)}, bf16[3,3,3,256,256]{4,3,2,1,0:T(8,128)(2,1)}, u32[]{:S(2)}) copy-start(bf16[3,3,3,256,256]{4,3,2,1,0:T(8,128)(2,1)} %w_ref.9) | copy-start | bytes 10616836
  0.0 16.0 %collective-permute-start = (bf16[2,4,128,256]{3,2,1,0:T(8,128)(2,1)}, bf16[2,4,128,256]{3,2,1,0:T(8,128)(2,1)S(1)}, u32[]{:S(2)}, u32[]{:S(2)}) collective-permute-start(bf16[2,4,128,256]{3,2,1,0:T(8,128)(2,1)} %x_ref.1), channel_id=1, source_target_pairs={{0,1},{1,2},{2,3},{3,0},{4,5},{5,6},{6,7},{7,4},{8,9},{9,10},{10,1... | collective-permute-start | bytes 1572872 | tf_op jit(solution)/shard_map/ppermute | solution.py:259
  3.2 16.3 %collective-permute-start.2 = (bf16[2,2,128,256]{3,2,1,0:T(8,128)(2,1)S(1)}, bf16[2,2,128,256]{3,2,1,0:T(8,128)(2,1)S(1)}, u32[]{:S(2)}, u32[]{:S(2)}) collective-permute-start(bf16[2,2,128,256]{3,2,1,0:T(8,128)(2,1)S(1)} %get-tuple-element.21), channel_id=1, source_target_pairs={{4,8},{8,4},{0,12},{12,0},{5,9},{9,5},{1,13},{13,1},{6,10},{10,6},... | collective-permute-start | bytes 786440 | tf_op jit(solution)/shard_map/ppermute | solution.py:269
  5.4 15.3 %collective-permute-start.4 = (bf16[2,2,128,256]{3,2,1,0:T(8,128)(2,1)S(1)}, bf16[2,2,128,256]{3,2,1,0:T(8,128)(2,1)S(1)}, u32[]{:S(2)}, u32[]{:S(2)}) collective-permute-start(bf16[2,2,128,256]{3,2,1,0:T(8,128)(2,1)S(1)} %get-tuple-element.24), channel_id=1, source_target_pairs={{0,4},{8,12},{4,0},{12,8},{1,5},{9,13},{5,1},{13,9},{2,6},{10,14},... | collective-permute-start | bytes 786440 | tf_op jit(solution)/shard_map/ppermute | solution.py:268
  16.0 6.9 %collective-permute-start.3 = (bf16[2,2,128,256]{3,2,1,0:T(8,128)(2,1)S(1)}, bf16[2,2,128,256]{3,2,1,0:T(8,128)(2,1)S(1)}, u32[]{:S(2)}, u32[]{:S(2)}) collective-permute-start(bf16[2,2,128,256]{3,2,1,0:T(8,128)(2,1)S(1)} %shard_map.57), channel_id=1, source_target_pairs={{0,4},{8,12},{4,0},{12,8},{1,5},{9,13},{5,1},{13,9},{2,6},{10,14},... | collective-permute-start | bytes 786440 | tf_op jit(solution)/shard_map/ppermute | solution.py:289
  17.3 6.7 %collective-permute-start.1 = (bf16[2,2,128,256]{3,2,1,0:T(8,128)(2,1)S(1)}, bf16[2,2,128,256]{3,2,1,0:T(8,128)(2,1)S(1)}, u32[]{:S(2)}, u32[]{:S(2)}) collective-permute-start(bf16[2,2,128,256]{3,2,1,0:T(8,128)(2,1)S(1)} %get-tuple-element.21), channel_id=1, source_target_pairs={{4,9},{5,10},{6,11},{8,5},{9,6},{10,7},{20,25},{21,26},{22,27},{24... | collective-permute-start | bytes 786440 | tf_op jit(solution)/shard_map/ppermute | solution.py:270
  20.7 2.0 %copy-start.1 = (bf16[3,3,3,256,256]{4,3,2,1,0:T(8,128)(2,1)S(1)}, bf16[3,3,3,256,256]{4,3,2,1,0:T(8,128)(2,1)}, u32[]{:S(2)}) copy-start(bf16[3,3,3,256,256]{4,3,2,1,0:T(8,128)(2,1)} %v_ref.5) | copy-start | bytes 10616836
  24.0 6.9 %copy-start.3 = (f32[256]{0:T(256)S(1)}, f32[256]{0:T(256)}, u32[]{:S(2)}) copy-start(f32[256]{0:T(256)} %param.9) | copy-start | bytes 3076
  25.2 7.2 %collective-permute-start.6 = (bf16[2,128,256]{2,1,0:T(8,128)(2,1)S(1)}, bf16[2,128,256]{2,1,0:T(8,128)(2,1)S(1)}, u32[]{:S(2)}, u32[]{:S(2)}) collective-permute-start(bf16[2,128,256]{2,1,0:T(8,128)(2,1)S(1)} %get-tuple-element.34), channel_id=1, source_target_pairs={{0,1},{1,2},{2,3},{3,0},{4,5},{5,6},{6,7},{7,4},{8,9},{9,10},{10,1... | collective-permute-start | bytes 393224 | tf_op jit(solution)/shard_map/ppermute | solution.py:316
  29.7 5.6 %collective-permute-start.5 = (bf16[2,128,256]{2,1,0:T(8,128)(2,1)S(1)}, bf16[2,128,256]{2,1,0:T(8,128)(2,1)S(1)}, u32[]{:S(2)}, u32[]{:S(2)}) collective-permute-start(bf16[2,128,256]{2,1,0:T(8,128)(2,1)S(1)} %get-tuple-element.33), channel_id=1, source_target_pairs={{0,1},{1,2},{2,3},{3,0},{4,5},{5,6},{6,7},{7,4},{8,9},{9,10},{10,1... | collective-permute-start | bytes 393224 | tf_op jit(solution)/shard_map/ppermute | solution.py:308
where the time goes:
time: 36.2 us; the launch traced here: 36.1 us
  starting transfers between devices  13.6 us (38%)
  waiting for transfers between devices  13.5 us (37%)
  Pallas kernels  8.81 us (24%)
    ppermute x1, waiting for transfers between devices, block(): earlier = lax.ppermute(x, 'tm', ring)  10.6 us
    pallas_call x9, Pallas kernels, call(): pl.pallas_call(body, out_shape=outs, in_specs=in_specs or [VMEM] * len(ar...  8.81 us
    ppermute x1, starting transfers between devices, block(): far_part = lax.ppermute(far_send, 'tm', ring)  4.5 us
    ppermute x1, waiting for transfers between devices, block(): near_part = lax.ppermute(near_send, 'tm', ring)  2.89 us
    ppermute x1, starting transfers between devices, block(): corner = lax.ppermute(outer_edge, ('tile', 'tm'), diagonal)  2.21 us
    ppermute x1, starting transfers between devices, block(): outer = lax.ppermute(outer_edge, 'tile', outer_pairs + unpaired)  2.15 us
    ppermute x1, starting transfers between devices, block(): earlier = lax.ppermute(x, 'tm', ring)  2.11 us
    ppermute x1, starting transfers between devices, block(): inner_corner = lax.ppermute(inner_edge, 'tile', inner_pairs)  1.32 us
  transfers between devices with their start and end apart: 7, of which 2 were waited for; matrix products, arithmetic and copies ran while one was open for 0% of the time, Pallas kernels for 19%

commit v1 on v0

v1 whole, which is shorter than its diff:
```python
import functools

import jax
import jax.numpy as jnp
from jax import lax
from jax.experimental import pallas as pl
from jax.experimental.pallas import tpu as pltpu
from jax.sharding import PartitionSpec as P


VMEM = pl.BlockSpec(memory_space=pltpu.VMEM)
HBM = pl.BlockSpec(memory_space=pltpu.HBM)


def call(body, outs, args, flops, in_specs=None, scratch=()):
    return pl.pallas_call(
        body,
        out_shape=outs,
        in_specs=in_specs or [VMEM] * len(args),
        out_specs=[VMEM] * len(outs),
        scratch_shapes=scratch,
        compiler_params=pltpu.CompilerParams(vmem_limit_bytes=16 << 20),
        cost_estimate=pl.CostEstimate(flops=flops, bytes_accessed=0, transcendentals=0),
    )(*args)


def flat(value):
    return value.reshape(-1, value.shape[-1])


def row_taps(slab, rows):
    return [flat(slab[p : p + rows]) for p in range(3)]


def convolved(lhs, weights, rows, cols):
    stacked = jnp.concatenate(lhs, axis=1)
    total = None
    for q in range(3):
        taps = jnp.concatenate([w[q] for w in weights], axis=0)
        part = jnp.dot(stacked, taps, preferred_element_type=jnp.float32)
        part = part.reshape(rows, cols, part.shape[-1])
        if q != 1:
            col = lax.broadcasted_iota(jnp.int32, part.shape, 1)
            edge = 0 if q == 0 else cols - 1
            part = jnp.where(col == edge, 0.0, pltpu.roll(part, 1 if q == 0 else cols - 1, 1))
        total = part if total is None else total + part
    return total


def parity():
    return lax.rem(lax.axis_index("tile"), 2)


def either(first, second):
    even = parity() == 0
    return jnp.concatenate([jnp.where(even, a, b) for a, b in zip(first, second)], axis=0)


def own_edge(own, side):
    odd = parity()
    last = own.shape[0] - 2
    return own[pl.ds((odd if side == 0 else 1 - odd) * last, 2)]


def outer_slab(outer, own, tiles):
    tile = lax.axis_index("tile")
    beyond = (tile == 0) | ((tile == tiles - 1) & (parity() == 1))
    outer = jnp.where(beyond, jnp.zeros_like(outer), outer)
    edge = own_edge(own, 0)
    return either([outer, edge], [edge, outer])


def weight_rows(w_ref, a):
    return [[w_ref[a, p, q] for q in range(3)] for p in range(3)]


def silu_rows(value, start, rows, tiles):
    hidden = (value / (1.0 + jnp.exp(-value))).astype(jnp.bfloat16)
    row = lax.broadcasted_iota(jnp.int32, hidden.shape, 0) + start
    row = row + lax.axis_index("tile") * rows - 1
    inside = (row >= 0) & (row < tiles * rows)
    return jnp.where(inside, hidden, jnp.zeros_like(hidden))


def cut_body(x_ref, late_ref, sem):
    copy = pltpu.make_async_copy(x_ref.at[1], late_ref, sem)
    copy.start()
    copy.wait()


def edges_body(x_ref, late_ref, early_ref, outer_ref, inner_ref, sem):
    copy = pltpu.make_async_copy(x_ref.at[0], early_ref, sem)
    copy.start()
    outer_ref[1], inner_ref[1] = own_edge(late_ref, 0), own_edge(late_ref, 1)
    copy.wait()
    outer_ref[0], inner_ref[0] = own_edge(early_ref, 0), own_edge(early_ref, 1)


def turn_body(m_ref, inner_ref):
    inner_ref[...] = own_edge(m_ref, 1)


def own_sums(slabs, w_ref, b_ref, acc0_ref, acc1_ref):
    rows, cols = acc0_ref.shape[:2]
    taps = [row_taps(slab, rows) for slab in slabs]
    acc0_ref[...] = b_ref[...] + convolved(taps[0], weight_rows(w_ref, 2), rows, cols)
    weights = weight_rows(w_ref, 1) + weight_rows(w_ref, 2)
    acc1_ref[...] = b_ref[...] + convolved(taps[0] + taps[1], weights, rows, cols)


def near_slab(frame, inner):
    return jnp.where(
        parity() == 0,
        jnp.concatenate([frame, inner], axis=0),
        jnp.concatenate([inner, frame], axis=0),
    )


def own_near_body(early_ref, late_ref, inner_ref, w_ref, b_ref, acc0_ref, acc1_ref):
    slabs = [near_slab(early_ref[...], inner_ref[0]), near_slab(late_ref[...], inner_ref[1])]
    own_sums(slabs, w_ref, b_ref, acc0_ref, acc1_ref)


def own_far_body(tiles, early_ref, late_ref, outer_ref, w_ref, b_ref, acc0_ref, acc1_ref):
    slabs = [outer_slab(outer_ref[f], ref, tiles) for f, ref in enumerate((early_ref, late_ref))]
    own_sums(slabs, w_ref, b_ref, acc0_ref, acc1_ref)


def add_earlier(total_ref, base, product):
    started = lax.axis_index("tm") > 0

    @pl.when(started)
    def _():
        total_ref[...] = base() + product()

    @pl.when(jnp.logical_not(started))
    def _():
        total_ref[...] = base()


def partial_rows(times, h0, h1, v_ref, rows, cols, send_ref):
    has_next = lax.axis_index("tm") < times - 1

    @pl.when(has_next)
    def _():
        both = (h0.astype(jnp.float32) + h1.astype(jnp.float32)).astype(jnp.bfloat16)
        taps = row_taps(both, rows) + row_taps(h1, rows)
        part = convolved(taps, weight_rows(v_ref, 0) + weight_rows(v_ref, 1), rows, cols)
        send_ref[...] = part.astype(jnp.bfloat16)

    @pl.when(jnp.logical_not(has_next))
    def _():
        send_ref[...] = jnp.zeros_like(send_ref)


def near_place(rows):
    return pl.ds(2 * (1 - parity()), rows)


def late_near_body(
    tiles, m_ref, inner_ref, w_ref, _, acc0_ref, acc1_ref, sum0_ref, h1_ref, sum1_ref
):
    rows, cols = m_ref.shape[:2]

    def product(a):
        taps = row_taps(near_slab(m_ref[...], inner_ref[...]), rows)
        return convolved(taps, weight_rows(w_ref, a), rows, cols)

    add_earlier(sum1_ref, lambda: acc1_ref[...], lambda: product(0))
    h1_ref[...] = silu_rows(sum1_ref[...], near_place(rows).start, rows, tiles)
    add_earlier(sum0_ref, lambda: acc0_ref[...], lambda: product(1))


def early_near_body(
    tiles, times, m_ref, inner_ref, w_ref, v_ref, acc0_ref, h1_ref, send_ref, h0_ref, sum0_ref
):
    rows, cols = m_ref.shape[:2]

    def product():
        taps = row_taps(near_slab(m_ref[...], inner_ref[...]), rows)
        return convolved(taps, weight_rows(w_ref, 0), rows, cols)

    add_earlier(sum0_ref, lambda: acc0_ref[...], product)
    h0 = silu_rows(sum0_ref[...], near_place(rows).start, rows, tiles)
    h0_ref[...] = h0
    partial_rows(times, h0, h1_ref[...], v_ref, rows - 2, cols, send_ref)


def far_body(
    tiles, times, early_ref, late_ref, outer_ref, w_ref, v_ref, acc0_ref, acc1_ref, near0_ref,
    near1_ref, send_ref, h0_ref, h1_ref, sum0_ref, sum1_ref,
):
    rows, cols = early_ref.shape[:2]
    odd = parity()
    near, far, side = near_place(rows), pl.ds(odd * rows, 2), pl.ds(odd * (rows - 2), 4)
    h0_ref[near], h1_ref[near] = near0_ref[...], near1_ref[...]

    def taps(f, frame_ref):
        return row_taps(outer_slab(outer_ref[f], frame_ref, tiles), 2)

    def product0():
        weights = weight_rows(w_ref, 0) + weight_rows(w_ref, 1)
        return convolved(taps(0, early_ref) + taps(1, late_ref), weights, 2, cols)

    def product1():
        return convolved(taps(1, late_ref), weight_rows(w_ref, 0), 2, cols)

    add_earlier(sum0_ref, lambda: acc0_ref[...], product0)
    add_earlier(sum1_ref, lambda: acc1_ref[...], product1)
    h0_ref[far] = silu_rows(sum0_ref[...], far.start, rows, tiles)
    h1_ref[far] = silu_rows(sum1_ref[...], far.start, rows, tiles)
    partial_rows(times, h0_ref[side], h1_ref[side], v_ref, 2, cols, send_ref)


def rest_body(early_ref, late_ref, h0_ref, h1_ref, v_ref, b_ref, out_ref):
    rows, cols = early_ref.shape[:2]
    h0, h1 = h0_ref[...], h1_ref[...]
    both = (h0.astype(jnp.float32) + h1.astype(jnp.float32)).astype(jnp.bfloat16)
    taps = row_taps(h0, rows) + row_taps(both, rows)
    part = convolved(taps, weight_rows(v_ref, 1) + weight_rows(v_ref, 2), rows, cols)
    total = early_ref[...].astype(jnp.float32) + late_ref[...].astype(jnp.float32) + part
    out_ref[0] = total * 0.5 + b_ref[...]


def join_body(rest_ref, near_ref, far_ref, out_ref):
    rows = rest_ref.shape[1]
    odd = parity()
    first = lax.axis_index("tm") == 0
    for part_ref, start in ((near_ref, 2 * (1 - odd)), (far_ref, odd * (rows - 2))):
        part = part_ref[...].astype(jnp.float32)
        part = jnp.where(first, jnp.zeros_like(part), part)
        place = pl.ds(start, part.shape[0])
        out_ref[0, place] = (rest_ref[0, place] + 0.5 * part).astype(jnp.bfloat16)


def block(x, weight_first, bias_first, weight_second, bias_second):
    _, rows, cols, channels = x.shape
    tiles, times = lax.axis_size("tile"), lax.axis_size("tm")
    forward = [(i, i + 1) for i in range(times - 1)]
    ring = forward + [(times - 1, 0)]
    inner_pairs = [(i, i + 1) for i in range(0, tiles - 1, 2)]
    outer_pairs = [(i, i + 1) for i in range(1, tiles - 1, 2)]
    inner_pairs += [(j, i) for i, j in inner_pairs]
    outer_pairs += [(j, i) for i, j in outer_pairs]
    unpaired = [(0, tiles - 1), (tiles - 1, 0)] if tiles % 2 == 0 else []
    diagonal = [(i * times + s, j * times + t) for i, j in outer_pairs for s, t in ring]
    diagonal += [(i * times + s, j * times + s) for i, j in unpaired for s in range(times)]

    def frames(*lead, dtype=jnp.bfloat16):
        return jax.ShapeDtypeStruct((*lead, cols, channels), dtype)

    f32 = jnp.float32
    x = pltpu.with_memory_space_constraint(x, pltpu.HBM)
    dma = [pltpu.SemaphoreType.DMA(())]
    (late,) = call(cut_body, [frames(rows)], (x,), 0, in_specs=[HBM], scratch=dma)
    late_before = lax.ppermute(late, "tm", ring)
    early, outer_edge, inner_edge = call(
        edges_body,
        [frames(rows), frames(2, 2), frames(2, 2)],
        (x, late),
        10**10,
        in_specs=[HBM, VMEM],
        scratch=dma,
    )
    inner = lax.ppermute(inner_edge, "tile", inner_pairs)
    outer = lax.ppermute(outer_edge, "tile", outer_pairs + unpaired)
    early_before = lax.ppermute(early, "tm", forward)
    corner = lax.ppermute(outer_edge, ("tile", "tm"), diagonal)

    bias_first = bias_first.reshape(1, 1, -1)
    bias_second = bias_second.reshape(1, 1, -1)
    unit = 2 * 9 * channels * channels * cols
    wide = rows + 2
    sums0, sums1 = call(
        own_near_body,
        [frames(rows, dtype=f32), frames(rows, dtype=f32)],
        (early, late, inner, weight_first, bias_first),
        3 * unit * rows,
    )
    far0, far1 = call(
        functools.partial(own_far_body, tiles),
        [frames(2, dtype=f32), frames(2, dtype=f32)],
        (early, late, outer, weight_first, bias_first),
        0,
    )

    def sums(count, frame_count):
        return [pltpu.VMEM((count, cols, channels), f32)] * frame_count

    (edge,) = call(turn_body, [frames(2)], (late_before,), 0)
    late_inner = lax.ppermute(edge, "tile", inner_pairs)
    sums0, near1 = call(
        functools.partial(late_near_body, tiles),
        [frames(rows, dtype=f32), frames(rows)],
        (late_before, late_inner, weight_first, weight_second, sums0, sums1),
        0,
        scratch=sums(rows, 1),
    )
    (edge,) = call(turn_body, [frames(2)], (early_before,), 0)
    early_inner = lax.ppermute(edge, "tile", inner_pairs)
    near_send, near0 = call(
        functools.partial(early_near_body, tiles, times),
        [frames(rows - 2), frames(rows)],
        (early_before, early_inner, weight_first, weight_second, sums0, near1),
        0,
        scratch=sums(rows, 1),
    )
    near_part = lax.ppermute(near_send, "tm", ring)
    far_send, h0, h1 = call(
        functools.partial(far_body, tiles, times),
        [frames(2), frames(wide), frames(wide)],
        (
            early_before, late_before, corner, weight_first, weight_second, far0, far1, near0,
            near1,
        ),
        0,
        scratch=sums(2, 2),
    )
    far_part = lax.ppermute(far_send, "tm", ring)
    (rest,) = call(
        rest_body,
        [frames(1, rows, dtype=f32)],
        (early, late, h0, h1, weight_second, bias_second),
        2 * unit * rows,
    )
    (pooled,) = call(join_body, [frames(1, rows)], (rest, near_part, far_part), 0)
    return pooled


def solution(mesh):
    in_specs = (P(("clips", "tm"), "tile", None, None), P(), P(), P(), P())
    out_specs = P(("clips", "tm"), "tile", None, None)
    return jax.shard_map(block, mesh=mesh, in_specs=in_specs, out_specs=out_specs, check_vma=False)
```

time: 36.2 us -> 37 us (1.022)
  the two profiles are of different devices: /device:TPU:1 before, /device:TPU:4 now
where the time goes in v1:
time: 37 us; the launch traced here: 36.8 us
  waiting for transfers between devices  13.8 us (37%)
  starting transfers between devices  13.3 us (36%)
  Pallas kernels  9.57 us (26%)
    pallas_call x11, Pallas kernels, call(): pl.pallas_call(body, out_shape=outs, in_specs=in_specs or [VMEM] * len(ar...  9.57 us
    ppermute x1, starting transfers between devices, block(): far_part = lax.ppermute(far_send, 'tm', ring)  5.14 us
    ppermute x1, waiting for transfers between devices, block(): outer = lax.ppermute(outer_edge, 'tile', outer_pairs + unpaired)  4.69 us
    ppermute x1, waiting for transfers between devices, block(): near_part = lax.ppermute(near_send, 'tm', ring)  4.24 us
    ppermute x1, starting transfers between devices, block(): early_before = lax.ppermute(early, 'tm', forward)  3.5 us
    ppermute x1, waiting for transfers between devices, block(): early_before = lax.ppermute(early, 'tm', forward)  2.76 us
    ppermute x1, starting transfers between devices, block(): corner = lax.ppermute(outer_edge, ('tile', 'tm'), diagonal)  2.13 us
    ppermute x1, starting transfers between devices, block(): late_before = lax.ppermute(late, 'tm', ring)  1.63 us
  transfers between devices with their start and end apart: 9, of which 5 were waited for; matrix products, arithmetic and copies ran while one was open for 0% of the time, Pallas kernels for 18%

profile of v1, /device:TPU:4, one launch (start us, length us, event | category | flops | bytes accessed | tf_op | source)
XLA Modules:
  0.0 36.8 jit_solution(17372165993020050945)
XLA Ops:
  0.0 1.0 %shard_map.55.late_ref = bf16[4,128,256]{2,1,0:T(8,128)(2,1)S(1)} custom-call(bf16[2,4,128,256]{3,2,1,0:T(8,128)(2,1)} %x_ref.3), custom_call_target="tpu_custom_call" | custom-call | tf_op jit(solution)/shard_map/pallas_call | solution.py:16
  1.0 0.0 copy-start
  1.0 0.0 copy-start.2
  1.0 1.6 %collective-permute-start.1 = (bf16[4,128,256]{2,1,0:T(8,128)(2,1)S(1)}, bf16[4,128,256]{2,1,0:T(8,128)(2,1)S(1)}, u32[]{:S(2)}, u32[]{:S(2)}) collective-permute-start(bf16[4,128,256]{2,1,0:T(8,128)(2,1)S(1)} %shard_map.55.late_ref), channel_id=1, source_target_pairs={{0,1},{1,2},{2,3},{3,0},{4,5},{5,6},{6,7},{7,4},{8,9},{9,10},{10,1... | collective-permute-start | bytes 786440 | tf_op jit(solution)/shard_map/ppermute | solution.py:256
  2.6 1.0 %shard_map.56 = (bf16[4,128,256]{2,1,0:T(8,128)(2,1)S(1)}, bf16[2,2,128,256]{3,2,1,0:T(8,128)(2,1)S(1)}, bf16[2,2,128,256]{3,2,1,0:T(8,128)(2,1)S(1)}) custom-call(bf16[2,4,128,256]{3,2,1,0:T(8,128)(2,1)} %x_ref.3, bf16[4,128,256]{2,1,0:T(8,128)(2,1)S(1)} %shard_map.55.late_ref), custom_call_target="tpu_custom_call" | custom-call | flops 10000000000 | tf_op jit(solution)/shard_map/pallas_call | solution.py:16
  3.6 3.5 %collective-permute-start = (bf16[4,128,256]{2,1,0:T(8,128)(2,1)S(1)}, bf16[4,128,256]{2,1,0:T(8,128)(2,1)S(1)}, u32[]{:S(2)}, u32[]{:S(2)}) collective-permute-start(bf16[4,128,256]{2,1,0:T(8,128)(2,1)S(1)} %get-tuple-element.19.early_ref), channel_id=1, source_target_pairs={{0,1},{1,2},{2,3},{4,5},{5,6},{6,7},{8,9},{9,10},{10,11},{12,13},{... | collective-permute-start | bytes 786440 | tf_op jit(solution)/shard_map/ppermute | solution.py:267
  7.1 0.1 collective-permute-start.3
  7.2 0.6 %collective-permute-start.6 = (bf16[2,2,128,256]{3,2,1,0:T(8,128)(2,1)S(1)}, bf16[2,2,128,256]{3,2,1,0:T(8,128)(2,1)S(1)}, u32[]{:S(2)}, u32[]{:S(2)}) collective-permute-start(bf16[2,2,128,256]{3,2,1,0:T(8,128)(2,1)S(1)} %get-tuple-element.23), channel_id=1, source_target_pairs={{0,4},{8,12},{4,0},{12,8},{1,5},{9,13},{5,1},{13,9},{2,6},{10,14},... | collective-permute-start | bytes 786440 | tf_op jit(solution)/shard_map/ppermute | solution.py:265
  7.8 2.1 %collective-permute-start.2 = (bf16[2,2,128,256]{3,2,1,0:T(8,128)(2,1)S(1)}, bf16[2,2,128,256]{3,2,1,0:T(8,128)(2,1)S(1)}, u32[]{:S(2)}, u32[]{:S(2)}) collective-permute-start(bf16[2,2,128,256]{3,2,1,0:T(8,128)(2,1)S(1)} %get-tuple-element.20), channel_id=1, source_target_pairs={{4,9},{5,10},{6,11},{7,8},{8,5},{9,6},{10,7},{11,4},{0,12},{1,13},... | collective-permute-start | bytes 786440 | tf_op jit(solution)/shard_map/ppermute | solution.py:268
  9.9 1.0 %collective-permute-done.1.m_ref.late_ref = bf16[4,128,256]{2,1,0:T(8,128)(2,1)S(1)} collective-permute-done((bf16[4,128,256]{2,1,0:T(8,128)(2,1)S(1)}, bf16[4,128,256]{2,1,0:T(8,128)(2,1)S(1)}, u32[]{:S(2)}, u32[]{:S(2)}) %collective-permute-start.1) | collective-permute-done | bytes 262176 | tf_op jit(solution)/shard_map/ppermute | solution.py:256
  11.0 0.1 collective-permute-start.5
  11.0 2.8 %collective-permute-done.m_ref.early_ref = bf16[4,128,256]{2,1,0:T(8,128)(2,1)S(1)} collective-permute-done((bf16[4,128,256]{2,1,0:T(8,128)(2,1)S(1)}, bf16[4,128,256]{2,1,0:T(8,128)(2,1)S(1)}, u32[]{:S(2)}, u32[]{:S(2)}) %collective-permute-start) | collective-permute-done | bytes 262176 | tf_op jit(solution)/shard_map/ppermute | solution.py:267
  13.8 0.1 collective-permute-start.4
  13.9 4.7 %collective-permute-done.3.outer_ref = bf16[2,2,128,256]{3,2,1,0:T(8,128)(2,1)S(1)} collective-permute-done((bf16[2,2,128,256]{3,2,1,0:T(8,128)(2,1)S(1)}, bf16[2,2,128,256]{3,2,1,0:T(8,128)(2,1)S(1)}, u32[]{:S(2)}, u32[]{:S(2)}) %collective-permute-start.3) | collective-permute-done | bytes 262176 | tf_op jit(solution)/shard_map/ppermute | solution.py:266
  18.6 0.0 copy-done
  18.6 1.1 %shard_map.57 = (f32[2,128,256]{2,1,0:T(8,128)S(1)}, f32[2,128,256]{2,1,0:T(8,128)S(1)}) custom-call(bf16[4,128,256]{2,1,0:T(8,128)(2,1)S(1)} %get-tuple-element.19.early_ref, bf16[4,128,256]{2,1,0:T(8,128)(2,1)S(1)} %shard_map.55.late_ref, bf16[2,2,128,256]{3,2,1,0:T(8,128)(2,1)S(1)} %collective-permute-done.3.outer_ref, ...), custom_call_target="tpu_custom_call" | custom-call | tf_op jit(solution)/shard_map/pallas_call | solution.py:16
  19.7 0.0 copy-start.1
  19.7 0.0 collective-permute-done.6.inner_ref
  19.7 2.0 %shard_map.60 = (f32[4,128,256]{2,1,0:T(8,128)S(1)}, f32[4,128,256]{2,1,0:T(8,128)S(1)}) custom-call(bf16[4,128,256]{2,1,0:T(8,128)(2,1)S(1)} %get-tuple-element.19.early_ref, bf16[4,128,256]{2,1,0:T(8,128)(2,1)S(1)} %shard_map.55.late_ref, bf16[2,2,128,256]{3,2,1,0:T(8,128)(2,1)S(1)} %collective-permute-done.6.inner_ref, ...), custom_call_target="tpu_custom_call" | custom-call | flops 1811939328 | tf_op jit(solution)/shard_map/pallas_call | solution.py:16
  21.7 0.0 collective-permute-done.5.inner_ref
  21.7 0.2 shard_map.61
  22.0 0.0 collective-permute-done.4.inner_ref
  22.0 1.0 %shard_map.62 = (bf16[2,128,256]{2,1,0:T(8,128)(2,1)S(1)}, bf16[4,128,256]{2,1,0:T(8,128)(2,1)S(1)}) custom-call(bf16[4,128,256]{2,1,0:T(8,128)(2,1)S(1)} %collective-permute-done.m_ref.early_ref, bf16[2,128,256]{2,1,0:T(8,128)(2,1)S(1)} %collective-permute-done.4.inner_ref, bf16[3,3,3,256,256]{4,3,2,1,0:T(8,128)(2,1)S(1)} %copy-done, ...), custom_call_target="tpu_custom_call" | custom-call | tf_op jit(solution)/shard_map/pallas_call | solution.py:16
  23.0 0.0 collective-permute-done.2.outer_ref
  23.0 0.0 copy-start.3
  23.0 1.1 %shard_map.63 = (bf16[2,128,256]{2,1,0:T(8,128)(2,1)S(1)}, bf16[6,128,256]{2,1,0:T(8,128)(2,1)S(1)}, bf16[6,128,256]{2,1,0:T(8,128)(2,1)S(1)}) custom-call(bf16[4,128,256]{2,1,0:T(8,128)(2,1)S(1)} %collective-permute-done.m_ref.early_ref, bf16[4,128,256]{2,1,0:T(8,128)(2,1)S(1)} %collective-permute-done.1.m_ref.late_ref, ...), custom_call_target="tpu_custom_call" | custom-call | tf_op jit(solution)/shard_map/pallas_call | solution.py:16
  24.1 5.1 %collective-permute-start.8 = (bf16[2,128,256]{2,1,0:T(8,128)(2,1)S(1)}, bf16[2,128,256]{2,1,0:T(8,128)(2,1)S(1)}, u32[]{:S(2)}, u32[]{:S(2)}) collective-permute-start(bf16[2,128,256]{2,1,0:T(8,128)(2,1)S(1)} %get-tuple-element.32), channel_id=1, source_target_pairs={{0,1},{1,2},{2,3},{3,0},{4,5},{5,6},{6,7},{7,4},{8,9},{9,10},{10,1... | collective-permute-start | bytes 393224 | tf_op jit(solution)/shard_map/ppermute | solution.py:319
  29.3 0.1 collective-permute-start.7
  29.3 1.4 %shard_map.64.rest_ref = f32[1,4,128,256]{3,2,1,0:T(8,128)S(1)} custom-call(bf16[4,128,256]{2,1,0:T(8,128)(2,1)S(1)} %get-tuple-element.19.early_ref, bf16[4,128,256]{2,1,0:T(8,128)(2,1)S(1)} %shard_map.55.late_ref, bf16[6,128,256]{2,1,0:T(8,128)(2,1)S(1)} %get-tuple-element.29.h0_ref, bf16[6,128,256]{2,1,0:T(8,128)(2,1)S(1)} %get-tuple-element.30.h1_ref, ...), custom_call_target="tpu_custom_call" | custom-call | flops 1207959552 | tf_op jit(solution)/shard_map/pallas_call | solution.py:16
  30.8 1.0 %collective-permute-done.8.far_ref = bf16[2,128,256]{2,1,0:T(8,128)(2,1)S(1)} collective-permute-done((bf16[2,128,256]{2,1,0:T(8,128)(2,1)S(1)}, bf16[2,128,256]{2,1,0:T(8,128)(2,1)S(1)}, u32[]{:S(2)}, u32[]{:S(2)}) %collective-permute-start.8) | collective-permute-done | bytes 131104 | tf_op jit(solution)/shard_map/ppermute | solution.py:319
  31.8 4.2 %collective-permute-done.7.near_ref = bf16[2,128,256]{2,1,0:T(8,128)(2,1)S(1)} collective-permute-done((bf16[2,128,256]{2,1,0:T(8,128)(2,1)S(1)}, bf16[2,128,256]{2,1,0:T(8,128)(2,1)S(1)}, u32[]{:S(2)}, u32[]{:S(2)}) %collective-permute-start.7) | collective-permute-done | bytes 131104 | tf_op jit(solution)/shard_map/ppermute | solution.py:308
  36.0 0.8 %shard_map.65 = bf16[1,4,128,256]{3,2,1,0:T(8,128)(2,1)} custom-call(f32[1,4,128,256]{3,2,1,0:T(8,128)S(1)} %shard_map.64.rest_ref, bf16[2,128,256]{2,1,0:T(8,128)(2,1)S(1)} %collective-permute-done.7.near_ref, bf16[2,128,256]{2,1,0:T(8,128)(2,1)S(1)} %collective-permute-done.8.far_ref), custom_call_target="tpu_custom_call" | custom-call | tf_op jit(solution)/shard_map/pallas_call | solution.py:16
  (5 shorter events, 0.0 us)
Async XLA Ops:
  1.0 17.6 %copy-start = (bf16[3,3,3,256,256]{4,3,2,1,0:T(8,128)(2,1)S(1)}, bf16[3,3,3,256,256]{4,3,2,1,0:T(8,128)(2,1)}, u32[]{:S(2)}) copy-start(bf16[3,3,3,256,256]{4,3,2,1,0:T(8,128)(2,1)} %w_ref.9) | copy-start | bytes 10616836
  1.0 17.6 %copy-start.2 = (f32[256]{0:T(256)S(1)}, f32[256]{0:T(256)}, u32[]{:S(2)}) copy-start(f32[256]{0:T(256)} %param.7) | copy-start | bytes 3076
  1.0 10.0 %collective-permute-start.1 = (bf16[4,128,256]{2,1,0:T(8,128)(2,1)S(1)}, bf16[4,128,256]{2,1,0:T(8,128)(2,1)S(1)}, u32[]{:S(2)}, u32[]{:S(2)}) collective-permute-start(bf16[4,128,256]{2,1,0:T(8,128)(2,1)S(1)} %shard_map.55.late_ref), channel_id=1, source_target_pairs={{0,1},{1,2},{2,3},{3,0},{4,5},{5,6},{6,7},{7,4},{8,9},{9,10},{10,1... | collective-permute-start | bytes 786440 | tf_op jit(solution)/shard_map/ppermute | solution.py:256
  3.6 10.2 %collective-permute-start = (bf16[4,128,256]{2,1,0:T(8,128)(2,1)S(1)}, bf16[4,128,256]{2,1,0:T(8,128)(2,1)S(1)}, u32[]{:S(2)}, u32[]{:S(2)}) collective-permute-start(bf16[4,128,256]{2,1,0:T(8,128)(2,1)S(1)} %get-tuple-element.19.early_ref), channel_id=1, source_target_pairs={{0,1},{1,2},{2,3},{4,5},{5,6},{6,7},{8,9},{9,10},{10,11},{12,13},{... | collective-permute-start | bytes 786440 | tf_op jit(solution)/shard_map/ppermute | solution.py:267
  7.1 11.5 %collective-permute-start.3 = (bf16[2,2,128,256]{3,2,1,0:T(8,128)(2,1)S(1)}, bf16[2,2,128,256]{3,2,1,0:T(8,128)(2,1)S(1)}, u32[]{:S(2)}, u32[]{:S(2)}) collective-permute-start(bf16[2,2,128,256]{3,2,1,0:T(8,128)(2,1)S(1)} %get-tuple-element.20), channel_id=1, source_target_pairs={{4,8},{8,4},{0,12},{12,0},{5,9},{9,5},{1,13},{13,1},{6,10},{10,6},... | collective-permute-start | bytes 786440 | tf_op jit(solution)/shard_map/ppermute | solution.py:266
  7.2 12.5 %collective-permute-start.6 = (bf16[2,2,128,256]{3,2,1,0:T(8,128)(2,1)S(1)}, bf16[2,2,128,256]{3,2,1,0:T(8,128)(2,1)S(1)}, u32[]{:S(2)}, u32[]{:S(2)}) collective-permute-start(bf16[2,2,128,256]{3,2,1,0:T(8,128)(2,1)S(1)} %get-tuple-element.23), channel_id=1, source_target_pairs={{0,4},{8,12},{4,0},{12,8},{1,5},{9,13},{5,1},{13,9},{2,6},{10,14},... | collective-permute-start | bytes 786440 | tf_op jit(solution)/shard_map/ppermute | solution.py:265
  7.8 15.2 %collective-permute-start.2 = (bf16[2,2,128,256]{3,2,1,0:T(8,128)(2,1)S(1)}, bf16[2,2,128,256]{3,2,1,0:T(8,128)(2,1)S(1)}, u32[]{:S(2)}, u32[]{:S(2)}) collective-permute-start(bf16[2,2,128,256]{3,2,1,0:T(8,128)(2,1)S(1)} %get-tuple-element.20), channel_id=1, source_target_pairs={{4,9},{5,10},{6,11},{7,8},{8,5},{9,6},{10,7},{11,4},{0,12},{1,13},... | collective-permute-start | bytes 786440 | tf_op jit(solution)/shard_map/ppermute | solution.py:268
  11.0 10.8 %collective-permute-start.5 = (bf16[2,128,256]{2,1,0:T(8,128)(2,1)S(1)}, bf16[2,128,256]{2,1,0:T(8,128)(2,1)S(1)}, u32[]{:S(2)}, u32[]{:S(2)}) collective-permute-start(bf16[2,128,256]{2,1,0:T(8,128)(2,1)S(1)} %shard_map.59), channel_id=1, source_target_pairs={{0,4},{8,12},{4,0},{12,8},{1,5},{9,13},{5,1},{13,9},{2,6},{10,14},... | collective-permute-start | bytes 393224 | tf_op jit(solution)/shard_map/ppermute | solution.py:291
  13.8 8.2 %collective-permute-start.4 = (bf16[2,128,256]{2,1,0:T(8,128)(2,1)S(1)}, bf16[2,128,256]{2,1,0:T(8,128)(2,1)S(1)}, u32[]{:S(2)}, u32[]{:S(2)}) collective-permute-start(bf16[2,128,256]{2,1,0:T(8,128)(2,1)S(1)} %shard_map.58), channel_id=1, source_target_pairs={{0,4},{8,12},{4,0},{12,8},{1,5},{9,13},{5,1},{13,9},{2,6},{10,14},... | collective-permute-start | bytes 393224 | tf_op jit(solution)/shard_map/ppermute | solution.py:300
  19.7 2.0 %copy-start.1 = (bf16[3,3,3,256,256]{4,3,2,1,0:T(8,128)(2,1)S(1)}, bf16[3,3,3,256,256]{4,3,2,1,0:T(8,128)(2,1)}, u32[]{:S(2)}) copy-start(bf16[3,3,3,256,256]{4,3,2,1,0:T(8,128)(2,1)} %v_ref.5) | copy-start | bytes 10616836
  23.0 6.3 %copy-start.3 = (f32[256]{0:T(256)S(1)}, f32[256]{0:T(256)}, u32[]{:S(2)}) copy-start(f32[256]{0:T(256)} %param.9) | copy-start | bytes 3076
  24.1 7.7 %collective-permute-start.8 = (bf16[2,128,256]{2,1,0:T(8,128)(2,1)S(1)}, bf16[2,128,256]{2,1,0:T(8,128)(2,1)S(1)}, u32[]{:S(2)}, u32[]{:S(2)}) collective-permute-start(bf16[2,128,256]{2,1,0:T(8,128)(2,1)S(1)} %get-tuple-element.32), channel_id=1, source_target_pairs={{0,1},{1,2},{2,3},{3,0},{4,5},{5,6},{6,7},{7,4},{8,9},{9,10},{10,1... | collective-permute-start | bytes 393224 | tf_op jit(solution)/shard_map/ppermute | solution.py:319
  29.3 6.8 %collective-permute-start.7 = (bf16[2,128,256]{2,1,0:T(8,128)(2,1)S(1)}, bf16[2,128,256]{2,1,0:T(8,128)(2,1)S(1)}, u32[]{:S(2)}, u32[]{:S(2)}) collective-permute-start(bf16[2,128,256]{2,1,0:T(8,128)(2,1)S(1)} %get-tuple-element.31), channel_id=1, source_target_pairs={{0,1},{1,2},{2,3},{3,0},{4,5},{5,6},{6,7},{7,4},{8,9},{9,10},{10,1... | collective-permute-start | bytes 393224 | tf_op jit(solution)/shard_map/ppermute | solution.py:308

commit v2 on v0

--- a/solution.py
+++ b/solution.py
@@ -242,14 +242,17 @@
 
 def block(x, weight_first, bias_first, weight_second, bias_second):
     _, rows, cols, channels = x.shape
-    tiles, times = lax.axis_size("tile"), lax.axis_size("tm")
+    clips, tiles, times = (lax.axis_size(axis) for axis in ("clips", "tile", "tm"))
     forward = [(i, i + 1) for i in range(times - 1)]
     ring = forward + [(times - 1, 0)]
     inner_pairs = [(i, i + 1) for i in range(0, tiles - 1, 2)]
     outer_pairs = [(i, i + 1) for i in range(1, tiles - 1, 2)]
     inner_pairs += [(j, i) for i, j in inner_pairs]
     outer_pairs += [(j, i) for i, j in outer_pairs]
-    unpaired = [(0, tiles - 1), (tiles - 1, 0)] if tiles % 2 == 0 else []
+    paired = {i for i, _ in outer_pairs}
+    unpaired = [i for i in range(tiles) if i not in paired]
+    outer_full = [(c * tiles + i, c * tiles + j) for c in range(clips) for i, j in outer_pairs]
+    outer_full += [(c * tiles + i, (c + 1) % clips * tiles + i) for c in range(clips) for i in unpaired]
     diagonal = [(i * times + s, j * times + t) for i, j in outer_pairs for s, t in forward]
 
     def frames(*lead, dtype=jnp.bfloat16):
@@ -266,7 +269,7 @@
         scratch=[pltpu.SemaphoreType.DMA(())],
     )
     inner = lax.ppermute(inner_edge, "tile", inner_pairs)
-    outer = lax.ppermute(outer_edge, "tile", outer_pairs + unpaired)
+    outer = lax.ppermute(outer_edge, ("clips", "tile"), outer_full)
     corner = lax.ppermute(outer_edge, ("tile", "tm"), diagonal)
 
     bias_first = bias_first.reshape(1, 1, -1)
@@ -313,7 +316,7 @@
         0,
         scratch=sums(2),
     )
-    far_part = lax.ppermute(far_send, "tm", ring)
+    far_part = lax.ppermute(far_send, "tm", forward)
     (rest,) = call(
         rest_body,
         [frames(1, rows, dtype=f32)],

time: 36.2 us -> 38.2 us (1.055)
  starting transfers between devices: 13.6 us -> 15.9 us
  waiting for transfers between devices: 13.5 us -> 13.1 us
    ppermute x2, starting transfers between devices: 6.65 us -> 8.51 us  [the longest x1 6.36 us: block(): far_part = lax.ppermute(far_send, 'tm', forward)]
  transfers between devices with their start and end apart: 7 -> 7, of which waited for: 2 -> 2; matrix products, arithmetic and copies ran while one was open for 0% -> 0% of each run, Pallas kernels for 19% -> 18%
where the time goes in v2:
time: 38.2 us; the launch traced here: 38 us
  starting transfers between devices  15.9 us (42%)
  waiting for transfers between devices  13.1 us (34%)
  Pallas kernels  8.81 us (23%)
    ppermute x1, waiting for transfers between devices, block(): earlier = lax.ppermute(x, 'tm', ring)  10.2 us
    pallas_call x9, Pallas kernels, call(): pl.pallas_call(body, out_shape=outs, in_specs=in_specs or [VMEM] * len(ar...  8.81 us
    ppermute x1, starting transfers between devices, block(): far_part = lax.ppermute(far_send, 'tm', forward)  6.36 us
    ppermute x1, waiting for transfers between devices, block(): near_part = lax.ppermute(near_send, 'tm', ring)  2.89 us
    ppermute x1, starting transfers between devices, block(): corner = lax.ppermute(outer_edge, ('tile', 'tm'), diagonal)  2.21 us
    ppermute x1, starting transfers between devices, block(): outer = lax.ppermute(outer_edge, ('clips', 'tile'), outer_full)  2.14 us
    ppermute x1, starting transfers between devices, block(): earlier = lax.ppermute(x, 'tm', ring)  2.11 us
    ppermute x1, starting transfers between devices, block(): near_part = lax.ppermute(near_send, 'tm', ring)  1.35 us
  transfers between devices with their start and end apart: 7, of which 2 were waited for; matrix products, arithmetic and copies ran while one was open for 0% of the time, Pallas kernels for 18%

profile of v2, /device:TPU:1, one launch (start us, length us, event | category | flops | bytes accessed | tf_op | source)
XLA Modules:
  0.0 38.0 jit_solution(14487476189927469051)
XLA Ops:
  0.0 0.0 copy-start.2
  0.0 0.0 copy-start
  0.0 2.1 %collective-permute-start = (bf16[2,4,128,256]{3,2,1,0:T(8,128)(2,1)}, bf16[2,4,128,256]{3,2,1,0:T(8,128)(2,1)S(1)}, u32[]{:S(2)}, u32[]{:S(2)}) collective-permute-start(bf16[2,4,128,256]{3,2,1,0:T(8,128)(2,1)} %x_ref.1), channel_id=1, source_target_pairs={{0,1},{1,2},{2,3},{3,0},{4,5},{5,6},{6,7},{7,4},{8,9},{9,10},{10,1... | collective-permute-start | bytes 1572872 | tf_op jit(solution)/shard_map/ppermute | solution.py:262
  2.1 1.1 %shard_map.55 = (bf16[2,4,128,256]{3,2,1,0:T(8,128)(2,1)S(1)}, bf16[2,2,128,256]{3,2,1,0:T(8,128)(2,1)S(1)}, bf16[2,2,128,256]{3,2,1,0:T(8,128)(2,1)S(1)}) custom-call(bf16[2,4,128,256]{3,2,1,0:T(8,128)(2,1)} %x_ref.1), custom_call_target="tpu_custom_call" | custom-call | flops 10000000000 | tf_op jit(solution)/shard_map/pallas_call | solution.py:16
  3.2 2.1 %collective-permute-start.2 = (bf16[2,2,128,256]{3,2,1,0:T(8,128)(2,1)S(1)}, bf16[2,2,128,256]{3,2,1,0:T(8,128)(2,1)S(1)}, u32[]{:S(2)}, u32[]{:S(2)}) collective-permute-start(bf16[2,2,128,256]{3,2,1,0:T(8,128)(2,1)S(1)} %get-tuple-element.21), channel_id=1, source_target_pairs={{4,8},{8,4},{20,24},{24,20},{0,16},{12,28},{16,0},{28,12},{5,9},{9... | collective-permute-start | bytes 786440 | tf_op jit(solution)/shard_map/ppermute | solution.py:272
  5.4 0.4 collective-permute-start.4
  5.8 10.2 %collective-permute-done.m_ref = bf16[2,4,128,256]{3,2,1,0:T(8,128)(2,1)S(1)} collective-permute-done((bf16[2,4,128,256]{3,2,1,0:T(8,128)(2,1)}, bf16[2,4,128,256]{3,2,1,0:T(8,128)(2,1)S(1)}, u32[]{:S(2)}, u32[]{:S(2)}) %collective-permute-start) | collective-permute-done | bytes 524320 | tf_op jit(solution)/shard_map/ppermute | solution.py:262
  16.0 1.3 %collective-permute-start.3 = (bf16[2,2,128,256]{3,2,1,0:T(8,128)(2,1)S(1)}, bf16[2,2,128,256]{3,2,1,0:T(8,128)(2,1)S(1)}, u32[]{:S(2)}, u32[]{:S(2)}) collective-permute-start(bf16[2,2,128,256]{3,2,1,0:T(8,128)(2,1)S(1)} %shard_map.57), channel_id=1, source_target_pairs={{0,4},{8,12},{4,0},{12,8},{1,5},{9,13},{5,1},{13,9},{2,6},{10,14},... | collective-permute-start | bytes 786440 | tf_op jit(solution)/shard_map/ppermute | solution.py:292
  17.3 2.2 %collective-permute-start.1 = (bf16[2,2,128,256]{3,2,1,0:T(8,128)(2,1)S(1)}, bf16[2,2,128,256]{3,2,1,0:T(8,128)(2,1)S(1)}, u32[]{:S(2)}, u32[]{:S(2)}) collective-permute-start(bf16[2,2,128,256]{3,2,1,0:T(8,128)(2,1)S(1)} %get-tuple-element.21), channel_id=1, source_target_pairs={{4,9},{5,10},{6,11},{8,5},{9,6},{10,7},{20,25},{21,26},{22,27},{24... | collective-permute-start | bytes 786440 | tf_op jit(solution)/shard_map/ppermute | solution.py:273
  19.5 0.0 collective-permute-done.2.outer_ref
  19.5 0.0 copy-done.2
  19.6 0.0 copy-done
  19.6 1.1 %shard_map.56 = (f32[2,128,256]{2,1,0:T(8,128)S(1)}, f32[2,128,256]{2,1,0:T(8,128)S(1)}) custom-call(bf16[2,4,128,256]{3,2,1,0:T(8,128)(2,1)S(1)} %get-tuple-element.20.x_ref, bf16[2,2,128,256]{3,2,1,0:T(8,128)(2,1)S(1)} %collective-permute-done.2.outer_ref, bf16[3,3,3,256,256]{4,3,2,1,0:T(8,128)(2,1)S(1)} %copy-done, f32[1,1,256]{2,1,0:T(1,128)S(1)} %bitcast.2), custom_call_target="tpu_custom_call" | custom-call | tf_op jit(solution)/shard_map/pallas_call | solution.py:16
  20.7 0.0 copy-start.1
  20.7 0.0 collective-permute-done.4.inner_ref
  20.7 2.0 %shard_map.58 = (f32[4,128,256]{2,1,0:T(8,128)S(1)}, f32[4,128,256]{2,1,0:T(8,128)S(1)}) custom-call(bf16[2,4,128,256]{3,2,1,0:T(8,128)(2,1)S(1)} %get-tuple-element.20.x_ref, bf16[2,2,128,256]{3,2,1,0:T(8,128)(2,1)S(1)} %collective-permute-done.4.inner_ref, bf16[3,3,3,256,256]{4,3,2,1,0:T(8,128)(2,1)S(1)} %copy-done, f32[1,1,256]{2,1,0:T(1,128)S(1)} %bitcast.3), custom_call_target="tpu_custom_call" | custom-call | flops 1811939328 | tf_op jit(solution)/shard_map/pallas_call | solution.py:16
  22.7 0.0 copy-done.1
  22.7 0.2 shard_map.59
  22.9 0.0 collective-permute-done.3.inner_ref
  22.9 1.1 %shard_map.60 = (bf16[2,128,256]{2,1,0:T(8,128)(2,1)S(1)}, bf16[4,128,256]{2,1,0:T(8,128)(2,1)S(1)}, bf16[4,128,256]{2,1,0:T(8,128)(2,1)S(1)}) custom-call(bf16[2,4,128,256]{3,2,1,0:T(8,128)(2,1)S(1)} %collective-permute-done.m_ref, bf16[2,2,128,256]{3,2,1,0:T(8,128)(2,1)S(1)} %collective-permute-done.3.inner_ref, bf16[3,3,3,256,256]{4,3,2,1,0:T(8,128)(2,1)S(1)} %copy-done, ...), custom_call_target="tpu_custom_call" | custom-call | tf_op jit(solution)/shard_map/pallas_call | solution.py:16
  24.0 0.0 collective-permute-done.1.outer_ref
  24.0 0.0 copy-start.3
  24.0 1.1 %shard_map.61 = (bf16[2,128,256]{2,1,0:T(8,128)(2,1)S(1)}, bf16[6,128,256]{2,1,0:T(8,128)(2,1)S(1)}, bf16[6,128,256]{2,1,0:T(8,128)(2,1)S(1)}) custom-call(bf16[2,4,128,256]{3,2,1,0:T(8,128)(2,1)S(1)} %collective-permute-done.m_ref, bf16[2,2,128,256]{3,2,1,0:T(8,128)(2,1)S(1)} %collective-permute-done.1.outer_ref, bf16[3,3,3,256,256]{4,3,2,1,0:T(8,128)(2,1)S(1)} %copy-done, ...), custom_call_target="tpu_custom_call" | custom-call | tf_op jit(solution)/shard_map/pallas_call | solution.py:16
  25.2 6.4 %collective-permute-start.6 = (bf16[2,128,256]{2,1,0:T(8,128)(2,1)S(1)}, bf16[2,128,256]{2,1,0:T(8,128)(2,1)S(1)}, u32[]{:S(2)}, u32[]{:S(2)}) collective-permute-start(bf16[2,128,256]{2,1,0:T(8,128)(2,1)S(1)} %get-tuple-element.34), channel_id=1, source_target_pairs={{0,1},{1,2},{2,3},{4,5},{5,6},{6,7},{8,9},{9,10},{10,11},{12,13},{... | collective-permute-start | bytes 393224 | tf_op jit(solution)/shard_map/ppermute | solution.py:319
  31.5 1.4 %collective-permute-start.5 = (bf16[2,128,256]{2,1,0:T(8,128)(2,1)S(1)}, bf16[2,128,256]{2,1,0:T(8,128)(2,1)S(1)}, u32[]{:S(2)}, u32[]{:S(2)}) collective-permute-start(bf16[2,128,256]{2,1,0:T(8,128)(2,1)S(1)} %get-tuple-element.33), channel_id=1, source_target_pairs={{0,1},{1,2},{2,3},{3,0},{4,5},{5,6},{6,7},{7,4},{8,9},{9,10},{10,1... | collective-permute-start | bytes 393224 | tf_op jit(solution)/shard_map/ppermute | solution.py:311
  32.9 0.0 copy-done.3
  32.9 1.4 %shard_map.62.rest_ref = f32[1,4,128,256]{3,2,1,0:T(8,128)S(1)} custom-call(bf16[2,4,128,256]{3,2,1,0:T(8,128)(2,1)S(1)} %get-tuple-element.20.x_ref, bf16[6,128,256]{2,1,0:T(8,128)(2,1)S(1)} %get-tuple-element.31.h0_ref, bf16[6,128,256]{2,1,0:T(8,128)(2,1)S(1)} %get-tuple-element.32.h1_ref, bf16[3,3,3,256,256]{4,3,2,1,0:T(8,128)(2,1)S(1)} %copy-done.1, ...), custom_call_target="tpu_custom_call" | custom-call | flops 1207959552 | tf_op jit(solution)/shard_map/pallas_call | solution.py:16
  34.3 0.0 collective-permute-done.6.far_ref
  34.3 2.9 %collective-permute-done.5.near_ref = bf16[2,128,256]{2,1,0:T(8,128)(2,1)S(1)} collective-permute-done((bf16[2,128,256]{2,1,0:T(8,128)(2,1)S(1)}, bf16[2,128,256]{2,1,0:T(8,128)(2,1)S(1)}, u32[]{:S(2)}, u32[]{:S(2)}) %collective-permute-start.5) | collective-permute-done | bytes 131104 | tf_op jit(solution)/shard_map/ppermute | solution.py:311
  37.2 0.8 %shard_map.63 = bf16[1,4,128,256]{3,2,1,0:T(8,128)(2,1)} custom-call(f32[1,4,128,256]{3,2,1,0:T(8,128)S(1)} %shard_map.62.rest_ref, bf16[2,128,256]{2,1,0:T(8,128)(2,1)S(1)} %collective-permute-done.5.near_ref, bf16[2,128,256]{2,1,0:T(8,128)(2,1)S(1)} %collective-permute-done.6.far_ref), custom_call_target="tpu_custom_call" | custom-call | tf_op jit(solution)/shard_map/pallas_call | solution.py:16
  (1 shorter events, 0.0 us)
Async XLA Ops:
  0.0 19.6 %copy-start.2 = (f32[256]{0:T(256)S(1)}, f32[256]{0:T(256)}, u32[]{:S(2)}) copy-start(f32[256]{0:T(256)} %param.7) | copy-start | bytes 3076
  0.0 19.6 %copy-start = (bf16[3,3,3,256,256]{4,3,2,1,0:T(8,128)(2,1)S(1)}, bf16[3,3,3,256,256]{4,3,2,1,0:T(8,128)(2,1)}, u32[]{:S(2)}) copy-start(bf16[3,3,3,256,256]{4,3,2,1,0:T(8,128)(2,1)} %w_ref.9) | copy-start | bytes 10616836
  0.0 16.0 %collective-permute-start = (bf16[2,4,128,256]{3,2,1,0:T(8,128)(2,1)}, bf16[2,4,128,256]{3,2,1,0:T(8,128)(2,1)S(1)}, u32[]{:S(2)}, u32[]{:S(2)}) collective-permute-start(bf16[2,4,128,256]{3,2,1,0:T(8,128)(2,1)} %x_ref.1), channel_id=1, source_target_pairs={{0,1},{1,2},{2,3},{3,0},{4,5},{5,6},{6,7},{7,4},{8,9},{9,10},{10,1... | collective-permute-start | bytes 1572872 | tf_op jit(solution)/shard_map/ppermute | solution.py:262
  3.2 16.3 %collective-permute-start.2 = (bf16[2,2,128,256]{3,2,1,0:T(8,128)(2,1)S(1)}, bf16[2,2,128,256]{3,2,1,0:T(8,128)(2,1)S(1)}, u32[]{:S(2)}, u32[]{:S(2)}) collective-permute-start(bf16[2,2,128,256]{3,2,1,0:T(8,128)(2,1)S(1)} %get-tuple-element.21), channel_id=1, source_target_pairs={{4,8},{8,4},{20,24},{24,20},{0,16},{12,28},{16,0},{28,12},{5,9},{9... | collective-permute-start | bytes 786440 | tf_op jit(solution)/shard_map/ppermute | solution.py:272
  5.4 15.3 %collective-permute-start.4 = (bf16[2,2,128,256]{3,2,1,0:T(8,128)(2,1)S(1)}, bf16[2,2,128,256]{3,2,1,0:T(8,128)(2,1)S(1)}, u32[]{:S(2)}, u32[]{:S(2)}) collective-permute-start(bf16[2,2,128,256]{3,2,1,0:T(8,128)(2,1)S(1)} %get-tuple-element.24), channel_id=1, source_target_pairs={{0,4},{8,12},{4,0},{12,8},{1,5},{9,13},{5,1},{13,9},{2,6},{10,14},... | collective-permute-start | bytes 786440 | tf_op jit(solution)/shard_map/ppermute | solution.py:271
  16.0 6.9 %collective-permute-start.3 = (bf16[2,2,128,256]{3,2,1,0:T(8,128)(2,1)S(1)}, bf16[2,2,128,256]{3,2,1,0:T(8,128)(2,1)S(1)}, u32[]{:S(2)}, u32[]{:S(2)}) collective-permute-start(bf16[2,2,128,256]{3,2,1,0:T(8,128)(2,1)S(1)} %shard_map.57), channel_id=1, source_target_pairs={{0,4},{8,12},{4,0},{12,8},{1,5},{9,13},{5,1},{13,9},{2,6},{10,14},... | collective-permute-start | bytes 786440 | tf_op jit(solution)/shard_map/ppermute | solution.py:292
  17.3 6.7 %collective-permute-start.1 = (bf16[2,2,128,256]{3,2,1,0:T(8,128)(2,1)S(1)}, bf16[2,2,128,256]{3,2,1,0:T(8,128)(2,1)S(1)}, u32[]{:S(2)}, u32[]{:S(2)}) collective-permute-start(bf16[2,2,128,256]{3,2,1,0:T(8,128)(2,1)S(1)} %get-tuple-element.21), channel_id=1, source_target_pairs={{4,9},{5,10},{6,11},{8,5},{9,6},{10,7},{20,25},{21,26},{22,27},{24... | collective-permute-start | bytes 786440 | tf_op jit(solution)/shard_map/ppermute | solution.py:273
  20.7 2.0 %copy-start.1 = (bf16[3,3,3,256,256]{4,3,2,1,0:T(8,128)(2,1)S(1)}, bf16[3,3,3,256,256]{4,3,2,1,0:T(8,128)(2,1)}, u32[]{:S(2)}) copy-start(bf16[3,3,3,256,256]{4,3,2,1,0:T(8,128)(2,1)} %v_ref.5) | copy-start | bytes 10616836
  24.0 8.8 %copy-start.3 = (f32[256]{0:T(256)S(1)}, f32[256]{0:T(256)}, u32[]{:S(2)}) copy-start(f32[256]{0:T(256)} %param.9) | copy-start | bytes 3076
  25.2 9.1 %collective-permute-start.6 = (bf16[2,128,256]{2,1,0:T(8,128)(2,1)S(1)}, bf16[2,128,256]{2,1,0:T(8,128)(2,1)S(1)}, u32[]{:S(2)}, u32[]{:S(2)}) collective-permute-start(bf16[2,128,256]{2,1,0:T(8,128)(2,1)S(1)} %get-tuple-element.34), channel_id=1, source_target_pairs={{0,1},{1,2},{2,3},{4,5},{5,6},{6,7},{8,9},{9,10},{10,11},{12,13},{... | collective-permute-start | bytes 393224 | tf_op jit(solution)/shard_map/ppermute | solution.py:319
  31.5 5.7 %collective-permute-start.5 = (bf16[2,128,256]{2,1,0:T(8,128)(2,1)S(1)}, bf16[2,128,256]{2,1,0:T(8,128)(2,1)S(1)}, u32[]{:S(2)}, u32[]{:S(2)}) collective-permute-start(bf16[2,128,256]{2,1,0:T(8,128)(2,1)S(1)} %get-tuple-element.33), channel_id=1, source_target_pairs={{0,1},{1,2},{2,3},{3,0},{4,5},{5,6},{6,7},{7,4},{8,9},{9,10},{10,1... | collective-permute-start | bytes 393224 | tf_op jit(solution)/shard_map/ppermute | solution.py:311

commit v3 on v2

--- a/solution.py
+++ b/solution.py
@@ -229,13 +229,13 @@
     out_ref[0] = total * 0.5 + b_ref[...]
 
 
-def join_body(rest_ref, near_ref, far_ref, out_ref):
+def join_body(rest_ref, near_ref, odd_ref, even_ref, out_ref):
     rows = rest_ref.shape[1]
     odd = parity()
-    first = lax.axis_index("tm") == 0
-    for part_ref, start in ((near_ref, 2 * (1 - odd)), (far_ref, odd * (rows - 2))):
-        part = part_ref[...].astype(jnp.float32)
-        part = jnp.where(first, jnp.zeros_like(part), part)
+    time = lax.axis_index("tm")
+    far = jnp.where(lax.rem(time, 2) == 1, odd_ref[...], even_ref[...])
+    for part, start in ((near_ref[...], 2 * (1 - odd)), (far, odd * (rows - 2))):
+        part = jnp.where(time == 0, jnp.zeros_like(part), part).astype(jnp.float32)
         place = pl.ds(start, part.shape[0])
         out_ref[0, place] = (rest_ref[0, place] + 0.5 * part).astype(jnp.bfloat16)
 
@@ -255,6 +255,16 @@
     outer_full += [(c * tiles + i, (c + 1) % clips * tiles + i) for c in range(clips) for i in unpaired]
     diagonal = [(i * times + s, j * times + t) for i, j in outer_pairs for s, t in forward]
 
+    def swaps(first):
+        turns = {}
+        for t in range(first, times - 1, 2):
+            turns[t], turns[t + 1] = t + 1, t
+        return [
+            (c * times + t, c * times + turns[t] if t in turns else (c + 1) % clips * times + t)
+            for c in range(clips)
+            for t in range(times)
+        ]
+
     def frames(*lead, dtype=jnp.bfloat16):
         return jax.ShapeDtypeStruct((*lead, cols, channels), dtype)
 
@@ -316,14 +326,15 @@
         0,
         scratch=sums(2),
     )
-    far_part = lax.ppermute(far_send, "tm", forward)
+    far_odd = lax.ppermute(far_send, ("clips", "tm"), swaps(0))
+    far_even = lax.ppermute(far_send, ("clips", "tm"), swaps(1))
     (rest,) = call(
         rest_body,
         [frames(1, rows, dtype=f32)],
         (x, h0, h1, weight_second, bias_second),
         2 * unit * rows,
     )
-    (pooled,) = call(join_body, [frames(1, rows)], (rest, near_part, far_part), 0)
+    (pooled,) = call(join_body, [frames(1, rows)], (rest, near_part, far_odd, far_even), 0)
     return pooled
 
 

time: 38.2 us -> 37.9 us (level)
  starting transfers between devices: 15.9 us -> 14.1 us
  waiting for transfers between devices: 13.1 us -> 14.7 us
    ppermute x1 -> x2, waiting for transfers between devices: 0.01 us -> 1.31 us  [the longest x1 1.31 us: block(): far_even = lax.ppermute(far_send, ('clips', 'tm'), swaps(1))]
    ppermute x1, starting transfers between devices: 1.35 us -> 0.17 us  [block(): near_part = lax.ppermute(near_send, 'tm', ring)]
    ppermute x1 -> x2, starting transfers between devices: 6.36 us -> 5.73 us  [the longest x1 4.52 us: block(): far_odd = lax.ppermute(far_send, ('clips', 'tm'), swaps(0))]
  transfers between devices with their start and end apart: 7 -> 8, of which waited for: 2 -> 3; matrix products, arithmetic and copies ran while one was open for 0% -> 0% of each run, Pallas kernels for 18% -> 18%
where the time goes in v3:
time: 37.9 us; the launch traced here: 37.7 us
  waiting for transfers between devices  14.7 us (39%)
  starting transfers between devices  14.1 us (37%)
  Pallas kernels  8.8 us (23%)
    ppermute x1, waiting for transfers between devices, block(): earlier = lax.ppermute(x, 'tm', ring)  10.2 us
    pallas_call x9, Pallas kernels, call(): pl.pallas_call(body, out_shape=outs, in_specs=in_specs or [VMEM] * len(ar...  8.8 us
    ppermute x1, starting transfers between devices, block(): far_odd = lax.ppermute(far_send, ('clips', 'tm'), swaps(0))  4.52 us
    ppermute x1, waiting for transfers between devices, block(): near_part = lax.ppermute(near_send, 'tm', ring)  3.18 us
    ppermute x1, starting transfers between devices, block(): corner = lax.ppermute(outer_edge, ('tile', 'tm'), diagonal)  2.21 us
    ppermute x1, starting transfers between devices, block(): outer = lax.ppermute(outer_edge, ('clips', 'tile'), outer_full)  2.14 us
    ppermute x1, starting transfers between devices, block(): earlier = lax.ppermute(x, 'tm', ring)  2.11 us
    ppermute x1, starting transfers between devices, block(): inner_corner = lax.ppermute(inner_edge, 'tile', inner_pairs)  1.32 us
  transfers between devices with their start and end apart: 8, of which 3 were waited for; matrix products, arithmetic and copies ran while one was open for 0% of the time, Pallas kernels for 18%

profile of v3, /device:TPU:1, one launch (start us, length us, event | category | flops | bytes accessed | tf_op | source)
XLA Modules:
  0.0 37.7 jit_solution(13692174683545435438)
XLA Ops:
  0.0 0.0 copy-start.2
  0.0 0.0 copy-start
  0.0 2.1 %collective-permute-start = (bf16[2,4,128,256]{3,2,1,0:T(8,128)(2,1)}, bf16[2,4,128,256]{3,2,1,0:T(8,128)(2,1)S(1)}, u32[]{:S(2)}, u32[]{:S(2)}) collective-permute-start(bf16[2,4,128,256]{3,2,1,0:T(8,128)(2,1)} %x_ref.1), channel_id=1, source_target_pairs={{0,1},{1,2},{2,3},{3,0},{4,5},{5,6},{6,7},{7,4},{8,9},{9,10},{10,1... | collective-permute-start | bytes 1572872 | tf_op jit(solution)/shard_map/ppermute | solution.py:272
  2.1 1.1 %shard_map.55 = (bf16[2,4,128,256]{3,2,1,0:T(8,128)(2,1)S(1)}, bf16[2,2,128,256]{3,2,1,0:T(8,128)(2,1)S(1)}, bf16[2,2,128,256]{3,2,1,0:T(8,128)(2,1)S(1)}) custom-call(bf16[2,4,128,256]{3,2,1,0:T(8,128)(2,1)} %x_ref.1), custom_call_target="tpu_custom_call" | custom-call | flops 10000000000 | tf_op jit(solution)/shard_map/pallas_call | solution.py:16
  3.2 2.1 %collective-permute-start.2 = (bf16[2,2,128,256]{3,2,1,0:T(8,128)(2,1)S(1)}, bf16[2,2,128,256]{3,2,1,0:T(8,128)(2,1)S(1)}, u32[]{:S(2)}, u32[]{:S(2)}) collective-permute-start(bf16[2,2,128,256]{3,2,1,0:T(8,128)(2,1)S(1)} %get-tuple-element.21), channel_id=1, source_target_pairs={{4,8},{8,4},{20,24},{24,20},{0,16},{12,28},{16,0},{28,12},{5,9},{9... | collective-permute-start | bytes 786440 | tf_op jit(solution)/shard_map/ppermute | solution.py:282
  5.4 0.4 collective-permute-start.4
  5.8 10.2 %collective-permute-done.m_ref = bf16[2,4,128,256]{3,2,1,0:T(8,128)(2,1)S(1)} collective-permute-done((bf16[2,4,128,256]{3,2,1,0:T(8,128)(2,1)}, bf16[2,4,128,256]{3,2,1,0:T(8,128)(2,1)S(1)}, u32[]{:S(2)}, u32[]{:S(2)}) %collective-permute-start) | collective-permute-done | bytes 524320 | tf_op jit(solution)/shard_map/ppermute | solution.py:272
  16.0 1.3 %collective-permute-start.3 = (bf16[2,2,128,256]{3,2,1,0:T(8,128)(2,1)S(1)}, bf16[2,2,128,256]{3,2,1,0:T(8,128)(2,1)S(1)}, u32[]{:S(2)}, u32[]{:S(2)}) collective-permute-start(bf16[2,2,128,256]{3,2,1,0:T(8,128)(2,1)S(1)} %shard_map.57), channel_id=1, source_target_pairs={{0,4},{8,12},{4,0},{12,8},{1,5},{9,13},{5,1},{13,9},{2,6},{10,14},... | collective-permute-start | bytes 786440 | tf_op jit(solution)/shard_map/ppermute | solution.py:302
  17.3 2.2 %collective-permute-start.1 = (bf16[2,2,128,256]{3,2,1,0:T(8,128)(2,1)S(1)}, bf16[2,2,128,256]{3,2,1,0:T(8,128)(2,1)S(1)}, u32[]{:S(2)}, u32[]{:S(2)}) collective-permute-start(bf16[2,2,128,256]{3,2,1,0:T(8,128)(2,1)S(1)} %get-tuple-element.21), channel_id=1, source_target_pairs={{4,9},{5,10},{6,11},{8,5},{9,6},{10,7},{20,25},{21,26},{22,27},{24... | collective-permute-start | bytes 786440 | tf_op jit(solution)/shard_map/ppermute | solution.py:283
  19.5 0.0 collective-permute-done.2.outer_ref
  19.5 0.0 copy-done.2
  19.6 0.0 copy-done
  19.6 1.1 %shard_map.56 = (f32[2,128,256]{2,1,0:T(8,128)S(1)}, f32[2,128,256]{2,1,0:T(8,128)S(1)}) custom-call(bf16[2,4,128,256]{3,2,1,0:T(8,128)(2,1)S(1)} %get-tuple-element.20.x_ref, bf16[2,2,128,256]{3,2,1,0:T(8,128)(2,1)S(1)} %collective-permute-done.2.outer_ref, bf16[3,3,3,256,256]{4,3,2,1,0:T(8,128)(2,1)S(1)} %copy-done, f32[1,1,256]{2,1,0:T(1,128)S(1)} %bitcast.2), custom_call_target="tpu_custom_call" | custom-call | tf_op jit(solution)/shard_map/pallas_call | solution.py:16
  20.7 0.0 copy-start.1
  20.7 0.0 collective-permute-done.4.inner_ref
  20.7 2.0 %shard_map.58 = (f32[4,128,256]{2,1,0:T(8,128)S(1)}, f32[4,128,256]{2,1,0:T(8,128)S(1)}) custom-call(bf16[2,4,128,256]{3,2,1,0:T(8,128)(2,1)S(1)} %get-tuple-element.20.x_ref, bf16[2,2,128,256]{3,2,1,0:T(8,128)(2,1)S(1)} %collective-permute-done.4.inner_ref, bf16[3,3,3,256,256]{4,3,2,1,0:T(8,128)(2,1)S(1)} %copy-done, f32[1,1,256]{2,1,0:T(1,128)S(1)} %bitcast.3), custom_call_target="tpu_custom_call" | custom-call | flops 1811939328 | tf_op jit(solution)/shard_map/pallas_call | solution.py:16
  22.7 0.0 copy-done.1
  22.7 0.2 shard_map.59
  22.9 0.0 collective-permute-done.3.inner_ref
  22.9 1.1 %shard_map.60 = (bf16[2,128,256]{2,1,0:T(8,128)(2,1)S(1)}, bf16[4,128,256]{2,1,0:T(8,128)(2,1)S(1)}, bf16[4,128,256]{2,1,0:T(8,128)(2,1)S(1)}) custom-call(bf16[2,4,128,256]{3,2,1,0:T(8,128)(2,1)S(1)} %collective-permute-done.m_ref, bf16[2,2,128,256]{3,2,1,0:T(8,128)(2,1)S(1)} %collective-permute-done.3.inner_ref, bf16[3,3,3,256,256]{4,3,2,1,0:T(8,128)(2,1)S(1)} %copy-done, ...), custom_call_target="tpu_custom_call" | custom-call | tf_op jit(solution)/shard_map/pallas_call | solution.py:16
  24.0 0.0 collective-permute-done.1.outer_ref
  24.0 0.0 copy-start.3
  24.0 1.1 %shard_map.61 = (bf16[2,128,256]{2,1,0:T(8,128)(2,1)S(1)}, bf16[6,128,256]{2,1,0:T(8,128)(2,1)S(1)}, bf16[6,128,256]{2,1,0:T(8,128)(2,1)S(1)}) custom-call(bf16[2,4,128,256]{3,2,1,0:T(8,128)(2,1)S(1)} %collective-permute-done.m_ref, bf16[2,2,128,256]{3,2,1,0:T(8,128)(2,1)S(1)} %collective-permute-done.1.outer_ref, bf16[3,3,3,256,256]{4,3,2,1,0:T(8,128)(2,1)S(1)} %copy-done, ...), custom_call_target="tpu_custom_call" | custom-call | tf_op jit(solution)/shard_map/pallas_call | solution.py:16
  25.2 4.5 %collective-permute-start.6 = (bf16[2,128,256]{2,1,0:T(8,128)(2,1)S(1)}, bf16[2,128,256]{2,1,0:T(8,128)(2,1)S(1)}, u32[]{:S(2)}, u32[]{:S(2)}) collective-permute-start(bf16[2,128,256]{2,1,0:T(8,128)(2,1)S(1)} %get-tuple-element.34), channel_id=1, source_target_pairs={{0,1},{1,0},{2,3},{3,2},{16,17},{17,16},{18,19},{19,18},{4,5},{5,4... | collective-permute-start | bytes 393224 | tf_op jit(solution)/shard_map/ppermute | solution.py:329
  29.7 1.2 %collective-permute-start.7 = (bf16[2,128,256]{2,1,0:T(8,128)(2,1)S(1)}, bf16[2,128,256]{2,1,0:T(8,128)(2,1)S(1)}, u32[]{:S(2)}, u32[]{:S(2)}) collective-permute-start(bf16[2,128,256]{2,1,0:T(8,128)(2,1)S(1)} %get-tuple-element.34), channel_id=1, source_target_pairs={{0,16},{1,2},{2,1},{3,19},{16,0},{17,18},{18,17},{19,3},{4,20},{5,... | collective-permute-start | bytes 393224 | tf_op jit(solution)/shard_map/ppermute | solution.py:330
  30.9 0.2 collective-permute-start.5
  31.1 0.0 copy-done.3
  31.1 1.4 %shard_map.62.rest_ref = f32[1,4,128,256]{3,2,1,0:T(8,128)S(1)} custom-call(bf16[2,4,128,256]{3,2,1,0:T(8,128)(2,1)S(1)} %get-tuple-element.20.x_ref, bf16[6,128,256]{2,1,0:T(8,128)(2,1)S(1)} %get-tuple-element.31.h0_ref, bf16[6,128,256]{2,1,0:T(8,128)(2,1)S(1)} %get-tuple-element.32.h1_ref, bf16[3,3,3,256,256]{4,3,2,1,0:T(8,128)(2,1)S(1)} %copy-done.1, ...), custom_call_target="tpu_custom_call" | custom-call | flops 1207959552 | tf_op jit(solution)/shard_map/pallas_call | solution.py:16
  32.5 0.0 collective-permute-done.6.odd_ref
  32.5 1.3 %collective-permute-done.7.even_ref = bf16[2,128,256]{2,1,0:T(8,128)(2,1)S(1)} collective-permute-done((bf16[2,128,256]{2,1,0:T(8,128)(2,1)S(1)}, bf16[2,128,256]{2,1,0:T(8,128)(2,1)S(1)}, u32[]{:S(2)}, u32[]{:S(2)}) %collective-permute-start.7) | collective-permute-done | bytes 131104 | tf_op jit(solution)/shard_map/ppermute | solution.py:330
  33.8 3.2 %collective-permute-done.5.near_ref = bf16[2,128,256]{2,1,0:T(8,128)(2,1)S(1)} collective-permute-done((bf16[2,128,256]{2,1,0:T(8,128)(2,1)S(1)}, bf16[2,128,256]{2,1,0:T(8,128)(2,1)S(1)}, u32[]{:S(2)}, u32[]{:S(2)}) %collective-permute-start.5) | collective-permute-done | bytes 131104 | tf_op jit(solution)/shard_map/ppermute | solution.py:321
  37.0 0.8 %shard_map.63 = bf16[1,4,128,256]{3,2,1,0:T(8,128)(2,1)} custom-call(f32[1,4,128,256]{3,2,1,0:T(8,128)S(1)} %shard_map.62.rest_ref, bf16[2,128,256]{2,1,0:T(8,128)(2,1)S(1)} %collective-permute-done.5.near_ref, bf16[2,128,256]{2,1,0:T(8,128)(2,1)S(1)} %collective-permute-done.6.odd_ref, bf16[2,128,256]{2,1,0:T(8,128)(2,1)S(1)} %collective-permute-done.7.even_ref), custom_call_target="tpu_custom_call" | custom-call | tf_op jit(solution)/shard_map/pallas_call | solution.py:16
  (1 shorter events, 0.0 us)
Async XLA Ops:
  0.0 19.6 %copy-start.2 = (f32[256]{0:T(256)S(1)}, f32[256]{0:T(256)}, u32[]{:S(2)}) copy-start(f32[256]{0:T(256)} %param.7) | copy-start | bytes 3076
  0.0 19.6 %copy-start = (bf16[3,3,3,256,256]{4,3,2,1,0:T(8,128)(2,1)S(1)}, bf16[3,3,3,256,256]{4,3,2,1,0:T(8,128)(2,1)}, u32[]{:S(2)}) copy-start(bf16[3,3,3,256,256]{4,3,2,1,0:T(8,128)(2,1)} %w_ref.9) | copy-start | bytes 10616836
  0.0 16.0 %collective-permute-start = (bf16[2,4,128,256]{3,2,1,0:T(8,128)(2,1)}, bf16[2,4,128,256]{3,2,1,0:T(8,128)(2,1)S(1)}, u32[]{:S(2)}, u32[]{:S(2)}) collective-permute-start(bf16[2,4,128,256]{3,2,1,0:T(8,128)(2,1)} %x_ref.1), channel_id=1, source_target_pairs={{0,1},{1,2},{2,3},{3,0},{4,5},{5,6},{6,7},{7,4},{8,9},{9,10},{10,1... | collective-permute-start | bytes 1572872 | tf_op jit(solution)/shard_map/ppermute | solution.py:272
  3.2 16.3 %collective-permute-start.2 = (bf16[2,2,128,256]{3,2,1,0:T(8,128)(2,1)S(1)}, bf16[2,2,128,256]{3,2,1,0:T(8,128)(2,1)S(1)}, u32[]{:S(2)}, u32[]{:S(2)}) collective-permute-start(bf16[2,2,128,256]{3,2,1,0:T(8,128)(2,1)S(1)} %get-tuple-element.21), channel_id=1, source_target_pairs={{4,8},{8,4},{20,24},{24,20},{0,16},{12,28},{16,0},{28,12},{5,9},{9... | collective-permute-start | bytes 786440 | tf_op jit(solution)/shard_map/ppermute | solution.py:282
  5.4 15.3 %collective-permute-start.4 = (bf16[2,2,128,256]{3,2,1,0:T(8,128)(2,1)S(1)}, bf16[2,2,128,256]{3,2,1,0:T(8,128)(2,1)S(1)}, u32[]{:S(2)}, u32[]{:S(2)}) collective-permute-start(bf16[2,2,128,256]{3,2,1,0:T(8,128)(2,1)S(1)} %get-tuple-element.24), channel_id=1, source_target_pairs={{0,4},{8,12},{4,0},{12,8},{1,5},{9,13},{5,1},{13,9},{2,6},{10,14},... | collective-permute-start | bytes 786440 | tf_op jit(solution)/shard_map/ppermute | solution.py:281
  16.0 6.9 %collective-permute-start.3 = (bf16[2,2,128,256]{3,2,1,0:T(8,128)(2,1)S(1)}, bf16[2,2,128,256]{3,2,1,0:T(8,128)(2,1)S(1)}, u32[]{:S(2)}, u32[]{:S(2)}) collective-permute-start(bf16[2,2,128,256]{3,2,1,0:T(8,128)(2,1)S(1)} %shard_map.57), channel_id=1, source_target_pairs={{0,4},{8,12},{4,0},{12,8},{1,5},{9,13},{5,1},{13,9},{2,6},{10,14},... | collective-permute-start | bytes 786440 | tf_op jit(solution)/shard_map/ppermute | solution.py:302
  17.3 6.7 %collective-permute-start.1 = (bf16[2,2,128,256]{3,2,1,0:T(8,128)(2,1)S(1)}, bf16[2,2,128,256]{3,2,1,0:T(8,128)(2,1)S(1)}, u32[]{:S(2)}, u32[]{:S(2)}) collective-permute-start(bf16[2,2,128,256]{3,2,1,0:T(8,128)(2,1)S(1)} %get-tuple-element.21), channel_id=1, source_target_pairs={{4,9},{5,10},{6,11},{8,5},{9,6},{10,7},{20,25},{21,26},{22,27},{24... | collective-permute-start | bytes 786440 | tf_op jit(solution)/shard_map/ppermute | solution.py:283
  20.7 2.0 %copy-start.1 = (bf16[3,3,3,256,256]{4,3,2,1,0:T(8,128)(2,1)S(1)}, bf16[3,3,3,256,256]{4,3,2,1,0:T(8,128)(2,1)}, u32[]{:S(2)}) copy-start(bf16[3,3,3,256,256]{4,3,2,1,0:T(8,128)(2,1)} %v_ref.5) | copy-start | bytes 10616836
  24.0 7.0 %copy-start.3 = (f32[256]{0:T(256)S(1)}, f32[256]{0:T(256)}, u32[]{:S(2)}) copy-start(f32[256]{0:T(256)} %param.9) | copy-start | bytes 3076
  25.2 7.3 %collective-permute-start.6 = (bf16[2,128,256]{2,1,0:T(8,128)(2,1)S(1)}, bf16[2,128,256]{2,1,0:T(8,128)(2,1)S(1)}, u32[]{:S(2)}, u32[]{:S(2)}) collective-permute-start(bf16[2,128,256]{2,1,0:T(8,128)(2,1)S(1)} %get-tuple-element.34), channel_id=1, source_target_pairs={{0,1},{1,0},{2,3},{3,2},{16,17},{17,16},{18,19},{19,18},{4,5},{5,4... | collective-permute-start | bytes 393224 | tf_op jit(solution)/shard_map/ppermute | solution.py:329
  29.7 4.1 %collective-permute-start.7 = (bf16[2,128,256]{2,1,0:T(8,128)(2,1)S(1)}, bf16[2,128,256]{2,1,0:T(8,128)(2,1)S(1)}, u32[]{:S(2)}, u32[]{:S(2)}) collective-permute-start(bf16[2,128,256]{2,1,0:T(8,128)(2,1)S(1)} %get-tuple-element.34), channel_id=1, source_target_pairs={{0,16},{1,2},{2,1},{3,19},{16,0},{17,18},{18,17},{19,3},{4,20},{5,... | collective-permute-start | bytes 393224 | tf_op jit(solution)/shard_map/ppermute | solution.py:330
  30.9 6.1 %collective-permute-start.5 = (bf16[2,128,256]{2,1,0:T(8,128)(2,1)S(1)}, bf16[2,128,256]{2,1,0:T(8,128)(2,1)S(1)}, u32[]{:S(2)}, u32[]{:S(2)}) collective-permute-start(bf16[2,128,256]{2,1,0:T(8,128)(2,1)S(1)} %get-tuple-element.33), channel_id=1, source_target_pairs={{0,1},{1,2},{2,3},{3,0},{4,5},{5,6},{6,7},{7,4},{8,9},{9,10},{10,1... | collective-permute-start | bytes 393224 | tf_op jit(solution)/shard_map/ppermute | solution.py:321

commit v4 on v2

--- a/solution.py
+++ b/solution.py
@@ -253,7 +253,14 @@
     unpaired = [i for i in range(tiles) if i not in paired]
     outer_full = [(c * tiles + i, c * tiles + j) for c in range(clips) for i, j in outer_pairs]
     outer_full += [(c * tiles + i, (c + 1) % clips * tiles + i) for c in range(clips) for i in unpaired]
-    diagonal = [(i * times + s, j * times + t) for i, j in outer_pairs for s, t in forward]
+    outer_tiles = [(c * tiles + i, c * tiles + j) for c in range(clips) for i, j in outer_pairs]
+    diagonal = [(i * times + s, j * times + t) for i, j in outer_tiles for s, t in ring]
+    diagonal += [
+        (i * times + t, j * times + t)
+        for i, j in outer_full
+        if i % tiles in unpaired
+        for t in range(times)
+    ]
 
     def frames(*lead, dtype=jnp.bfloat16):
         return jax.ShapeDtypeStruct((*lead, cols, channels), dtype)
@@ -270,7 +277,7 @@
     )
     inner = lax.ppermute(inner_edge, "tile", inner_pairs)
     outer = lax.ppermute(outer_edge, ("clips", "tile"), outer_full)
-    corner = lax.ppermute(outer_edge, ("tile", "tm"), diagonal)
+    corner = lax.ppermute(outer_edge, ("clips", "tile", "tm"), diagonal)
 
     bias_first = bias_first.reshape(1, 1, -1)
     bias_second = bias_second.reshape(1, 1, -1)

time: 38.2 us -> 38.4 us (level)
  the two profiles are of different devices: /device:TPU:1 before, /device:TPU:0 now
where the time goes in v4:
time: 38.4 us; the launch traced here: 38.2 us
  waiting for transfers between devices  16.8 us (44%)
  starting transfers between devices  12.4 us (32%)
  Pallas kernels  8.8 us (23%)
    ppermute x1, waiting for transfers between devices, block(): earlier = lax.ppermute(x, 'tm', ring)  11.3 us
    pallas_call x9, Pallas kernels, call(): pl.pallas_call(body, out_shape=outs, in_specs=in_specs or [VMEM] * len(ar...  8.8 us
    ppermute x1, waiting for transfers between devices, block(): near_part = lax.ppermute(near_send, 'tm', ring)  4.46 us
    ppermute x1, starting transfers between devices, block(): far_part = lax.ppermute(far_send, 'tm', forward)  4.41 us
    ppermute x1, starting transfers between devices, block(): earlier = lax.ppermute(x, 'tm', ring)  3.05 us
    ppermute x1, starting transfers between devices, block(): near_part = lax.ppermute(near_send, 'tm', ring)  1.63 us
    ppermute x1, starting transfers between devices, block(): outer = lax.ppermute(outer_edge, ('clips', 'tile'), outer_full)  1.56 us
    ppermute x1, starting transfers between devices, block(): corner = lax.ppermute(outer_edge, ('clips', 'tile', 'tm'), diagonal)  1.54 us
  transfers between devices with their start and end apart: 7, of which 4 were waited for; matrix products, arithmetic and copies ran while one was open for 0% of the time, Pallas kernels for 18%

profile of v4, /device:TPU:0, one launch (start us, length us, event | category | flops | bytes accessed | tf_op | source)
XLA Modules:
  0.0 38.2 jit_solution(1406847363244370931)
XLA Ops:
  0.0 0.0 copy-start.2
  0.0 0.0 copy-start
  0.0 3.1 %collective-permute-start = (bf16[2,4,128,256]{3,2,1,0:T(8,128)(2,1)}, bf16[2,4,128,256]{3,2,1,0:T(8,128)(2,1)S(1)}, u32[]{:S(2)}, u32[]{:S(2)}) collective-permute-start(bf16[2,4,128,256]{3,2,1,0:T(8,128)(2,1)} %x_ref.1), channel_id=1, source_target_pairs={{0,1},{1,2},{2,3},{3,0},{4,5},{5,6},{6,7},{7,4},{8,9},{9,10},{10,1... | collective-permute-start | bytes 1572872 | tf_op jit(solution)/shard_map/ppermute | solution.py:269
  3.1 1.1 %shard_map.55 = (bf16[2,4,128,256]{3,2,1,0:T(8,128)(2,1)S(1)}, bf16[2,2,128,256]{3,2,1,0:T(8,128)(2,1)S(1)}, bf16[2,2,128,256]{3,2,1,0:T(8,128)(2,1)S(1)}) custom-call(bf16[2,4,128,256]{3,2,1,0:T(8,128)(2,1)} %x_ref.1), custom_call_target="tpu_custom_call" | custom-call | flops 10000000000 | tf_op jit(solution)/shard_map/pallas_call | solution.py:16
  4.2 1.6 %collective-permute-start.2 = (bf16[2,2,128,256]{3,2,1,0:T(8,128)(2,1)S(1)}, bf16[2,2,128,256]{3,2,1,0:T(8,128)(2,1)S(1)}, u32[]{:S(2)}, u32[]{:S(2)}) collective-permute-start(bf16[2,2,128,256]{3,2,1,0:T(8,128)(2,1)S(1)} %get-tuple-element.21), channel_id=1, source_target_pairs={{4,8},{8,4},{20,24},{24,20},{0,16},{12,28},{16,0},{28,12},{5,9},{9... | collective-permute-start | bytes 786440 | tf_op jit(solution)/shard_map/ppermute | solution.py:279
  5.7 0.1 collective-permute-start.4
  5.9 11.3 %collective-permute-done.m_ref = bf16[2,4,128,256]{3,2,1,0:T(8,128)(2,1)S(1)} collective-permute-done((bf16[2,4,128,256]{3,2,1,0:T(8,128)(2,1)}, bf16[2,4,128,256]{3,2,1,0:T(8,128)(2,1)S(1)}, u32[]{:S(2)}, u32[]{:S(2)}) %collective-permute-start) | collective-permute-done | bytes 524320 | tf_op jit(solution)/shard_map/ppermute | solution.py:269
  17.2 0.1 collective-permute-start.3
  17.3 1.5 %collective-permute-start.1 = (bf16[2,2,128,256]{3,2,1,0:T(8,128)(2,1)S(1)}, bf16[2,2,128,256]{3,2,1,0:T(8,128)(2,1)S(1)}, u32[]{:S(2)}, u32[]{:S(2)}) collective-permute-start(bf16[2,2,128,256]{3,2,1,0:T(8,128)(2,1)S(1)} %get-tuple-element.21), channel_id=1, source_target_pairs={{4,9},{5,10},{6,11},{7,8},{8,5},{9,6},{10,7},{11,4},{20,25},{21,26... | collective-permute-start | bytes 786440 | tf_op jit(solution)/shard_map/ppermute | solution.py:280
  18.9 0.0 collective-permute-done.2.outer_ref
  18.9 0.0 copy-done.2
  18.9 0.0 copy-done
  18.9 1.1 %shard_map.56 = (f32[2,128,256]{2,1,0:T(8,128)S(1)}, f32[2,128,256]{2,1,0:T(8,128)S(1)}) custom-call(bf16[2,4,128,256]{3,2,1,0:T(8,128)(2,1)S(1)} %get-tuple-element.20.x_ref, bf16[2,2,128,256]{3,2,1,0:T(8,128)(2,1)S(1)} %collective-permute-done.2.outer_ref, bf16[3,3,3,256,256]{4,3,2,1,0:T(8,128)(2,1)S(1)} %copy-done, f32[1,1,256]{2,1,0:T(1,128)S(1)} %bitcast.2), custom_call_target="tpu_custom_call" | custom-call | tf_op jit(solution)/shard_map/pallas_call | solution.py:16
  20.0 0.0 copy-start.1
  20.0 0.0 collective-permute-done.4.inner_ref
  20.0 2.0 %shard_map.58 = (f32[4,128,256]{2,1,0:T(8,128)S(1)}, f32[4,128,256]{2,1,0:T(8,128)S(1)}) custom-call(bf16[2,4,128,256]{3,2,1,0:T(8,128)(2,1)S(1)} %get-tuple-element.20.x_ref, bf16[2,2,128,256]{3,2,1,0:T(8,128)(2,1)S(1)} %collective-permute-done.4.inner_ref, bf16[3,3,3,256,256]{4,3,2,1,0:T(8,128)(2,1)S(1)} %copy-done, f32[1,1,256]{2,1,0:T(1,128)S(1)} %bitcast.3), custom_call_target="tpu_custom_call" | custom-call | flops 1811939328 | tf_op jit(solution)/shard_map/pallas_call | solution.py:16
  22.0 0.0 copy-done.1
  22.0 0.2 shard_map.59
  22.2 0.0 collective-permute-done.3.inner_ref
  22.2 1.1 %shard_map.60 = (bf16[2,128,256]{2,1,0:T(8,128)(2,1)S(1)}, bf16[4,128,256]{2,1,0:T(8,128)(2,1)S(1)}, bf16[4,128,256]{2,1,0:T(8,128)(2,1)S(1)}) custom-call(bf16[2,4,128,256]{3,2,1,0:T(8,128)(2,1)S(1)} %collective-permute-done.m_ref, bf16[2,2,128,256]{3,2,1,0:T(8,128)(2,1)S(1)} %collective-permute-done.3.inner_ref, bf16[3,3,3,256,256]{4,3,2,1,0:T(8,128)(2,1)S(1)} %copy-done, ...), custom_call_target="tpu_custom_call" | custom-call | tf_op jit(solution)/shard_map/pallas_call | solution.py:16
  23.3 0.4 %collective-permute-done.1.outer_ref = bf16[2,2,128,256]{3,2,1,0:T(8,128)(2,1)S(1)} collective-permute-done((bf16[2,2,128,256]{3,2,1,0:T(8,128)(2,1)S(1)}, bf16[2,2,128,256]{3,2,1,0:T(8,128)(2,1)S(1)}, u32[]{:S(2)}, u32[]{:S(2)}) %collective-permute-start.1) | collective-permute-done | bytes 262176 | tf_op jit(solution)/shard_map/ppermute | solution.py:280
  23.7 0.0 copy-start.3
  23.7 1.1 %shard_map.61 = (bf16[2,128,256]{2,1,0:T(8,128)(2,1)S(1)}, bf16[6,128,256]{2,1,0:T(8,128)(2,1)S(1)}, bf16[6,128,256]{2,1,0:T(8,128)(2,1)S(1)}) custom-call(bf16[2,4,128,256]{3,2,1,0:T(8,128)(2,1)S(1)} %collective-permute-done.m_ref, bf16[2,2,128,256]{3,2,1,0:T(8,128)(2,1)S(1)} %collective-permute-done.1.outer_ref, bf16[3,3,3,256,256]{4,3,2,1,0:T(8,128)(2,1)S(1)} %copy-done, ...), custom_call_target="tpu_custom_call" | custom-call | tf_op jit(solution)/shard_map/pallas_call | solution.py:16
  24.8 4.4 %collective-permute-start.6 = (bf16[2,128,256]{2,1,0:T(8,128)(2,1)S(1)}, bf16[2,128,256]{2,1,0:T(8,128)(2,1)S(1)}, u32[]{:S(2)}, u32[]{:S(2)}) collective-permute-start(bf16[2,128,256]{2,1,0:T(8,128)(2,1)S(1)} %get-tuple-element.34), channel_id=1, source_target_pairs={{0,1},{1,2},{2,3},{4,5},{5,6},{6,7},{8,9},{9,10},{10,11},{12,13},{... | collective-permute-start | bytes 393224 | tf_op jit(solution)/shard_map/ppermute | solution.py:326
  29.3 1.6 %collective-permute-start.5 = (bf16[2,128,256]{2,1,0:T(8,128)(2,1)S(1)}, bf16[2,128,256]{2,1,0:T(8,128)(2,1)S(1)}, u32[]{:S(2)}, u32[]{:S(2)}) collective-permute-start(bf16[2,128,256]{2,1,0:T(8,128)(2,1)S(1)} %get-tuple-element.33), channel_id=1, source_target_pairs={{0,1},{1,2},{2,3},{3,0},{4,5},{5,6},{6,7},{7,4},{8,9},{9,10},{10,1... | collective-permute-start | bytes 393224 | tf_op jit(solution)/shard_map/ppermute | solution.py:318
  30.9 0.0 copy-done.3
  30.9 1.4 %shard_map.62.rest_ref = f32[1,4,128,256]{3,2,1,0:T(8,128)S(1)} custom-call(bf16[2,4,128,256]{3,2,1,0:T(8,128)(2,1)S(1)} %get-tuple-element.20.x_ref, bf16[6,128,256]{2,1,0:T(8,128)(2,1)S(1)} %get-tuple-element.31.h0_ref, bf16[6,128,256]{2,1,0:T(8,128)(2,1)S(1)} %get-tuple-element.32.h1_ref, bf16[3,3,3,256,256]{4,3,2,1,0:T(8,128)(2,1)S(1)} %copy-done.1, ...), custom_call_target="tpu_custom_call" | custom-call | flops 1207959552 | tf_op jit(solution)/shard_map/pallas_call | solution.py:16
  32.3 0.6 %collective-permute-done.6.far_ref = bf16[2,128,256]{2,1,0:T(8,128)(2,1)S(1)} collective-permute-done((bf16[2,128,256]{2,1,0:T(8,128)(2,1)S(1)}, bf16[2,128,256]{2,1,0:T(8,128)(2,1)S(1)}, u32[]{:S(2)}, u32[]{:S(2)}) %collective-permute-start.6) | collective-permute-done | bytes 131104 | tf_op jit(solution)/shard_map/ppermute | solution.py:326
  32.9 4.5 %collective-permute-done.5.near_ref = bf16[2,128,256]{2,1,0:T(8,128)(2,1)S(1)} collective-permute-done((bf16[2,128,256]{2,1,0:T(8,128)(2,1)S(1)}, bf16[2,128,256]{2,1,0:T(8,128)(2,1)S(1)}, u32[]{:S(2)}, u32[]{:S(2)}) %collective-permute-start.5) | collective-permute-done | bytes 131104 | tf_op jit(solution)/shard_map/ppermute | solution.py:318
  37.4 0.8 %shard_map.63 = bf16[1,4,128,256]{3,2,1,0:T(8,128)(2,1)} custom-call(f32[1,4,128,256]{3,2,1,0:T(8,128)S(1)} %shard_map.62.rest_ref, bf16[2,128,256]{2,1,0:T(8,128)(2,1)S(1)} %collective-permute-done.5.near_ref, bf16[2,128,256]{2,1,0:T(8,128)(2,1)S(1)} %collective-permute-done.6.far_ref), custom_call_target="tpu_custom_call" | custom-call | tf_op jit(solution)/shard_map/pallas_call | solution.py:16
  (1 shorter events, 0.0 us)
Async XLA Ops:
  0.0 18.9 %copy-start.2 = (f32[256]{0:T(256)S(1)}, f32[256]{0:T(256)}, u32[]{:S(2)}) copy-start(f32[256]{0:T(256)} %param.7) | copy-start | bytes 3076
  0.0 18.9 %copy-start = (bf16[3,3,3,256,256]{4,3,2,1,0:T(8,128)(2,1)S(1)}, bf16[3,3,3,256,256]{4,3,2,1,0:T(8,128)(2,1)}, u32[]{:S(2)}) copy-start(bf16[3,3,3,256,256]{4,3,2,1,0:T(8,128)(2,1)} %w_ref.9) | copy-start | bytes 10616836
  0.0 17.2 %collective-permute-start = (bf16[2,4,128,256]{3,2,1,0:T(8,128)(2,1)}, bf16[2,4,128,256]{3,2,1,0:T(8,128)(2,1)S(1)}, u32[]{:S(2)}, u32[]{:S(2)}) collective-permute-start(bf16[2,4,128,256]{3,2,1,0:T(8,128)(2,1)} %x_ref.1), channel_id=1, source_target_pairs={{0,1},{1,2},{2,3},{3,0},{4,5},{5,6},{6,7},{7,4},{8,9},{9,10},{10,1... | collective-permute-start | bytes 1572872 | tf_op jit(solution)/shard_map/ppermute | solution.py:269
  4.2 14.7 %collective-permute-start.2 = (bf16[2,2,128,256]{3,2,1,0:T(8,128)(2,1)S(1)}, bf16[2,2,128,256]{3,2,1,0:T(8,128)(2,1)S(1)}, u32[]{:S(2)}, u32[]{:S(2)}) collective-permute-start(bf16[2,2,128,256]{3,2,1,0:T(8,128)(2,1)S(1)} %get-tuple-element.21), channel_id=1, source_target_pairs={{4,8},{8,4},{20,24},{24,20},{0,16},{12,28},{16,0},{28,12},{5,9},{9... | collective-permute-start | bytes 786440 | tf_op jit(solution)/shard_map/ppermute | solution.py:279
  5.7 14.2 %collective-permute-start.4 = (bf16[2,2,128,256]{3,2,1,0:T(8,128)(2,1)S(1)}, bf16[2,2,128,256]{3,2,1,0:T(8,128)(2,1)S(1)}, u32[]{:S(2)}, u32[]{:S(2)}) collective-permute-start(bf16[2,2,128,256]{3,2,1,0:T(8,128)(2,1)S(1)} %get-tuple-element.24), channel_id=1, source_target_pairs={{0,4},{8,12},{4,0},{12,8},{1,5},{9,13},{5,1},{13,9},{2,6},{10,14},... | collective-permute-start | bytes 786440 | tf_op jit(solution)/shard_map/ppermute | solution.py:278
  17.2 5.0 %collective-permute-start.3 = (bf16[2,2,128,256]{3,2,1,0:T(8,128)(2,1)S(1)}, bf16[2,2,128,256]{3,2,1,0:T(8,128)(2,1)S(1)}, u32[]{:S(2)}, u32[]{:S(2)}) collective-permute-start(bf16[2,2,128,256]{3,2,1,0:T(8,128)(2,1)S(1)} %shard_map.57), channel_id=1, source_target_pairs={{0,4},{8,12},{4,0},{12,8},{1,5},{9,13},{5,1},{13,9},{2,6},{10,14},... | collective-permute-start | bytes 786440 | tf_op jit(solution)/shard_map/ppermute | solution.py:299
  17.3 6.4 %collective-permute-start.1 = (bf16[2,2,128,256]{3,2,1,0:T(8,128)(2,1)S(1)}, bf16[2,2,128,256]{3,2,1,0:T(8,128)(2,1)S(1)}, u32[]{:S(2)}, u32[]{:S(2)}) collective-permute-start(bf16[2,2,128,256]{3,2,1,0:T(8,128)(2,1)S(1)} %get-tuple-element.21), channel_id=1, source_target_pairs={{4,9},{5,10},{6,11},{7,8},{8,5},{9,6},{10,7},{11,4},{20,25},{21,26... | collective-permute-start | bytes 786440 | tf_op jit(solution)/shard_map/ppermute | solution.py:280
  20.0 2.0 %copy-start.1 = (bf16[3,3,3,256,256]{4,3,2,1,0:T(8,128)(2,1)S(1)}, bf16[3,3,3,256,256]{4,3,2,1,0:T(8,128)(2,1)}, u32[]{:S(2)}) copy-start(bf16[3,3,3,256,256]{4,3,2,1,0:T(8,128)(2,1)} %v_ref.5) | copy-start | bytes 10616836
  23.7 7.2 %copy-start.3 = (f32[256]{0:T(256)S(1)}, f32[256]{0:T(256)}, u32[]{:S(2)}) copy-start(f32[256]{0:T(256)} %param.9) | copy-start | bytes 3076
  24.8 8.1 %collective-permute-start.6 = (bf16[2,128,256]{2,1,0:T(8,128)(2,1)S(1)}, bf16[2,128,256]{2,1,0:T(8,128)(2,1)S(1)}, u32[]{:S(2)}, u32[]{:S(2)}) collective-permute-start(bf16[2,128,256]{2,1,0:T(8,128)(2,1)S(1)} %get-tuple-element.34), channel_id=1, source_target_pairs={{0,1},{1,2},{2,3},{4,5},{5,6},{6,7},{8,9},{9,10},{10,11},{12,13},{... | collective-permute-start | bytes 393224 | tf_op jit(solution)/shard_map/ppermute | solution.py:326
  29.3 8.1 %collective-permute-start.5 = (bf16[2,128,256]{2,1,0:T(8,128)(2,1)S(1)}, bf16[2,128,256]{2,1,0:T(8,128)(2,1)S(1)}, u32[]{:S(2)}, u32[]{:S(2)}) collective-permute-start(bf16[2,128,256]{2,1,0:T(8,128)(2,1)S(1)} %get-tuple-element.33), channel_id=1, source_target_pairs={{0,1},{1,2},{2,3},{3,0},{4,5},{5,6},{6,7},{7,4},{8,9},{9,10},{10,1... | collective-permute-start | bytes 393224 | tf_op jit(solution)/shard_map/ppermute | solution.py:318

commit v5 on v2

--- a/solution.py
+++ b/solution.py
@@ -32,19 +32,38 @@
     return [flat(slab[p : p + rows]) for p in range(3)]
 
 
+def shifted_columns(part, q):
+    if q == 1:
+        return part
+    cols = part.shape[1]
+    col = lax.broadcasted_iota(jnp.int32, part.shape, 1)
+    edge, steps = (0, 1) if q == 0 else (cols - 1, cols - 1)
+    return jnp.where(col == edge, 0.0, pltpu.roll(part, steps, 1))
+
+
 def convolved(lhs, weights, rows, cols):
     stacked = jnp.concatenate(lhs, axis=1)
     total = None
     for q in range(3):
         taps = jnp.concatenate([w[q] for w in weights], axis=0)
         part = jnp.dot(stacked, taps, preferred_element_type=jnp.float32)
-        part = part.reshape(rows, cols, part.shape[-1])
-        if q != 1:
-            col = lax.broadcasted_iota(jnp.int32, part.shape, 1)
-            edge = 0 if q == 0 else cols - 1
-            part = jnp.where(col == edge, 0.0, pltpu.roll(part, 1 if q == 0 else cols - 1, 1))
+        part = shifted_columns(part.reshape(rows, cols, part.shape[-1]), q)
         total = part if total is None else total + part
     return total
+
+
+def convolved_pair(first, second, shared, extra, rows, cols):
+    lhs = jnp.concatenate([jnp.concatenate(taps, axis=1) for taps in (first, second)], axis=0)
+    count = rows * cols
+    total = None
+    for q in range(3):
+        taps = [jnp.concatenate([w[q] for w in weights], axis=0) for weights in (shared, extra)]
+        part = jnp.dot(lhs, taps[0], preferred_element_type=jnp.float32)
+        more = jnp.dot(lhs[count:], taps[1], preferred_element_type=jnp.float32)
+        part = jnp.concatenate([part[:count] + more, part[count:]], axis=0)
+        part = shifted_columns(part.reshape(2 * rows, cols, part.shape[-1]), q)
+        total = part if total is None else total + part
+    return total[:rows], total[rows:]
 
 
 def parity():
@@ -85,7 +104,7 @@
 
 
 def silu_rows(value, start, rows, tiles):
-    hidden = (value / (1.0 + jnp.exp(-value))).astype(jnp.bfloat16)
+    hidden = (0.5 * value * (1.0 + jnp.tanh(0.5 * value))).astype(jnp.bfloat16)
     row = lax.broadcasted_iota(jnp.int32, hidden.shape, 0) + start
     row = row + lax.axis_index("tile") * rows - 1
     inside = (row >= 0) & (row < tiles * rows)
@@ -109,9 +128,10 @@
 def own_sums(slabs, w_ref, b_ref, acc0_ref, acc1_ref):
     rows, cols = acc0_ref.shape[:2]
     taps = [row_taps(slab, rows) for slab in slabs]
-    acc0_ref[...] = b_ref[...] + convolved(taps[0], weight_rows(w_ref, 2), rows, cols)
-    weights = weight_rows(w_ref, 1) + weight_rows(w_ref, 2)
-    acc1_ref[...] = b_ref[...] + convolved(taps[0] + taps[1], weights, rows, cols)
+    shared, extra = weight_rows(w_ref, 2), weight_rows(w_ref, 1)
+    late, early = convolved_pair(taps[1], taps[0], shared, extra, rows, cols)
+    acc0_ref[...] = b_ref[...] + early
+    acc1_ref[...] = b_ref[...] + late
 
 
 def own_near_body(x_ref, inner_ref, w_ref, b_ref, acc0_ref, acc1_ref):
@@ -136,9 +156,10 @@
     @pl.when(started)
     def _():
         taps = [row_taps(slab(f), rows) for f in range(2)]
-        weights = weight_rows(w_ref, 0) + weight_rows(w_ref, 1)
-        sum0_ref[...] = bases[0]() + convolved(taps[0] + taps[1], weights, rows, cols)
-        sum1_ref[...] = bases[1]() + convolved(taps[1], weight_rows(w_ref, 0), rows, cols)
+        shared, extra = weight_rows(w_ref, 0), weight_rows(w_ref, 1)
+        early, late = convolved_pair(taps[0], taps[1], shared, extra, rows, cols)
+        sum0_ref[...] = bases[0]() + early
+        sum1_ref[...] = bases[1]() + late
 
     @pl.when(jnp.logical_not(started))
     def _():

time: 38.2 us -> 38 us (level)
  no operation moved by 1% of the time
where the time goes in v5:
time: 38 us; the launch traced here: 37.8 us
  starting transfers between devices  15.9 us (42%)
  waiting for transfers between devices  13.1 us (34%)
  Pallas kernels  8.61 us (23%)
    ppermute x1, waiting for transfers between devices, block(): earlier = lax.ppermute(x, 'tm', ring)  10.2 us
    pallas_call x9, Pallas kernels, call(): pl.pallas_call(body, out_shape=outs, in_specs=in_specs or [VMEM] * len(ar...  8.61 us
    ppermute x1, starting transfers between devices, block(): far_part = lax.ppermute(far_send, 'tm', forward)  6.36 us
    ppermute x1, waiting for transfers between devices, block(): near_part = lax.ppermute(near_send, 'tm', ring)  2.9 us
    ppermute x1, starting transfers between devices, block(): corner = lax.ppermute(outer_edge, ('tile', 'tm'), diagonal)  2.21 us
    ppermute x1, starting transfers between devices, block(): outer = lax.ppermute(outer_edge, ('clips', 'tile'), outer_full)  2.14 us
    ppermute x1, starting transfers between devices, block(): earlier = lax.ppermute(x, 'tm', ring)  2.11 us
    ppermute x1, starting transfers between devices, block(): near_part = lax.ppermute(near_send, 'tm', ring)  1.35 us
  transfers between devices with their start and end apart: 7, of which 2 were waited for; matrix products, arithmetic and copies ran while one was open for 0% of the time, Pallas kernels for 18%

profile of v5, /device:TPU:1, one launch (start us, length us, event | category | flops | bytes accessed | tf_op | source)
XLA Modules:
  0.0 37.8 jit_solution(11882273168078274833)
XLA Ops:
  0.0 0.0 copy-start.2
  0.0 0.0 copy-start
  0.0 2.1 %collective-permute-start = (bf16[2,4,128,256]{3,2,1,0:T(8,128)(2,1)}, bf16[2,4,128,256]{3,2,1,0:T(8,128)(2,1)S(1)}, u32[]{:S(2)}, u32[]{:S(2)}) collective-permute-start(bf16[2,4,128,256]{3,2,1,0:T(8,128)(2,1)} %x_ref.1), channel_id=1, source_target_pairs={{0,1},{1,2},{2,3},{3,0},{4,5},{5,6},{6,7},{7,4},{8,9},{9,10},{10,1... | collective-permute-start | bytes 1572872 | tf_op jit(solution)/shard_map/ppermute | solution.py:283
  2.1 1.1 %shard_map.55 = (bf16[2,4,128,256]{3,2,1,0:T(8,128)(2,1)S(1)}, bf16[2,2,128,256]{3,2,1,0:T(8,128)(2,1)S(1)}, bf16[2,2,128,256]{3,2,1,0:T(8,128)(2,1)S(1)}) custom-call(bf16[2,4,128,256]{3,2,1,0:T(8,128)(2,1)} %x_ref.1), custom_call_target="tpu_custom_call" | custom-call | flops 10000000000 | tf_op jit(solution)/shard_map/pallas_call | solution.py:16
  3.2 2.1 %collective-permute-start.2 = (bf16[2,2,128,256]{3,2,1,0:T(8,128)(2,1)S(1)}, bf16[2,2,128,256]{3,2,1,0:T(8,128)(2,1)S(1)}, u32[]{:S(2)}, u32[]{:S(2)}) collective-permute-start(bf16[2,2,128,256]{3,2,1,0:T(8,128)(2,1)S(1)} %get-tuple-element.21), channel_id=1, source_target_pairs={{4,8},{8,4},{20,24},{24,20},{0,16},{12,28},{16,0},{28,12},{5,9},{9... | collective-permute-start | bytes 786440 | tf_op jit(solution)/shard_map/ppermute | solution.py:293
  5.4 0.4 collective-permute-start.4
  5.8 10.2 %collective-permute-done.m_ref = bf16[2,4,128,256]{3,2,1,0:T(8,128)(2,1)S(1)} collective-permute-done((bf16[2,4,128,256]{3,2,1,0:T(8,128)(2,1)}, bf16[2,4,128,256]{3,2,1,0:T(8,128)(2,1)S(1)}, u32[]{:S(2)}, u32[]{:S(2)}) %collective-permute-start) | collective-permute-done | bytes 524320 | tf_op jit(solution)/shard_map/ppermute | solution.py:283
  16.0 1.3 %collective-permute-start.3 = (bf16[2,2,128,256]{3,2,1,0:T(8,128)(2,1)S(1)}, bf16[2,2,128,256]{3,2,1,0:T(8,128)(2,1)S(1)}, u32[]{:S(2)}, u32[]{:S(2)}) collective-permute-start(bf16[2,2,128,256]{3,2,1,0:T(8,128)(2,1)S(1)} %shard_map.57), channel_id=1, source_target_pairs={{0,4},{8,12},{4,0},{12,8},{1,5},{9,13},{5,1},{13,9},{2,6},{10,14},... | collective-permute-start | bytes 786440 | tf_op jit(solution)/shard_map/ppermute | solution.py:313
  17.3 2.2 %collective-permute-start.1 = (bf16[2,2,128,256]{3,2,1,0:T(8,128)(2,1)S(1)}, bf16[2,2,128,256]{3,2,1,0:T(8,128)(2,1)S(1)}, u32[]{:S(2)}, u32[]{:S(2)}) collective-permute-start(bf16[2,2,128,256]{3,2,1,0:T(8,128)(2,1)S(1)} %get-tuple-element.21), channel_id=1, source_target_pairs={{4,9},{5,10},{6,11},{8,5},{9,6},{10,7},{20,25},{21,26},{22,27},{24... | collective-permute-start | bytes 786440 | tf_op jit(solution)/shard_map/ppermute | solution.py:294
  19.5 0.0 collective-permute-done.2.outer_ref
  19.5 0.0 copy-done.2
  19.6 0.0 copy-done
  19.6 1.1 %shard_map.56 = (f32[2,128,256]{2,1,0:T(8,128)S(1)}, f32[2,128,256]{2,1,0:T(8,128)S(1)}) custom-call(bf16[2,4,128,256]{3,2,1,0:T(8,128)(2,1)S(1)} %get-tuple-element.20.x_ref, bf16[2,2,128,256]{3,2,1,0:T(8,128)(2,1)S(1)} %collective-permute-done.2.outer_ref, bf16[3,3,3,256,256]{4,3,2,1,0:T(8,128)(2,1)S(1)} %copy-done, f32[1,1,256]{2,1,0:T(1,128)S(1)} %bitcast.2), custom_call_target="tpu_custom_call" | custom-call | tf_op jit(solution)/shard_map/pallas_call | solution.py:16
  20.7 0.0 copy-start.1
  20.7 0.0 collective-permute-done.4.inner_ref
  20.7 2.0 %shard_map.58 = (f32[4,128,256]{2,1,0:T(8,128)S(1)}, f32[4,128,256]{2,1,0:T(8,128)S(1)}) custom-call(bf16[2,4,128,256]{3,2,1,0:T(8,128)(2,1)S(1)} %get-tuple-element.20.x_ref, bf16[2,2,128,256]{3,2,1,0:T(8,128)(2,1)S(1)} %collective-permute-done.4.inner_ref, bf16[3,3,3,256,256]{4,3,2,1,0:T(8,128)(2,1)S(1)} %copy-done, f32[1,1,256]{2,1,0:T(1,128)S(1)} %bitcast.3), custom_call_target="tpu_custom_call" | custom-call | flops 1811939328 | tf_op jit(solution)/shard_map/pallas_call | solution.py:16
  22.7 0.0 copy-done.1
  22.7 0.2 shard_map.59
  22.9 0.0 collective-permute-done.3.inner_ref
  22.9 1.0 %shard_map.60 = (bf16[2,128,256]{2,1,0:T(8,128)(2,1)S(1)}, bf16[4,128,256]{2,1,0:T(8,128)(2,1)S(1)}, bf16[4,128,256]{2,1,0:T(8,128)(2,1)S(1)}) custom-call(bf16[2,4,128,256]{3,2,1,0:T(8,128)(2,1)S(1)} %collective-permute-done.m_ref, bf16[2,2,128,256]{3,2,1,0:T(8,128)(2,1)S(1)} %collective-permute-done.3.inner_ref, bf16[3,3,3,256,256]{4,3,2,1,0:T(8,128)(2,1)S(1)} %copy-done, ...), custom_call_target="tpu_custom_call" | custom-call | tf_op jit(solution)/shard_map/pallas_call | solution.py:16
  23.9 0.0 collective-permute-done.1.outer_ref
  23.9 0.0 copy-start.3
  23.9 1.0 %shard_map.61 = (bf16[2,128,256]{2,1,0:T(8,128)(2,1)S(1)}, bf16[6,128,256]{2,1,0:T(8,128)(2,1)S(1)}, bf16[6,128,256]{2,1,0:T(8,128)(2,1)S(1)}) custom-call(bf16[2,4,128,256]{3,2,1,0:T(8,128)(2,1)S(1)} %collective-permute-done.m_ref, bf16[2,2,128,256]{3,2,1,0:T(8,128)(2,1)S(1)} %collective-permute-done.1.outer_ref, bf16[3,3,3,256,256]{4,3,2,1,0:T(8,128)(2,1)S(1)} %copy-done, ...), custom_call_target="tpu_custom_call" | custom-call | tf_op jit(solution)/shard_map/pallas_call | solution.py:16
  25.0 6.4 %collective-permute-start.6 = (bf16[2,128,256]{2,1,0:T(8,128)(2,1)S(1)}, bf16[2,128,256]{2,1,0:T(8,128)(2,1)S(1)}, u32[]{:S(2)}, u32[]{:S(2)}) collective-permute-start(bf16[2,128,256]{2,1,0:T(8,128)(2,1)S(1)} %get-tuple-element.34), channel_id=1, source_target_pairs={{0,1},{1,2},{2,3},{4,5},{5,6},{6,7},{8,9},{9,10},{10,11},{12,13},{... | collective-permute-start | bytes 393224 | tf_op jit(solution)/shard_map/ppermute | solution.py:340
  31.3 1.3 %collective-permute-start.5 = (bf16[2,128,256]{2,1,0:T(8,128)(2,1)S(1)}, bf16[2,128,256]{2,1,0:T(8,128)(2,1)S(1)}, u32[]{:S(2)}, u32[]{:S(2)}) collective-permute-start(bf16[2,128,256]{2,1,0:T(8,128)(2,1)S(1)} %get-tuple-element.33), channel_id=1, source_target_pairs={{0,1},{1,2},{2,3},{3,0},{4,5},{5,6},{6,7},{7,4},{8,9},{9,10},{10,1... | collective-permute-start | bytes 393224 | tf_op jit(solution)/shard_map/ppermute | solution.py:332
  32.7 0.0 copy-done.3
  32.7 1.4 %shard_map.62.rest_ref = f32[1,4,128,256]{3,2,1,0:T(8,128)S(1)} custom-call(bf16[2,4,128,256]{3,2,1,0:T(8,128)(2,1)S(1)} %get-tuple-element.20.x_ref, bf16[6,128,256]{2,1,0:T(8,128)(2,1)S(1)} %get-tuple-element.31.h0_ref, bf16[6,128,256]{2,1,0:T(8,128)(2,1)S(1)} %get-tuple-element.32.h1_ref, bf16[3,3,3,256,256]{4,3,2,1,0:T(8,128)(2,1)S(1)} %copy-done.1, ...), custom_call_target="tpu_custom_call" | custom-call | flops 1207959552 | tf_op jit(solution)/shard_map/pallas_call | solution.py:16
  34.1 0.0 collective-permute-done.6.far_ref
  34.1 2.9 %collective-permute-done.5.near_ref = bf16[2,128,256]{2,1,0:T(8,128)(2,1)S(1)} collective-permute-done((bf16[2,128,256]{2,1,0:T(8,128)(2,1)S(1)}, bf16[2,128,256]{2,1,0:T(8,128)(2,1)S(1)}, u32[]{:S(2)}, u32[]{:S(2)}) %collective-permute-start.5) | collective-permute-done | bytes 131104 | tf_op jit(solution)/shard_map/ppermute | solution.py:332
  37.0 0.8 %shard_map.63 = bf16[1,4,128,256]{3,2,1,0:T(8,128)(2,1)} custom-call(f32[1,4,128,256]{3,2,1,0:T(8,128)S(1)} %shard_map.62.rest_ref, bf16[2,128,256]{2,1,0:T(8,128)(2,1)S(1)} %collective-permute-done.5.near_ref, bf16[2,128,256]{2,1,0:T(8,128)(2,1)S(1)} %collective-permute-done.6.far_ref), custom_call_target="tpu_custom_call" | custom-call | tf_op jit(solution)/shard_map/pallas_call | solution.py:16
  (1 shorter events, 0.0 us)
Async XLA Ops:
  0.0 19.6 %copy-start.2 = (f32[256]{0:T(256)S(1)}, f32[256]{0:T(256)}, u32[]{:S(2)}) copy-start(f32[256]{0:T(256)} %param.7) | copy-start | bytes 3076
  0.0 19.6 %copy-start = (bf16[3,3,3,256,256]{4,3,2,1,0:T(8,128)(2,1)S(1)}, bf16[3,3,3,256,256]{4,3,2,1,0:T(8,128)(2,1)}, u32[]{:S(2)}) copy-start(bf16[3,3,3,256,256]{4,3,2,1,0:T(8,128)(2,1)} %w_ref.9) | copy-start | bytes 10616836
  0.0 16.0 %collective-permute-start = (bf16[2,4,128,256]{3,2,1,0:T(8,128)(2,1)}, bf16[2,4,128,256]{3,2,1,0:T(8,128)(2,1)S(1)}, u32[]{:S(2)}, u32[]{:S(2)}) collective-permute-start(bf16[2,4,128,256]{3,2,1,0:T(8,128)(2,1)} %x_ref.1), channel_id=1, source_target_pairs={{0,1},{1,2},{2,3},{3,0},{4,5},{5,6},{6,7},{7,4},{8,9},{9,10},{10,1... | collective-permute-start | bytes 1572872 | tf_op jit(solution)/shard_map/ppermute | solution.py:283
  3.2 16.3 %collective-permute-start.2 = (bf16[2,2,128,256]{3,2,1,0:T(8,128)(2,1)S(1)}, bf16[2,2,128,256]{3,2,1,0:T(8,128)(2,1)S(1)}, u32[]{:S(2)}, u32[]{:S(2)}) collective-permute-start(bf16[2,2,128,256]{3,2,1,0:T(8,128)(2,1)S(1)} %get-tuple-element.21), channel_id=1, source_target_pairs={{4,8},{8,4},{20,24},{24,20},{0,16},{12,28},{16,0},{28,12},{5,9},{9... | collective-permute-start | bytes 786440 | tf_op jit(solution)/shard_map/ppermute | solution.py:293
  5.4 15.3 %collective-permute-start.4 = (bf16[2,2,128,256]{3,2,1,0:T(8,128)(2,1)S(1)}, bf16[2,2,128,256]{3,2,1,0:T(8,128)(2,1)S(1)}, u32[]{:S(2)}, u32[]{:S(2)}) collective-permute-start(bf16[2,2,128,256]{3,2,1,0:T(8,128)(2,1)S(1)} %get-tuple-element.24), channel_id=1, source_target_pairs={{0,4},{8,12},{4,0},{12,8},{1,5},{9,13},{5,1},{13,9},{2,6},{10,14},... | collective-permute-start | bytes 786440 | tf_op jit(solution)/shard_map/ppermute | solution.py:292
  16.0 6.9 %collective-permute-start.3 = (bf16[2,2,128,256]{3,2,1,0:T(8,128)(2,1)S(1)}, bf16[2,2,128,256]{3,2,1,0:T(8,128)(2,1)S(1)}, u32[]{:S(2)}, u32[]{:S(2)}) collective-permute-start(bf16[2,2,128,256]{3,2,1,0:T(8,128)(2,1)S(1)} %shard_map.57), channel_id=1, source_target_pairs={{0,4},{8,12},{4,0},{12,8},{1,5},{9,13},{5,1},{13,9},{2,6},{10,14},... | collective-permute-start | bytes 786440 | tf_op jit(solution)/shard_map/ppermute | solution.py:313
  17.3 6.6 %collective-permute-start.1 = (bf16[2,2,128,256]{3,2,1,0:T(8,128)(2,1)S(1)}, bf16[2,2,128,256]{3,2,1,0:T(8,128)(2,1)S(1)}, u32[]{:S(2)}, u32[]{:S(2)}) collective-permute-start(bf16[2,2,128,256]{3,2,1,0:T(8,128)(2,1)S(1)} %get-tuple-element.21), channel_id=1, source_target_pairs={{4,9},{5,10},{6,11},{8,5},{9,6},{10,7},{20,25},{21,26},{22,27},{24... | collective-permute-start | bytes 786440 | tf_op jit(solution)/shard_map/ppermute | solution.py:294
  20.7 2.0 %copy-start.1 = (bf16[3,3,3,256,256]{4,3,2,1,0:T(8,128)(2,1)S(1)}, bf16[3,3,3,256,256]{4,3,2,1,0:T(8,128)(2,1)}, u32[]{:S(2)}) copy-start(bf16[3,3,3,256,256]{4,3,2,1,0:T(8,128)(2,1)} %v_ref.5) | copy-start | bytes 10616836
  23.9 8.8 %copy-start.3 = (f32[256]{0:T(256)S(1)}, f32[256]{0:T(256)}, u32[]{:S(2)}) copy-start(f32[256]{0:T(256)} %param.9) | copy-start | bytes 3076
  25.0 9.1 %collective-permute-start.6 = (bf16[2,128,256]{2,1,0:T(8,128)(2,1)S(1)}, bf16[2,128,256]{2,1,0:T(8,128)(2,1)S(1)}, u32[]{:S(2)}, u32[]{:S(2)}) collective-permute-start(bf16[2,128,256]{2,1,0:T(8,128)(2,1)S(1)} %get-tuple-element.34), channel_id=1, source_target_pairs={{0,1},{1,2},{2,3},{4,5},{5,6},{6,7},{8,9},{9,10},{10,11},{12,13},{... | collective-permute-start | bytes 393224 | tf_op jit(solution)/shard_map/ppermute | solution.py:340
  31.3 5.7 %collective-permute-start.5 = (bf16[2,128,256]{2,1,0:T(8,128)(2,1)S(1)}, bf16[2,128,256]{2,1,0:T(8,128)(2,1)S(1)}, u32[]{:S(2)}, u32[]{:S(2)}) collective-permute-start(bf16[2,128,256]{2,1,0:T(8,128)(2,1)S(1)} %get-tuple-element.33), channel_id=1, source_target_pairs={{0,1},{1,2},{2,3},{3,0},{4,5},{5,6},{6,7},{7,4},{8,9},{9,10},{10,1... | collective-permute-start | bytes 393224 | tf_op jit(solution)/shard_map/ppermute | solution.py:332

commit v6 on v5

--- a/solution.py
+++ b/solution.py
@@ -149,40 +149,25 @@
     own_sums(slabs, w_ref, b_ref, acc0_ref, acc1_ref)
 
 
-def hidden(slab, bases, places_of, w_ref, tiles, whole, h0_ref, h1_ref, sum0_ref, sum1_ref):
-    rows, cols = sum0_ref.shape[:2]
-    started = lax.axis_index("tm") > 0
-
-    @pl.when(started)
-    def _():
-        taps = [row_taps(slab(f), rows) for f in range(2)]
-        shared, extra = weight_rows(w_ref, 0), weight_rows(w_ref, 1)
-        early, late = convolved_pair(taps[0], taps[1], shared, extra, rows, cols)
-        sum0_ref[...] = bases[0]() + early
-        sum1_ref[...] = bases[1]() + late
-
-    @pl.when(jnp.logical_not(started))
-    def _():
-        sum0_ref[...] = bases[0]()
-        sum1_ref[...] = bases[1]()
-
-    h0_ref[...] = silu_rows(sum0_ref[...], places_of.start, whole, tiles)
-    h1_ref[...] = silu_rows(sum1_ref[...], places_of.start, whole, tiles)
+def hidden(slab, bases, place, w_ref, tiles, whole, h0_ref, h1_ref):
+    rows, cols = h0_ref.shape[:2]
+    taps = [row_taps(slab(f), rows) for f in range(2)]
+    shared, extra = weight_rows(w_ref, 0), weight_rows(w_ref, 1)
+    early, late = convolved_pair(taps[0], taps[1], shared, extra, rows, cols)
+    h0_ref[...] = silu_rows(bases[0]() + early, place.start, whole, tiles)
+    h1_ref[...] = silu_rows(bases[1]() + late, place.start, whole, tiles)
+
+
+def started():
+    return lax.axis_index("tm") > 0
 
 
 def from_near(acc_ref, start, rows):
     return lambda: acc_ref[pl.ds(start, rows)]
 
 
-def middle_body(tiles, m_ref, w_ref, _, acc0_ref, acc1_ref, h0_ref, h1_ref, sum0_ref, sum1_ref):
-    rows = m_ref.shape[1]
-    start = 2 * parity()
-    bases = [from_near(acc_ref, start, rows - 2) for acc_ref in (acc0_ref, acc1_ref)]
-    place = places(rows)[0]
-    hidden(lambda f: m_ref[f], bases, place, w_ref, tiles, rows, h0_ref, h1_ref, sum0_ref, sum1_ref)
-
-
-def partial_rows(times, h0, h1, v_ref, rows, cols, send_ref):
+def partial_rows(times, h0, h1, v_ref, send_ref):
+    rows, cols = send_ref.shape[:2]
     has_next = lax.axis_index("tm") < times - 1
 
     @pl.when(has_next)
@@ -197,55 +182,96 @@
         send_ref[...] = jnp.zeros_like(send_ref)
 
 
+def far_side(rows):
+    return pl.ds(parity() * (rows - 2), 4)
+
+
+def near_place(rows):
+    return pl.ds(2 * (1 - parity()), rows)
+
+
+def origin_body(
+    tiles, times, v_ref, acc0_ref, acc1_ref, far0_ref, far1_ref, near_ref, far_ref, h0_ref, h1_ref
+):
+    rows = acc0_ref.shape[0]
+    near, far = near_place(rows), places(rows)[2]
+
+    @pl.when(jnp.logical_not(started()))
+    def _():
+        for h_ref, acc_ref, other_ref in ((h0_ref, acc0_ref, far0_ref), (h1_ref, acc1_ref, far1_ref)):
+            h_ref[near] = silu_rows(acc_ref[...], near.start, rows, tiles)
+            h_ref[far] = silu_rows(other_ref[...], far.start, rows, tiles)
+        partial_rows(times, h0_ref[near], h1_ref[near], v_ref, near_ref)
+        side = far_side(rows)
+        partial_rows(times, h0_ref[side], h1_ref[side], v_ref, far_ref)
+
+
+def middle_body(tiles, m_ref, w_ref, acc0_ref, acc1_ref, h0_ref, h1_ref):
+    rows = m_ref.shape[1]
+
+    @pl.when(started())
+    def _():
+        start = 2 * parity()
+        bases = [from_near(acc_ref, start, rows - 2) for acc_ref in (acc0_ref, acc1_ref)]
+        hidden(lambda f: m_ref[f], bases, places(rows)[0], w_ref, tiles, rows, h0_ref, h1_ref)
+
+
 def near_body(
-    tiles, times, m_ref, inner_ref, w_ref, v_ref, acc0_ref, acc1_ref, mid0_ref, mid1_ref,
-    send_ref, h0_ref, h1_ref, sum0_ref, sum1_ref,
+    tiles, times, m_ref, inner_ref, w_ref, v_ref, acc0_ref, acc1_ref, mid0_ref, mid1_ref, first_ref,
+    send_ref, h0_ref, h1_ref,
 ):
-    rows, cols = m_ref.shape[1:3]
-    odd = parity()
-    start = (1 - odd) * (rows - 2)
-    bases = [from_near(acc_ref, start, 2) for acc_ref in (acc0_ref, acc1_ref)]
-    place = places(rows)[1]
-
-    def slab(f):
-        return inner_slab(inner_ref[f], m_ref.at[f])
-
-    middle, near = pl.ds(2 * odd, rows - 2), pl.ds(start, 2)
-    h0_ref[middle], h1_ref[middle] = mid0_ref[...], mid1_ref[...]
-    hidden(
-        slab, bases, place, w_ref, tiles, rows, h0_ref.at[near], h1_ref.at[near], sum0_ref,
-        sum1_ref,
-    )
-    partial_rows(times, h0_ref[...], h1_ref[...], v_ref, rows - 2, cols, send_ref)
+    rows = m_ref.shape[1]
+
+    @pl.when(started())
+    def _():
+        odd = parity()
+        start = (1 - odd) * (rows - 2)
+        bases = [from_near(acc_ref, start, 2) for acc_ref in (acc0_ref, acc1_ref)]
+        middle, near = pl.ds(2 * odd, rows - 2), pl.ds(start, 2)
+
+        def slab(f):
+            return inner_slab(inner_ref[f], m_ref.at[f])
+
+        h0_ref[middle], h1_ref[middle] = mid0_ref[...], mid1_ref[...]
+        place = places(rows)[1]
+        hidden(slab, bases, place, w_ref, tiles, rows, h0_ref.at[near], h1_ref.at[near])
+        partial_rows(times, h0_ref[...], h1_ref[...], v_ref, send_ref)
+
+    @pl.when(jnp.logical_not(started()))
+    def _():
+        send_ref[...] = first_ref[...]
 
 
 def far_body(
     tiles, times, m_ref, outer_ref, w_ref, v_ref, acc0_ref, acc1_ref, near0_ref, near1_ref,
-    send_ref, h0_ref, h1_ref, sum0_ref, sum1_ref,
+    first_ref, first0_ref, first1_ref, send_ref, h0_ref, h1_ref,
 ):
-    rows, cols = m_ref.shape[1:3]
-    odd = parity()
-    far = places(rows)[2]
-    near = pl.ds(2 * (1 - odd), rows)
-
-    def slab(f):
-        return outer_slab(outer_ref[f], m_ref.at[f], tiles)
-
-    bases = [lambda: acc0_ref[...], lambda: acc1_ref[...]]
-    h0_ref[near], h1_ref[near] = near0_ref[...], near1_ref[...]
-    hidden(
-        slab, bases, far, w_ref, tiles, rows, h0_ref.at[far], h1_ref.at[far], sum0_ref, sum1_ref
-    )
-    side = pl.ds(odd * (rows - 2), 4)
-    partial_rows(times, h0_ref[side], h1_ref[side], v_ref, 2, cols, send_ref)
+    rows = m_ref.shape[1]
+
+    @pl.when(started())
+    def _():
+        near, far, side = near_place(rows), places(rows)[2], far_side(rows)
+
+        def slab(f):
+            return outer_slab(outer_ref[f], m_ref.at[f], tiles)
+
+        bases = [lambda: acc0_ref[...], lambda: acc1_ref[...]]
+        h0_ref[near], h1_ref[near] = near0_ref[...], near1_ref[...]
+        hidden(slab, bases, far, w_ref, tiles, rows, h0_ref.at[far], h1_ref.at[far])
+        partial_rows(times, h0_ref[side], h1_ref[side], v_ref, send_ref)
+
+    @pl.when(jnp.logical_not(started()))
+    def _():
+        send_ref[...] = first_ref[...]
+        h0_ref[...], h1_ref[...] = first0_ref[...], first1_ref[...]
 
 
 def rest_body(x_ref, h0_ref, h1_ref, v_ref, b_ref, out_ref):
     rows, cols = x_ref.shape[1:3]
     h0, h1 = h0_ref[...], h1_ref[...]
-    both = (h0.astype(jnp.float32) + h1.astype(jnp.float32)).astype(jnp.bfloat16)
-    taps = row_taps(h0, rows) + row_taps(both, rows)
-    part = convolved(taps, weight_rows(v_ref, 1) + weight_rows(v_ref, 2), rows, cols)
+    taps = row_taps(h0, rows) + row_taps(h0, rows) + row_taps(h1, rows)
+    weights = weight_rows(v_ref, 1) + 2 * weight_rows(v_ref, 2)
+    part = convolved(taps, weights, rows, cols)
     total = x_ref[0].astype(jnp.float32) + x_ref[1].astype(jnp.float32) + part
     out_ref[0] = total * 0.5 + b_ref[...]
 
@@ -309,40 +335,45 @@
         (x, outer, weight_first, bias_first),
         0,
     )
+    first_near, first_far, first0, first1 = call(
+        functools.partial(origin_body, tiles, times),
+        [frames(rows - 2), frames(2), frames(wide), frames(wide)],
+        (weight_second, sums0, sums1, far0, far1),
+        0,
+    )
     (inner_edge,) = call(turn_body, [frames(2, 2)], (earlier,), 0)
     inner_corner = lax.ppermute(inner_edge, "tile", inner_pairs)
-
-    def sums(count):
-        return [pltpu.VMEM((count, cols, channels), f32)] * 2
-
     mid0, mid1 = call(
         functools.partial(middle_body, tiles),
         [frames(rows - 2), frames(rows - 2)],
-        (earlier, weight_first, weight_second, sums0, sums1),
-        0,
-        scratch=sums(rows - 2),
+        (earlier, weight_first, sums0, sums1),
+        0,
     )
     near_send, near0, near1 = call(
         functools.partial(near_body, tiles, times),
         [frames(rows - 2), frames(rows), frames(rows)],
-        (earlier, inner_corner, weight_first, weight_second, sums0, sums1, mid0, mid1),
-        0,
-        scratch=sums(2),
+        (
+            earlier, inner_corner, weight_first, weight_second, sums0, sums1, mid0, mid1,
+            first_near,
+        ),
+        0,
     )
     near_part = lax.ppermute(near_send, "tm", ring)
     far_send, h0, h1 = call(
         functools.partial(far_body, tiles, times),
         [frames(2), frames(wide), frames(wide)],
-        (earlier, corner, weight_first, weight_second, far0, far1, near0, near1),
-        0,
-        scratch=sums(2),
+        (
+            earlier, corner, weight_first, weight_second, far0, far1, near0, near1, first_far,
+            first0, first1,
+        ),
+        0,
     )
     far_part = lax.ppermute(far_send, "tm", forward)
     (rest,) = call(
         rest_body,
         [frames(1, rows, dtype=f32)],
         (x, h0, h1, weight_second, bias_second),
-        2 * unit * rows,
+        3 * unit * rows,
     )
     (pooled,) = call(join_body, [frames(1, rows)], (rest, near_part, far_part), 0)
     return pooled

time: 38 us -> 37.9 us (level)
  waiting for transfers between devices: 13.1 us -> 12.5 us
  Pallas kernels: 8.61 us -> 9.2 us
    ppermute x1, waiting for transfers between devices: 2.9 us -> 2.29 us  [block(): near_part = lax.ppermute(near_send, 'tm', ring)]
    pallas_call x9 -> x10, Pallas kernels: 8.61 us -> 9.2 us  [call(): pl.pallas_call(body, out_shape=outs, in_specs=in_specs or [VMEM] * len(ar...]
  transfers between devices with their start and end apart: 7 -> 7, of which waited for: 2 -> 2; matrix products, arithmetic and copies ran while one was open for 0% -> 0% of each run, Pallas kernels for 18% -> 22%
where the time goes in v6:
time: 37.9 us; the launch traced here: 37.7 us
  starting transfers between devices  15.7 us (41%)
  waiting for transfers between devices  12.5 us (33%)
  Pallas kernels  9.2 us (24%)
    ppermute x1, waiting for transfers between devices, block(): earlier = lax.ppermute(x, 'tm', ring)  10.2 us
    pallas_call x10, Pallas kernels, call(): pl.pallas_call(body, out_shape=outs, in_specs=in_specs or [VMEM] * len(ar...  9.2 us
    ppermute x1, starting transfers between devices, block(): far_part = lax.ppermute(far_send, 'tm', forward)  6.24 us
    ppermute x1, waiting for transfers between devices, block(): near_part = lax.ppermute(near_send, 'tm', ring)  2.29 us
    ppermute x1, starting transfers between devices, block(): corner = lax.ppermute(outer_edge, ('tile', 'tm'), diagonal)  2.21 us
    ppermute x1, starting transfers between devices, block(): outer = lax.ppermute(outer_edge, ('clips', 'tile'), outer_full)  2.14 us
    ppermute x1, starting transfers between devices, block(): earlier = lax.ppermute(x, 'tm', ring)  2.11 us
    ppermute x1, starting transfers between devices, block(): near_part = lax.ppermute(near_send, 'tm', ring)  1.35 us
  transfers between devices with their start and end apart: 7, of which 2 were waited for; matrix products, arithmetic and copies ran while one was open for 0% of the time, Pallas kernels for 22%

profile of v6, /device:TPU:1, one launch (start us, length us, event | category | flops | bytes accessed | tf_op | source)
XLA Modules:
  0.0 37.7 jit_solution(17740502792292768398)
XLA Ops:
  0.0 0.0 copy-start
  0.0 0.0 copy-start.2
  0.0 2.1 %collective-permute-start = (bf16[2,4,128,256]{3,2,1,0:T(8,128)(2,1)}, bf16[2,4,128,256]{3,2,1,0:T(8,128)(2,1)S(1)}, u32[]{:S(2)}, u32[]{:S(2)}) collective-permute-start(bf16[2,4,128,256]{3,2,1,0:T(8,128)(2,1)} %x_ref.1), channel_id=1, source_target_pairs={{0,1},{1,2},{2,3},{3,0},{4,5},{5,6},{6,7},{7,4},{8,9},{9,10},{10,1... | collective-permute-start | bytes 1572872 | tf_op jit(solution)/shard_map/ppermute | solution.py:309
  2.1 1.1 %shard_map.55 = (bf16[2,4,128,256]{3,2,1,0:T(8,128)(2,1)S(1)}, bf16[2,2,128,256]{3,2,1,0:T(8,128)(2,1)S(1)}, bf16[2,2,128,256]{3,2,1,0:T(8,128)(2,1)S(1)}) custom-call(bf16[2,4,128,256]{3,2,1,0:T(8,128)(2,1)} %x_ref.1), custom_call_target="tpu_custom_call" | custom-call | flops 10000000000 | tf_op jit(solution)/shard_map/pallas_call | solution.py:16
  3.2 2.1 %collective-permute-start.2 = (bf16[2,2,128,256]{3,2,1,0:T(8,128)(2,1)S(1)}, bf16[2,2,128,256]{3,2,1,0:T(8,128)(2,1)S(1)}, u32[]{:S(2)}, u32[]{:S(2)}) collective-permute-start(bf16[2,2,128,256]{3,2,1,0:T(8,128)(2,1)S(1)} %get-tuple-element.25), channel_id=1, source_target_pairs={{4,8},{8,4},{20,24},{24,20},{0,16},{12,28},{16,0},{28,12},{5,9},{9... | collective-permute-start | bytes 786440 | tf_op jit(solution)/shard_map/ppermute | solution.py:319
  5.4 0.4 collective-permute-start.4
  5.8 10.2 %collective-permute-done.m_ref = bf16[2,4,128,256]{3,2,1,0:T(8,128)(2,1)S(1)} collective-permute-done((bf16[2,4,128,256]{3,2,1,0:T(8,128)(2,1)}, bf16[2,4,128,256]{3,2,1,0:T(8,128)(2,1)S(1)}, u32[]{:S(2)}, u32[]{:S(2)}) %collective-permute-start) | collective-permute-done | bytes 524320 | tf_op jit(solution)/shard_map/ppermute | solution.py:309
  16.0 1.3 %collective-permute-start.3 = (bf16[2,2,128,256]{3,2,1,0:T(8,128)(2,1)S(1)}, bf16[2,2,128,256]{3,2,1,0:T(8,128)(2,1)S(1)}, u32[]{:S(2)}, u32[]{:S(2)}) collective-permute-start(bf16[2,2,128,256]{3,2,1,0:T(8,128)(2,1)S(1)} %shard_map.57), channel_id=1, source_target_pairs={{0,4},{8,12},{4,0},{12,8},{1,5},{9,13},{5,1},{13,9},{2,6},{10,14},... | collective-permute-start | bytes 786440 | tf_op jit(solution)/shard_map/ppermute | solution.py:345
  17.3 2.2 %collective-permute-start.1 = (bf16[2,2,128,256]{3,2,1,0:T(8,128)(2,1)S(1)}, bf16[2,2,128,256]{3,2,1,0:T(8,128)(2,1)S(1)}, u32[]{:S(2)}, u32[]{:S(2)}) collective-permute-start(bf16[2,2,128,256]{3,2,1,0:T(8,128)(2,1)S(1)} %get-tuple-element.25), channel_id=1, source_target_pairs={{4,9},{5,10},{6,11},{8,5},{9,6},{10,7},{20,25},{21,26},{22,27},{24... | collective-permute-start | bytes 786440 | tf_op jit(solution)/shard_map/ppermute | solution.py:320
  19.5 0.0 collective-permute-done.2.outer_ref
  19.5 0.0 copy-done
  19.6 0.0 copy-done.2
  19.6 1.1 %shard_map.56 = (f32[2,128,256]{2,1,0:T(8,128)S(1)}, f32[2,128,256]{2,1,0:T(8,128)S(1)}) custom-call(bf16[2,4,128,256]{3,2,1,0:T(8,128)(2,1)S(1)} %get-tuple-element.24.x_ref, bf16[2,2,128,256]{3,2,1,0:T(8,128)(2,1)S(1)} %collective-permute-done.2.outer_ref, bf16[3,3,3,256,256]{4,3,2,1,0:T(8,128)(2,1)S(1)} %copy-done, f32[1,1,256]{2,1,0:T(1,128)S(1)} %bitcast.2), custom_call_target="tpu_custom_call" | custom-call | tf_op jit(solution)/shard_map/pallas_call | solution.py:16
  20.7 0.0 copy-start.1
  20.7 0.0 collective-permute-done.4.inner_ref
  20.7 2.0 %shard_map.58 = (f32[4,128,256]{2,1,0:T(8,128)S(1)}, f32[4,128,256]{2,1,0:T(8,128)S(1)}) custom-call(bf16[2,4,128,256]{3,2,1,0:T(8,128)(2,1)S(1)} %get-tuple-element.24.x_ref, bf16[2,2,128,256]{3,2,1,0:T(8,128)(2,1)S(1)} %collective-permute-done.4.inner_ref, bf16[3,3,3,256,256]{4,3,2,1,0:T(8,128)(2,1)S(1)} %copy-done, f32[1,1,256]{2,1,0:T(1,128)S(1)} %bitcast.3), custom_call_target="tpu_custom_call" | custom-call | flops 1811939328 | tf_op jit(solution)/shard_map/pallas_call | solution.py:16
  22.7 0.0 copy-done.1
  22.7 2.1 %shard_map.60 = (bf16[2,128,256]{2,1,0:T(8,128)(2,1)S(1)}, bf16[2,128,256]{2,1,0:T(8,128)(2,1)S(1)}, bf16[6,128,256]{2,1,0:T(8,128)(2,1)S(1)}, bf16[6,128,256]{2,1,0:T(8,128)(2,1)S(1)}) custom-call(bf16[3,3,3,256,256]{4,3,2,1,0:T(8,128)(2,1)S(1)} %copy-done.1, f32[4,128,256]{2,1,0:T(8,128)S(1)} %get-tuple-element.29.acc0_ref, ...), custom_call_target="tpu_custom_call" | custom-call | tf_op jit(solution)/shard_map/pallas_call | solution.py:16
  24.8 0.0 collective-permute-done.3.inner_ref
  24.8 0.0 collective-permute-done.1.outer_ref
  24.9 0.0 copy-start.3
  24.9 0.1 shard_map.62
  24.9 6.2 %collective-permute-start.6 = (bf16[2,128,256]{2,1,0:T(8,128)(2,1)S(1)}, bf16[2,128,256]{2,1,0:T(8,128)(2,1)S(1)}, u32[]{:S(2)}, u32[]{:S(2)}) collective-permute-start(bf16[2,128,256]{2,1,0:T(8,128)(2,1)S(1)} %get-tuple-element.42), channel_id=1, source_target_pairs={{0,1},{1,2},{2,3},{4,5},{5,6},{6,7},{8,9},{9,10},{10,11},{12,13},{... | collective-permute-start | bytes 393224 | tf_op jit(solution)/shard_map/ppermute | solution.py:371
  31.2 1.3 %collective-permute-start.5 = (bf16[2,128,256]{2,1,0:T(8,128)(2,1)S(1)}, bf16[2,128,256]{2,1,0:T(8,128)(2,1)S(1)}, u32[]{:S(2)}, u32[]{:S(2)}) collective-permute-start(bf16[2,128,256]{2,1,0:T(8,128)(2,1)S(1)} %get-tuple-element.41), channel_id=1, source_target_pairs={{0,1},{1,2},{2,3},{3,0},{4,5},{5,6},{6,7},{7,4},{8,9},{9,10},{10,1... | collective-permute-start | bytes 393224 | tf_op jit(solution)/shard_map/ppermute | solution.py:361
  32.5 0.0 copy-done.3
  32.5 2.0 %shard_map.63.rest_ref = f32[1,4,128,256]{3,2,1,0:T(8,128)S(1)} custom-call(bf16[2,4,128,256]{3,2,1,0:T(8,128)(2,1)S(1)} %get-tuple-element.24.x_ref, bf16[6,128,256]{2,1,0:T(8,128)(2,1)S(1)} %get-tuple-element.39.h0_ref, bf16[6,128,256]{2,1,0:T(8,128)(2,1)S(1)} %get-tuple-element.40.h1_ref, bf16[3,3,3,256,256]{4,3,2,1,0:T(8,128)(2,1)S(1)} %copy-done.1, ...), custom_call_target="tpu_custom_call" | custom-call | flops 1811939328 | tf_op jit(solution)/shard_map/pallas_call | solution.py:16
  34.6 0.0 collective-permute-done.6.far_ref
  34.6 2.3 %collective-permute-done.5.near_ref = bf16[2,128,256]{2,1,0:T(8,128)(2,1)S(1)} collective-permute-done((bf16[2,128,256]{2,1,0:T(8,128)(2,1)S(1)}, bf16[2,128,256]{2,1,0:T(8,128)(2,1)S(1)}, u32[]{:S(2)}, u32[]{:S(2)}) %collective-permute-start.5) | collective-permute-done | bytes 131104 | tf_op jit(solution)/shard_map/ppermute | solution.py:361
  36.9 0.8 %shard_map.64 = bf16[1,4,128,256]{3,2,1,0:T(8,128)(2,1)} custom-call(f32[1,4,128,256]{3,2,1,0:T(8,128)S(1)} %shard_map.63.rest_ref, bf16[2,128,256]{2,1,0:T(8,128)(2,1)S(1)} %collective-permute-done.5.near_ref, bf16[2,128,256]{2,1,0:T(8,128)(2,1)S(1)} %collective-permute-done.6.far_ref), custom_call_target="tpu_custom_call" | custom-call | tf_op jit(solution)/shard_map/pallas_call | solution.py:16
  (3 shorter events, 0.1 us)
Async XLA Ops:
  0.0 19.6 %copy-start = (bf16[3,3,3,256,256]{4,3,2,1,0:T(8,128)(2,1)S(1)}, bf16[3,3,3,256,256]{4,3,2,1,0:T(8,128)(2,1)}, u32[]{:S(2)}) copy-start(bf16[3,3,3,256,256]{4,3,2,1,0:T(8,128)(2,1)} %w_ref.9) | copy-start | bytes 10616836
  0.0 19.6 %copy-start.2 = (f32[256]{0:T(256)S(1)}, f32[256]{0:T(256)}, u32[]{:S(2)}) copy-start(f32[256]{0:T(256)} %param.7) | copy-start | bytes 3076
  0.0 16.0 %collective-permute-start = (bf16[2,4,128,256]{3,2,1,0:T(8,128)(2,1)}, bf16[2,4,128,256]{3,2,1,0:T(8,128)(2,1)S(1)}, u32[]{:S(2)}, u32[]{:S(2)}) collective-permute-start(bf16[2,4,128,256]{3,2,1,0:T(8,128)(2,1)} %x_ref.1), channel_id=1, source_target_pairs={{0,1},{1,2},{2,3},{3,0},{4,5},{5,6},{6,7},{7,4},{8,9},{9,10},{10,1... | collective-permute-start | bytes 1572872 | tf_op jit(solution)/shard_map/ppermute | solution.py:309
  3.2 16.3 %collective-permute-start.2 = (bf16[2,2,128,256]{3,2,1,0:T(8,128)(2,1)S(1)}, bf16[2,2,128,256]{3,2,1,0:T(8,128)(2,1)S(1)}, u32[]{:S(2)}, u32[]{:S(2)}) collective-permute-start(bf16[2,2,128,256]{3,2,1,0:T(8,128)(2,1)S(1)} %get-tuple-element.25), channel_id=1, source_target_pairs={{4,8},{8,4},{20,24},{24,20},{0,16},{12,28},{16,0},{28,12},{5,9},{9... | collective-permute-start | bytes 786440 | tf_op jit(solution)/shard_map/ppermute | solution.py:319
  5.4 15.3 %collective-permute-start.4 = (bf16[2,2,128,256]{3,2,1,0:T(8,128)(2,1)S(1)}, bf16[2,2,128,256]{3,2,1,0:T(8,128)(2,1)S(1)}, u32[]{:S(2)}, u32[]{:S(2)}) collective-permute-start(bf16[2,2,128,256]{3,2,1,0:T(8,128)(2,1)S(1)} %get-tuple-element.28), channel_id=1, source_target_pairs={{0,4},{8,12},{4,0},{12,8},{1,5},{9,13},{5,1},{13,9},{2,6},{10,14},... | collective-permute-start | bytes 786440 | tf_op jit(solution)/shard_map/ppermute | solution.py:318
  16.0 8.8 %collective-permute-start.3 = (bf16[2,2,128,256]{3,2,1,0:T(8,128)(2,1)S(1)}, bf16[2,2,128,256]{3,2,1,0:T(8,128)(2,1)S(1)}, u32[]{:S(2)}, u32[]{:S(2)}) collective-permute-start(bf16[2,2,128,256]{3,2,1,0:T(8,128)(2,1)S(1)} %shard_map.57), channel_id=1, source_target_pairs={{0,4},{8,12},{4,0},{12,8},{1,5},{9,13},{5,1},{13,9},{2,6},{10,14},... | collective-permute-start | bytes 786440 | tf_op jit(solution)/shard_map/ppermute | solution.py:345
  17.3 7.5 %collective-permute-start.1 = (bf16[2,2,128,256]{3,2,1,0:T(8,128)(2,1)S(1)}, bf16[2,2,128,256]{3,2,1,0:T(8,128)(2,1)S(1)}, u32[]{:S(2)}, u32[]{:S(2)}) collective-permute-start(bf16[2,2,128,256]{3,2,1,0:T(8,128)(2,1)S(1)} %get-tuple-element.25), channel_id=1, source_target_pairs={{4,9},{5,10},{6,11},{8,5},{9,6},{10,7},{20,25},{21,26},{22,27},{24... | collective-permute-start | bytes 786440 | tf_op jit(solution)/shard_map/ppermute | solution.py:320
  20.7 2.0 %copy-start.1 = (bf16[3,3,3,256,256]{4,3,2,1,0:T(8,128)(2,1)S(1)}, bf16[3,3,3,256,256]{4,3,2,1,0:T(8,128)(2,1)}, u32[]{:S(2)}) copy-start(bf16[3,3,3,256,256]{4,3,2,1,0:T(8,128)(2,1)} %v_ref.7) | copy-start | bytes 10616836
  24.9 7.7 %copy-start.3 = (f32[256]{0:T(256)S(1)}, f32[256]{0:T(256)}, u32[]{:S(2)}) copy-start(f32[256]{0:T(256)} %param.9) | copy-start | bytes 3076
  24.9 9.6 %collective-permute-start.6 = (bf16[2,128,256]{2,1,0:T(8,128)(2,1)S(1)}, bf16[2,128,256]{2,1,0:T(8,128)(2,1)S(1)}, u32[]{:S(2)}, u32[]{:S(2)}) collective-permute-start(bf16[2,128,256]{2,1,0:T(8,128)(2,1)S(1)} %get-tuple-element.42), channel_id=1, source_target_pairs={{0,1},{1,2},{2,3},{4,5},{5,6},{6,7},{8,9},{9,10},{10,11},{12,13},{... | collective-permute-start | bytes 393224 | tf_op jit(solution)/shard_map/ppermute | solution.py:371
  31.2 5.7 %collective-permute-start.5 = (bf16[2,128,256]{2,1,0:T(8,128)(2,1)S(1)}, bf16[2,128,256]{2,1,0:T(8,128)(2,1)S(1)}, u32[]{:S(2)}, u32[]{:S(2)}) collective-permute-start(bf16[2,128,256]{2,1,0:T(8,128)(2,1)S(1)} %get-tuple-element.41), channel_id=1, source_target_pairs={{0,1},{1,2},{2,3},{3,0},{4,5},{5,6},{6,7},{7,4},{8,9},{9,10},{10,1... | collective-permute-start | bytes 393224 | tf_op jit(solution)/shard_map/ppermute | solution.py:361

commit v7 on v6

--- a/solution.py
+++ b/solution.py
@@ -276,13 +276,15 @@
     out_ref[0] = total * 0.5 + b_ref[...]
 
 
-def join_body(rest_ref, near_ref, far_ref, out_ref):
+def join_body(rest_ref, near_odd_ref, near_even_ref, far_odd_ref, far_even_ref, out_ref):
     rows = rest_ref.shape[1]
     odd = parity()
-    first = lax.axis_index("tm") == 0
-    for part_ref, start in ((near_ref, 2 * (1 - odd)), (far_ref, odd * (rows - 2))):
-        part = part_ref[...].astype(jnp.float32)
-        part = jnp.where(first, jnp.zeros_like(part), part)
+    time = lax.axis_index("tm")
+    from_odd = lax.rem(time, 2) == 1
+    near = jnp.where(from_odd, near_odd_ref[...], near_even_ref[...])
+    far = jnp.where(from_odd, far_odd_ref[...], far_even_ref[...])
+    for part, start in ((near, 2 * (1 - odd)), (far, odd * (rows - 2))):
+        part = jnp.where(time == 0, jnp.zeros_like(part), part).astype(jnp.float32)
         place = pl.ds(start, part.shape[0])
         out_ref[0, place] = (rest_ref[0, place] + 0.5 * part).astype(jnp.bfloat16)
 
@@ -302,6 +304,16 @@
     outer_full += [(c * tiles + i, (c + 1) % clips * tiles + i) for c in range(clips) for i in unpaired]
     diagonal = [(i * times + s, j * times + t) for i, j in outer_pairs for s, t in forward]
 
+    def swaps(first):
+        turns = {}
+        for t in range(first, times - 1, 2):
+            turns[t], turns[t + 1] = t + 1, t
+        return [
+            (c * times + t, c * times + turns[t] if t in turns else (c + 1) % clips * times + t)
+            for c in range(clips)
+            for t in range(times)
+        ]
+
     def frames(*lead, dtype=jnp.bfloat16):
         return jax.ShapeDtypeStruct((*lead, cols, channels), dtype)
 
@@ -358,7 +370,8 @@
         ),
         0,
     )
-    near_part = lax.ppermute(near_send, "tm", ring)
+    near_odd = lax.ppermute(near_send, ("clips", "tm"), swaps(0))
+    near_even = lax.ppermute(near_send, ("clips", "tm"), swaps(1))
     far_send, h0, h1 = call(
         functools.partial(far_body, tiles, times),
         [frames(2), frames(wide), frames(wide)],
@@ -368,14 +381,15 @@
         ),
         0,
     )
-    far_part = lax.ppermute(far_send, "tm", forward)
+    far_odd = lax.ppermute(far_send, ("clips", "tm"), swaps(0))
+    far_even = lax.ppermute(far_send, ("clips", "tm"), swaps(1))
     (rest,) = call(
         rest_body,
         [frames(1, rows, dtype=f32)],
         (x, h0, h1, weight_second, bias_second),
         3 * unit * rows,
     )
-    (pooled,) = call(join_body, [frames(1, rows)], (rest, near_part, far_part), 0)
+    (pooled,) = call(join_body, [frames(1, rows)], (rest, near_odd, near_even, far_odd, far_even), 0)
     return pooled
 
 

time: 37.9 us -> 36.8 us (0.971)
  starting transfers between devices: 15.7 us -> 15 us
    ppermute x2 -> x4, starting transfers between devices: 7.58 us -> 6.89 us  [the longest x1 4.41 us: block(): far_odd = lax.ppermute(far_send, ('clips', 'tm'), swaps(0))]
    ppermute x2 -> x4, waiting for transfers between devices: 2.3 us -> 1.92 us  [the longest x1 1.05 us: block(): near_odd = lax.ppermute(near_send, ('clips', 'tm'), swaps(0))]
  transfers between devices with their start and end apart: 7 -> 9, of which waited for: 2 -> 4; matrix products, arithmetic and copies ran while one was open for 0% -> 0% of each run, Pallas kernels for 22% -> 23%
where the time goes in v7:
time: 36.8 us; the launch traced here: 36.6 us
  starting transfers between devices  15 us (41%)
  waiting for transfers between devices  12.2 us (33%)
  Pallas kernels  9.2 us (25%)
    ppermute x1, waiting for transfers between devices, block(): earlier = lax.ppermute(x, 'tm', ring)  10.2 us
    pallas_call x10, Pallas kernels, call(): pl.pallas_call(body, out_shape=outs, in_specs=in_specs or [VMEM] * len(ar...  9.2 us
    ppermute x1, starting transfers between devices, block(): far_odd = lax.ppermute(far_send, ('clips', 'tm'), swaps(0))  4.41 us
    ppermute x1, starting transfers between devices, block(): corner = lax.ppermute(outer_edge, ('tile', 'tm'), diagonal)  2.21 us
    ppermute x1, starting transfers between devices, block(): outer = lax.ppermute(outer_edge, ('clips', 'tile'), outer_full)  2.14 us
    ppermute x1, starting transfers between devices, block(): earlier = lax.ppermute(x, 'tm', ring)  2.11 us
    ppermute x1, starting transfers between devices, block(): inner_corner = lax.ppermute(inner_edge, 'tile', inner_pairs)  1.32 us
    ppermute x1, starting transfers between devices, block(): far_even = lax.ppermute(far_send, ('clips', 'tm'), swaps(1))  1.27 us
  transfers between devices with their start and end apart: 9, of which 4 were waited for; matrix products, arithmetic and copies ran while one was open for 0% of the time, Pallas kernels for 23%

profile of v7, /device:TPU:1, one launch (start us, length us, event | category | flops | bytes accessed | tf_op | source)
XLA Modules:
  0.0 36.6 jit_solution(2184532324839697076)
XLA Ops:
  0.0 0.0 copy-start
  0.0 2.1 %collective-permute-start = (bf16[2,4,128,256]{3,2,1,0:T(8,128)(2,1)}, bf16[2,4,128,256]{3,2,1,0:T(8,128)(2,1)S(1)}, u32[]{:S(2)}, u32[]{:S(2)}) collective-permute-start(bf16[2,4,128,256]{3,2,1,0:T(8,128)(2,1)} %x_ref.1), channel_id=1, source_target_pairs={{0,1},{1,2},{2,3},{3,0},{4,5},{5,6},{6,7},{7,4},{8,9},{9,10},{10,1... | collective-permute-start | bytes 1572872 | tf_op jit(solution)/shard_map/ppermute | solution.py:321
  2.1 1.1 %shard_map.55 = (bf16[2,4,128,256]{3,2,1,0:T(8,128)(2,1)S(1)}, bf16[2,2,128,256]{3,2,1,0:T(8,128)(2,1)S(1)}, bf16[2,2,128,256]{3,2,1,0:T(8,128)(2,1)S(1)}) custom-call(bf16[2,4,128,256]{3,2,1,0:T(8,128)(2,1)} %x_ref.1), custom_call_target="tpu_custom_call" | custom-call | flops 10000000000 | tf_op jit(solution)/shard_map/pallas_call | solution.py:16
  3.2 2.1 %collective-permute-start.2 = (bf16[2,2,128,256]{3,2,1,0:T(8,128)(2,1)S(1)}, bf16[2,2,128,256]{3,2,1,0:T(8,128)(2,1)S(1)}, u32[]{:S(2)}, u32[]{:S(2)}) collective-permute-start(bf16[2,2,128,256]{3,2,1,0:T(8,128)(2,1)S(1)} %get-tuple-element.25), channel_id=1, source_target_pairs={{4,8},{8,4},{20,24},{24,20},{0,16},{12,28},{16,0},{28,12},{5,9},{9... | collective-permute-start | bytes 786440 | tf_op jit(solution)/shard_map/ppermute | solution.py:331
  5.4 0.4 %collective-permute-start.4 = (bf16[2,2,128,256]{3,2,1,0:T(8,128)(2,1)S(1)}, bf16[2,2,128,256]{3,2,1,0:T(8,128)(2,1)S(1)}, u32[]{:S(2)}, u32[]{:S(2)}) collective-permute-start(bf16[2,2,128,256]{3,2,1,0:T(8,128)(2,1)S(1)} %get-tuple-element.28), channel_id=1, source_target_pairs={{0,4},{8,12},{4,0},{12,8},{1,5},{9,13},{5,1},{13,9},{2,6},{10,14},... | collective-permute-start | bytes 786440 | tf_op jit(solution)/shard_map/ppermute | solution.py:330
  5.8 10.2 %collective-permute-done.m_ref = bf16[2,4,128,256]{3,2,1,0:T(8,128)(2,1)S(1)} collective-permute-done((bf16[2,4,128,256]{3,2,1,0:T(8,128)(2,1)}, bf16[2,4,128,256]{3,2,1,0:T(8,128)(2,1)S(1)}, u32[]{:S(2)}, u32[]{:S(2)}) %collective-permute-start) | collective-permute-done | bytes 524320 | tf_op jit(solution)/shard_map/ppermute | solution.py:321
  16.0 1.3 %collective-permute-start.3 = (bf16[2,2,128,256]{3,2,1,0:T(8,128)(2,1)S(1)}, bf16[2,2,128,256]{3,2,1,0:T(8,128)(2,1)S(1)}, u32[]{:S(2)}, u32[]{:S(2)}) collective-permute-start(bf16[2,2,128,256]{3,2,1,0:T(8,128)(2,1)S(1)} %shard_map.57), channel_id=1, source_target_pairs={{0,4},{8,12},{4,0},{12,8},{1,5},{9,13},{5,1},{13,9},{2,6},{10,14},... | collective-permute-start | bytes 786440 | tf_op jit(solution)/shard_map/ppermute | solution.py:357
  17.3 2.2 %collective-permute-start.1 = (bf16[2,2,128,256]{3,2,1,0:T(8,128)(2,1)S(1)}, bf16[2,2,128,256]{3,2,1,0:T(8,128)(2,1)S(1)}, u32[]{:S(2)}, u32[]{:S(2)}) collective-permute-start(bf16[2,2,128,256]{3,2,1,0:T(8,128)(2,1)S(1)} %get-tuple-element.25), channel_id=1, source_target_pairs={{4,9},{5,10},{6,11},{8,5},{9,6},{10,7},{20,25},{21,26},{22,27},{24... | collective-permute-start | bytes 786440 | tf_op jit(solution)/shard_map/ppermute | solution.py:332
  19.5 0.0 collective-permute-done.2.outer_ref
  19.5 0.0 copy-done
  19.6 0.0 copy-done.2
  19.6 1.1 %shard_map.56 = (f32[2,128,256]{2,1,0:T(8,128)S(1)}, f32[2,128,256]{2,1,0:T(8,128)S(1)}) custom-call(bf16[2,4,128,256]{3,2,1,0:T(8,128)(2,1)S(1)} %get-tuple-element.24.x_ref, bf16[2,2,128,256]{3,2,1,0:T(8,128)(2,1)S(1)} %collective-permute-done.2.outer_ref, bf16[3,3,3,256,256]{4,3,2,1,0:T(8,128)(2,1)S(1)} %copy-done, f32[1,1,256]{2,1,0:T(1,128)S(1)} %bitcast.2), custom_call_target="tpu_custom_call" | custom-call | tf_op jit(solution)/shard_map/pallas_call | solution.py:16
  20.7 0.0 copy-start.1
  20.7 0.0 collective-permute-done.4.inner_ref
  20.7 2.0 %shard_map.58 = (f32[4,128,256]{2,1,0:T(8,128)S(1)}, f32[4,128,256]{2,1,0:T(8,128)S(1)}) custom-call(bf16[2,4,128,256]{3,2,1,0:T(8,128)(2,1)S(1)} %get-tuple-element.24.x_ref, bf16[2,2,128,256]{3,2,1,0:T(8,128)(2,1)S(1)} %collective-permute-done.4.inner_ref, bf16[3,3,3,256,256]{4,3,2,1,0:T(8,128)(2,1)S(1)} %copy-done, f32[1,1,256]{2,1,0:T(1,128)S(1)} %bitcast.3), custom_call_target="tpu_custom_call" | custom-call | flops 1811939328 | tf_op jit(solution)/shard_map/pallas_call | solution.py:16
  22.7 0.0 copy-done.1
  22.7 2.1 %shard_map.60 = (bf16[2,128,256]{2,1,0:T(8,128)(2,1)S(1)}, bf16[2,128,256]{2,1,0:T(8,128)(2,1)S(1)}, bf16[6,128,256]{2,1,0:T(8,128)(2,1)S(1)}, bf16[6,128,256]{2,1,0:T(8,128)(2,1)S(1)}) custom-call(bf16[3,3,3,256,256]{4,3,2,1,0:T(8,128)(2,1)S(1)} %copy-done.1, f32[4,128,256]{2,1,0:T(8,128)S(1)} %get-tuple-element.29.acc0_ref, ...), custom_call_target="tpu_custom_call" | custom-call | tf_op jit(solution)/shard_map/pallas_call | solution.py:16
  24.8 0.0 collective-permute-done.3.inner_ref
  24.8 0.0 collective-permute-done.1.outer_ref
  24.9 0.0 copy-start.3
  24.9 0.1 shard_map.62
  24.9 1.3 %collective-permute-start.8 = (bf16[2,128,256]{2,1,0:T(8,128)(2,1)S(1)}, bf16[2,128,256]{2,1,0:T(8,128)(2,1)S(1)}, u32[]{:S(2)}, u32[]{:S(2)}) collective-permute-start(bf16[2,128,256]{2,1,0:T(8,128)(2,1)S(1)} %get-tuple-element.42), channel_id=1, source_target_pairs={{0,16},{1,2},{2,1},{3,19},{16,0},{17,18},{18,17},{19,3},{4,20},{5,... | collective-permute-start | bytes 393224 | tf_op jit(solution)/shard_map/ppermute | solution.py:385
  26.2 4.4 %collective-permute-start.7 = (bf16[2,128,256]{2,1,0:T(8,128)(2,1)S(1)}, bf16[2,128,256]{2,1,0:T(8,128)(2,1)S(1)}, u32[]{:S(2)}, u32[]{:S(2)}) collective-permute-start(bf16[2,128,256]{2,1,0:T(8,128)(2,1)S(1)} %get-tuple-element.42), channel_id=1, source_target_pairs={{0,1},{1,0},{2,3},{3,2},{16,17},{17,16},{18,19},{19,18},{4,5},{5,4... | collective-permute-start | bytes 393224 | tf_op jit(solution)/shard_map/ppermute | solution.py:384
  30.6 1.2 %collective-permute-start.6 = (bf16[2,128,256]{2,1,0:T(8,128)(2,1)S(1)}, bf16[2,128,256]{2,1,0:T(8,128)(2,1)S(1)}, u32[]{:S(2)}, u32[]{:S(2)}) collective-permute-start(bf16[2,128,256]{2,1,0:T(8,128)(2,1)S(1)} %get-tuple-element.41), channel_id=1, source_target_pairs={{0,16},{1,2},{2,1},{3,19},{16,0},{17,18},{18,17},{19,3},{4,20},{5,... | collective-permute-start | bytes 393224 | tf_op jit(solution)/shard_map/ppermute | solution.py:374
  31.8 0.0 collective-permute-start.5
  31.8 0.0 copy-done.3
  31.8 2.0 %shard_map.63.rest_ref = f32[1,4,128,256]{3,2,1,0:T(8,128)S(1)} custom-call(bf16[2,4,128,256]{3,2,1,0:T(8,128)(2,1)S(1)} %get-tuple-element.24.x_ref, bf16[6,128,256]{2,1,0:T(8,128)(2,1)S(1)} %get-tuple-element.39.h0_ref, bf16[6,128,256]{2,1,0:T(8,128)(2,1)S(1)} %get-tuple-element.40.h1_ref, bf16[3,3,3,256,256]{4,3,2,1,0:T(8,128)(2,1)S(1)} %copy-done.1, ...), custom_call_target="tpu_custom_call" | custom-call | flops 1811939328 | tf_op jit(solution)/shard_map/pallas_call | solution.py:16
  33.9 0.0 collective-permute-done.8.far_even_ref
  33.9 0.2 collective-permute-done.7.far_odd_ref
  34.1 0.7 %collective-permute-done.6.near_even_ref = bf16[2,128,256]{2,1,0:T(8,128)(2,1)S(1)} collective-permute-done((bf16[2,128,256]{2,1,0:T(8,128)(2,1)S(1)}, bf16[2,128,256]{2,1,0:T(8,128)(2,1)S(1)}, u32[]{:S(2)}, u32[]{:S(2)}) %collective-permute-start.6) | collective-permute-done | bytes 131104 | tf_op jit(solution)/shard_map/ppermute | solution.py:374
  34.7 1.1 %collective-permute-done.5.near_odd_ref = bf16[2,128,256]{2,1,0:T(8,128)(2,1)S(1)} collective-permute-done((bf16[2,128,256]{2,1,0:T(8,128)(2,1)S(1)}, bf16[2,128,256]{2,1,0:T(8,128)(2,1)S(1)}, u32[]{:S(2)}, u32[]{:S(2)}) %collective-permute-start.5) | collective-permute-done | bytes 131104 | tf_op jit(solution)/shard_map/ppermute | solution.py:373
  35.8 0.8 %shard_map.64 = bf16[1,4,128,256]{3,2,1,0:T(8,128)(2,1)} custom-call(f32[1,4,128,256]{3,2,1,0:T(8,128)S(1)} %shard_map.63.rest_ref, bf16[2,128,256]{2,1,0:T(8,128)(2,1)S(1)} %collective-permute-done.5.near_odd_ref, bf16[2,128,256]{2,1,0:T(8,128)(2,1)S(1)} %collective-permute-done.6.near_even_ref, ...), custom_call_target="tpu_custom_call" | custom-call | tf_op jit(solution)/shard_map/pallas_call | solution.py:16
  (4 shorter events, 0.1 us)
Async XLA Ops:
  0.0 19.6 %copy-start = (bf16[3,3,3,256,256]{4,3,2,1,0:T(8,128)(2,1)S(1)}, bf16[3,3,3,256,256]{4,3,2,1,0:T(8,128)(2,1)}, u32[]{:S(2)}) copy-start(bf16[3,3,3,256,256]{4,3,2,1,0:T(8,128)(2,1)} %w_ref.9) | copy-start | bytes 10616836
  0.0 19.6 %copy-start.2 = (f32[256]{0:T(256)S(1)}, f32[256]{0:T(256)}, u32[]{:S(2)}) copy-start(f32[256]{0:T(256)} %param.7) | copy-start | bytes 3076
  0.0 16.0 %collective-permute-start = (bf16[2,4,128,256]{3,2,1,0:T(8,128)(2,1)}, bf16[2,4,128,256]{3,2,1,0:T(8,128)(2,1)S(1)}, u32[]{:S(2)}, u32[]{:S(2)}) collective-permute-start(bf16[2,4,128,256]{3,2,1,0:T(8,128)(2,1)} %x_ref.1), channel_id=1, source_target_pairs={{0,1},{1,2},{2,3},{3,0},{4,5},{5,6},{6,7},{7,4},{8,9},{9,10},{10,1... | collective-permute-start | bytes 1572872 | tf_op jit(solution)/shard_map/ppermute | solution.py:321
  3.2 16.3 %collective-permute-start.2 = (bf16[2,2,128,256]{3,2,1,0:T(8,128)(2,1)S(1)}, bf16[2,2,128,256]{3,2,1,0:T(8,128)(2,1)S(1)}, u32[]{:S(2)}, u32[]{:S(2)}) collective-permute-start(bf16[2,2,128,256]{3,2,1,0:T(8,128)(2,1)S(1)} %get-tuple-element.25), channel_id=1, source_target_pairs={{4,8},{8,4},{20,24},{24,20},{0,16},{12,28},{16,0},{28,12},{5,9},{9... | collective-permute-start | bytes 786440 | tf_op jit(solution)/shard_map/ppermute | solution.py:331
  5.4 15.3 %collective-permute-start.4 = (bf16[2,2,128,256]{3,2,1,0:T(8,128)(2,1)S(1)}, bf16[2,2,128,256]{3,2,1,0:T(8,128)(2,1)S(1)}, u32[]{:S(2)}, u32[]{:S(2)}) collective-permute-start(bf16[2,2,128,256]{3,2,1,0:T(8,128)(2,1)S(1)} %get-tuple-element.28), channel_id=1, source_target_pairs={{0,4},{8,12},{4,0},{12,8},{1,5},{9,13},{5,1},{13,9},{2,6},{10,14},... | collective-permute-start | bytes 786440 | tf_op jit(solution)/shard_map/ppermute | solution.py:330
  16.0 8.8 %collective-permute-start.3 = (bf16[2,2,128,256]{3,2,1,0:T(8,128)(2,1)S(1)}, bf16[2,2,128,256]{3,2,1,0:T(8,128)(2,1)S(1)}, u32[]{:S(2)}, u32[]{:S(2)}) collective-permute-start(bf16[2,2,128,256]{3,2,1,0:T(8,128)(2,1)S(1)} %shard_map.57), channel_id=1, source_target_pairs={{0,4},{8,12},{4,0},{12,8},{1,5},{9,13},{5,1},{13,9},{2,6},{10,14},... | collective-permute-start | bytes 786440 | tf_op jit(solution)/shard_map/ppermute | solution.py:357
  17.3 7.5 %collective-permute-start.1 = (bf16[2,2,128,256]{3,2,1,0:T(8,128)(2,1)S(1)}, bf16[2,2,128,256]{3,2,1,0:T(8,128)(2,1)S(1)}, u32[]{:S(2)}, u32[]{:S(2)}) collective-permute-start(bf16[2,2,128,256]{3,2,1,0:T(8,128)(2,1)S(1)} %get-tuple-element.25), channel_id=1, source_target_pairs={{4,9},{5,10},{6,11},{8,5},{9,6},{10,7},{20,25},{21,26},{22,27},{24... | collective-permute-start | bytes 786440 | tf_op jit(solution)/shard_map/ppermute | solution.py:332
  20.7 2.0 %copy-start.1 = (bf16[3,3,3,256,256]{4,3,2,1,0:T(8,128)(2,1)S(1)}, bf16[3,3,3,256,256]{4,3,2,1,0:T(8,128)(2,1)}, u32[]{:S(2)}) copy-start(bf16[3,3,3,256,256]{4,3,2,1,0:T(8,128)(2,1)} %v_ref.7) | copy-start | bytes 10616836
  24.9 7.0 %copy-start.3 = (f32[256]{0:T(256)S(1)}, f32[256]{0:T(256)}, u32[]{:S(2)}) copy-start(f32[256]{0:T(256)} %param.9) | copy-start | bytes 3076
  24.9 8.9 %collective-permute-start.8 = (bf16[2,128,256]{2,1,0:T(8,128)(2,1)S(1)}, bf16[2,128,256]{2,1,0:T(8,128)(2,1)S(1)}, u32[]{:S(2)}, u32[]{:S(2)}) collective-permute-start(bf16[2,128,256]{2,1,0:T(8,128)(2,1)S(1)} %get-tuple-element.42), channel_id=1, source_target_pairs={{0,16},{1,2},{2,1},{3,19},{16,0},{17,18},{18,17},{19,3},{4,20},{5,... | collective-permute-start | bytes 393224 | tf_op jit(solution)/shard_map/ppermute | solution.py:385
  26.2 7.9 %collective-permute-start.7 = (bf16[2,128,256]{2,1,0:T(8,128)(2,1)S(1)}, bf16[2,128,256]{2,1,0:T(8,128)(2,1)S(1)}, u32[]{:S(2)}, u32[]{:S(2)}) collective-permute-start(bf16[2,128,256]{2,1,0:T(8,128)(2,1)S(1)} %get-tuple-element.42), channel_id=1, source_target_pairs={{0,1},{1,0},{2,3},{3,2},{16,17},{17,16},{18,19},{19,18},{4,5},{5,4... | collective-permute-start | bytes 393224 | tf_op jit(solution)/shard_map/ppermute | solution.py:384
  30.6 4.1 %collective-permute-start.6 = (bf16[2,128,256]{2,1,0:T(8,128)(2,1)S(1)}, bf16[2,128,256]{2,1,0:T(8,128)(2,1)S(1)}, u32[]{:S(2)}, u32[]{:S(2)}) collective-permute-start(bf16[2,128,256]{2,1,0:T(8,128)(2,1)S(1)} %get-tuple-element.41), channel_id=1, source_target_pairs={{0,16},{1,2},{2,1},{3,19},{16,0},{17,18},{18,17},{19,3},{4,20},{5,... | collective-permute-start | bytes 393224 | tf_op jit(solution)/shard_map/ppermute | solution.py:374
  31.8 4.0 %collective-permute-start.5 = (bf16[2,128,256]{2,1,0:T(8,128)(2,1)S(1)}, bf16[2,128,256]{2,1,0:T(8,128)(2,1)S(1)}, u32[]{:S(2)}, u32[]{:S(2)}) collective-permute-start(bf16[2,128,256]{2,1,0:T(8,128)(2,1)S(1)} %get-tuple-element.41), channel_id=1, source_target_pairs={{0,1},{1,0},{2,3},{3,2},{16,17},{17,16},{18,19},{19,18},{4,5},{5,4... | collective-permute-start | bytes 393224 | tf_op jit(solution)/shard_map/ppermute | solution.py:373

commit v8 on v5

--- a/solution.py
+++ b/solution.py
@@ -243,9 +243,9 @@
 def rest_body(x_ref, h0_ref, h1_ref, v_ref, b_ref, out_ref):
     rows, cols = x_ref.shape[1:3]
     h0, h1 = h0_ref[...], h1_ref[...]
-    both = (h0.astype(jnp.float32) + h1.astype(jnp.float32)).astype(jnp.bfloat16)
-    taps = row_taps(h0, rows) + row_taps(both, rows)
-    part = convolved(taps, weight_rows(v_ref, 1) + weight_rows(v_ref, 2), rows, cols)
+    taps = row_taps(h0, rows) + row_taps(h0, rows) + row_taps(h1, rows)
+    weights = weight_rows(v_ref, 1) + 2 * weight_rows(v_ref, 2)
+    part = convolved(taps, weights, rows, cols)
     total = x_ref[0].astype(jnp.float32) + x_ref[1].astype(jnp.float32) + part
     out_ref[0] = total * 0.5 + b_ref[...]
 
@@ -342,7 +342,7 @@
         rest_body,
         [frames(1, rows, dtype=f32)],
         (x, h0, h1, weight_second, bias_second),
-        2 * unit * rows,
+        3 * unit * rows,
     )
     (pooled,) = call(join_body, [frames(1, rows)], (rest, near_part, far_part), 0)
     return pooled

time: 38 us -> 38 us (level)
  Pallas kernels: 8.61 us -> 9.22 us
  waiting for transfers between devices: 13.1 us -> 12.5 us
    ppermute x1, waiting for transfers between devices: 2.9 us -> 2.3 us  [block(): near_part = lax.ppermute(near_send, 'tm', ring)]
    pallas_call x9, Pallas kernels: 8.61 us -> 9.22 us  [call(): pl.pallas_call(body, out_shape=outs, in_specs=in_specs or [VMEM] * len(ar...]
  transfers between devices with their start and end apart: 7 -> 7, of which waited for: 2 -> 2; matrix products, arithmetic and copies ran while one was open for 0% -> 0% of each run, Pallas kernels for 18% -> 20%
where the time goes in v8:
time: 38 us; the launch traced here: 37.8 us
  starting transfers between devices  15.9 us (42%)
  waiting for transfers between devices  12.5 us (33%)
  Pallas kernels  9.22 us (24%)
    ppermute x1, waiting for transfers between devices, block(): earlier = lax.ppermute(x, 'tm', ring)  10.2 us
    pallas_call x9, Pallas kernels, call(): pl.pallas_call(body, out_shape=outs, in_specs=in_specs or [VMEM] * len(ar...  9.22 us
    ppermute x1, starting transfers between devices, block(): far_part = lax.ppermute(far_send, 'tm', forward)  6.36 us
    ppermute x1, waiting for transfers between devices, block(): near_part = lax.ppermute(near_send, 'tm', ring)  2.3 us
    ppermute x1, starting transfers between devices, block(): corner = lax.ppermute(outer_edge, ('tile', 'tm'), diagonal)  2.21 us
    ppermute x1, starting transfers between devices, block(): outer = lax.ppermute(outer_edge, ('clips', 'tile'), outer_full)  2.14 us
    ppermute x1, starting transfers between devices, block(): earlier = lax.ppermute(x, 'tm', ring)  2.11 us
    ppermute x1, starting transfers between devices, block(): near_part = lax.ppermute(near_send, 'tm', ring)  1.35 us
  transfers between devices with their start and end apart: 7, of which 2 were waited for; matrix products, arithmetic and copies ran while one was open for 0% of the time, Pallas kernels for 20%

profile of v8, /device:TPU:1, one launch (start us, length us, event | category | flops | bytes accessed | tf_op | source)
XLA Modules:
  0.0 37.8 jit_solution(15907051804867559078)
XLA Ops:
  0.0 0.0 copy-start.2
  0.0 0.0 copy-start
  0.0 2.1 %collective-permute-start = (bf16[2,4,128,256]{3,2,1,0:T(8,128)(2,1)}, bf16[2,4,128,256]{3,2,1,0:T(8,128)(2,1)S(1)}, u32[]{:S(2)}, u32[]{:S(2)}) collective-permute-start(bf16[2,4,128,256]{3,2,1,0:T(8,128)(2,1)} %x_ref.1), channel_id=1, source_target_pairs={{0,1},{1,2},{2,3},{3,0},{4,5},{5,6},{6,7},{7,4},{8,9},{9,10},{10,1... | collective-permute-start | bytes 1572872 | tf_op jit(solution)/shard_map/ppermute | solution.py:283
  2.1 1.1 %shard_map.55 = (bf16[2,4,128,256]{3,2,1,0:T(8,128)(2,1)S(1)}, bf16[2,2,128,256]{3,2,1,0:T(8,128)(2,1)S(1)}, bf16[2,2,128,256]{3,2,1,0:T(8,128)(2,1)S(1)}) custom-call(bf16[2,4,128,256]{3,2,1,0:T(8,128)(2,1)} %x_ref.1), custom_call_target="tpu_custom_call" | custom-call | flops 10000000000 | tf_op jit(solution)/shard_map/pallas_call | solution.py:16
  3.2 2.1 %collective-permute-start.2 = (bf16[2,2,128,256]{3,2,1,0:T(8,128)(2,1)S(1)}, bf16[2,2,128,256]{3,2,1,0:T(8,128)(2,1)S(1)}, u32[]{:S(2)}, u32[]{:S(2)}) collective-permute-start(bf16[2,2,128,256]{3,2,1,0:T(8,128)(2,1)S(1)} %get-tuple-element.21), channel_id=1, source_target_pairs={{4,8},{8,4},{20,24},{24,20},{0,16},{12,28},{16,0},{28,12},{5,9},{9... | collective-permute-start | bytes 786440 | tf_op jit(solution)/shard_map/ppermute | solution.py:293
  5.4 0.4 collective-permute-start.4
  5.8 10.2 %collective-permute-done.m_ref = bf16[2,4,128,256]{3,2,1,0:T(8,128)(2,1)S(1)} collective-permute-done((bf16[2,4,128,256]{3,2,1,0:T(8,128)(2,1)}, bf16[2,4,128,256]{3,2,1,0:T(8,128)(2,1)S(1)}, u32[]{:S(2)}, u32[]{:S(2)}) %collective-permute-start) | collective-permute-done | bytes 524320 | tf_op jit(solution)/shard_map/ppermute | solution.py:283
  16.0 1.3 %collective-permute-start.3 = (bf16[2,2,128,256]{3,2,1,0:T(8,128)(2,1)S(1)}, bf16[2,2,128,256]{3,2,1,0:T(8,128)(2,1)S(1)}, u32[]{:S(2)}, u32[]{:S(2)}) collective-permute-start(bf16[2,2,128,256]{3,2,1,0:T(8,128)(2,1)S(1)} %shard_map.57), channel_id=1, source_target_pairs={{0,4},{8,12},{4,0},{12,8},{1,5},{9,13},{5,1},{13,9},{2,6},{10,14},... | collective-permute-start | bytes 786440 | tf_op jit(solution)/shard_map/ppermute | solution.py:313
  17.3 2.2 %collective-permute-start.1 = (bf16[2,2,128,256]{3,2,1,0:T(8,128)(2,1)S(1)}, bf16[2,2,128,256]{3,2,1,0:T(8,128)(2,1)S(1)}, u32[]{:S(2)}, u32[]{:S(2)}) collective-permute-start(bf16[2,2,128,256]{3,2,1,0:T(8,128)(2,1)S(1)} %get-tuple-element.21), channel_id=1, source_target_pairs={{4,9},{5,10},{6,11},{8,5},{9,6},{10,7},{20,25},{21,26},{22,27},{24... | collective-permute-start | bytes 786440 | tf_op jit(solution)/shard_map/ppermute | solution.py:294
  19.5 0.0 collective-permute-done.2.outer_ref
  19.5 0.0 copy-done.2
  19.6 0.0 copy-done
  19.6 1.1 %shard_map.56 = (f32[2,128,256]{2,1,0:T(8,128)S(1)}, f32[2,128,256]{2,1,0:T(8,128)S(1)}) custom-call(bf16[2,4,128,256]{3,2,1,0:T(8,128)(2,1)S(1)} %get-tuple-element.20.x_ref, bf16[2,2,128,256]{3,2,1,0:T(8,128)(2,1)S(1)} %collective-permute-done.2.outer_ref, bf16[3,3,3,256,256]{4,3,2,1,0:T(8,128)(2,1)S(1)} %copy-done, f32[1,1,256]{2,1,0:T(1,128)S(1)} %bitcast.2), custom_call_target="tpu_custom_call" | custom-call | tf_op jit(solution)/shard_map/pallas_call | solution.py:16
  20.7 0.0 copy-start.1
  20.7 0.0 collective-permute-done.4.inner_ref
  20.7 2.0 %shard_map.58 = (f32[4,128,256]{2,1,0:T(8,128)S(1)}, f32[4,128,256]{2,1,0:T(8,128)S(1)}) custom-call(bf16[2,4,128,256]{3,2,1,0:T(8,128)(2,1)S(1)} %get-tuple-element.20.x_ref, bf16[2,2,128,256]{3,2,1,0:T(8,128)(2,1)S(1)} %collective-permute-done.4.inner_ref, bf16[3,3,3,256,256]{4,3,2,1,0:T(8,128)(2,1)S(1)} %copy-done, f32[1,1,256]{2,1,0:T(1,128)S(1)} %bitcast.3), custom_call_target="tpu_custom_call" | custom-call | flops 1811939328 | tf_op jit(solution)/shard_map/pallas_call | solution.py:16
  22.7 0.0 copy-done.1
  22.7 0.2 shard_map.59
  22.9 0.0 collective-permute-done.3.inner_ref
  22.9 1.0 %shard_map.60 = (bf16[2,128,256]{2,1,0:T(8,128)(2,1)S(1)}, bf16[4,128,256]{2,1,0:T(8,128)(2,1)S(1)}, bf16[4,128,256]{2,1,0:T(8,128)(2,1)S(1)}) custom-call(bf16[2,4,128,256]{3,2,1,0:T(8,128)(2,1)S(1)} %collective-permute-done.m_ref, bf16[2,2,128,256]{3,2,1,0:T(8,128)(2,1)S(1)} %collective-permute-done.3.inner_ref, bf16[3,3,3,256,256]{4,3,2,1,0:T(8,128)(2,1)S(1)} %copy-done, ...), custom_call_target="tpu_custom_call" | custom-call | tf_op jit(solution)/shard_map/pallas_call | solution.py:16
  23.9 0.0 collective-permute-done.1.outer_ref
  23.9 0.0 copy-start.3
  23.9 1.0 %shard_map.61 = (bf16[2,128,256]{2,1,0:T(8,128)(2,1)S(1)}, bf16[6,128,256]{2,1,0:T(8,128)(2,1)S(1)}, bf16[6,128,256]{2,1,0:T(8,128)(2,1)S(1)}) custom-call(bf16[2,4,128,256]{3,2,1,0:T(8,128)(2,1)S(1)} %collective-permute-done.m_ref, bf16[2,2,128,256]{3,2,1,0:T(8,128)(2,1)S(1)} %collective-permute-done.1.outer_ref, bf16[3,3,3,256,256]{4,3,2,1,0:T(8,128)(2,1)S(1)} %copy-done, ...), custom_call_target="tpu_custom_call" | custom-call | tf_op jit(solution)/shard_map/pallas_call | solution.py:16
  25.0 6.4 %collective-permute-start.6 = (bf16[2,128,256]{2,1,0:T(8,128)(2,1)S(1)}, bf16[2,128,256]{2,1,0:T(8,128)(2,1)S(1)}, u32[]{:S(2)}, u32[]{:S(2)}) collective-permute-start(bf16[2,128,256]{2,1,0:T(8,128)(2,1)S(1)} %get-tuple-element.34), channel_id=1, source_target_pairs={{0,1},{1,2},{2,3},{4,5},{5,6},{6,7},{8,9},{9,10},{10,11},{12,13},{... | collective-permute-start | bytes 393224 | tf_op jit(solution)/shard_map/ppermute | solution.py:340
  31.3 1.3 %collective-permute-start.5 = (bf16[2,128,256]{2,1,0:T(8,128)(2,1)S(1)}, bf16[2,128,256]{2,1,0:T(8,128)(2,1)S(1)}, u32[]{:S(2)}, u32[]{:S(2)}) collective-permute-start(bf16[2,128,256]{2,1,0:T(8,128)(2,1)S(1)} %get-tuple-element.33), channel_id=1, source_target_pairs={{0,1},{1,2},{2,3},{3,0},{4,5},{5,6},{6,7},{7,4},{8,9},{9,10},{10,1... | collective-permute-start | bytes 393224 | tf_op jit(solution)/shard_map/ppermute | solution.py:332
  32.7 0.0 copy-done.3
  32.7 2.0 %shard_map.62.rest_ref = f32[1,4,128,256]{3,2,1,0:T(8,128)S(1)} custom-call(bf16[2,4,128,256]{3,2,1,0:T(8,128)(2,1)S(1)} %get-tuple-element.20.x_ref, bf16[6,128,256]{2,1,0:T(8,128)(2,1)S(1)} %get-tuple-element.31.h0_ref, bf16[6,128,256]{2,1,0:T(8,128)(2,1)S(1)} %get-tuple-element.32.h1_ref, bf16[3,3,3,256,256]{4,3,2,1,0:T(8,128)(2,1)S(1)} %copy-done.1, ...), custom_call_target="tpu_custom_call" | custom-call | flops 1811939328 | tf_op jit(solution)/shard_map/pallas_call | solution.py:16
  34.7 0.0 collective-permute-done.6.far_ref
  34.7 2.3 %collective-permute-done.5.near_ref = bf16[2,128,256]{2,1,0:T(8,128)(2,1)S(1)} collective-permute-done((bf16[2,128,256]{2,1,0:T(8,128)(2,1)S(1)}, bf16[2,128,256]{2,1,0:T(8,128)(2,1)S(1)}, u32[]{:S(2)}, u32[]{:S(2)}) %collective-permute-start.5) | collective-permute-done | bytes 131104 | tf_op jit(solution)/shard_map/ppermute | solution.py:332
  37.0 0.8 %shard_map.63 = bf16[1,4,128,256]{3,2,1,0:T(8,128)(2,1)} custom-call(f32[1,4,128,256]{3,2,1,0:T(8,128)S(1)} %shard_map.62.rest_ref, bf16[2,128,256]{2,1,0:T(8,128)(2,1)S(1)} %collective-permute-done.5.near_ref, bf16[2,128,256]{2,1,0:T(8,128)(2,1)S(1)} %collective-permute-done.6.far_ref), custom_call_target="tpu_custom_call" | custom-call | tf_op jit(solution)/shard_map/pallas_call | solution.py:16
  (1 shorter events, 0.0 us)
Async XLA Ops:
  0.0 19.6 %copy-start.2 = (f32[256]{0:T(256)S(1)}, f32[256]{0:T(256)}, u32[]{:S(2)}) copy-start(f32[256]{0:T(256)} %param.7) | copy-start | bytes 3076
  0.0 19.6 %copy-start = (bf16[3,3,3,256,256]{4,3,2,1,0:T(8,128)(2,1)S(1)}, bf16[3,3,3,256,256]{4,3,2,1,0:T(8,128)(2,1)}, u32[]{:S(2)}) copy-start(bf16[3,3,3,256,256]{4,3,2,1,0:T(8,128)(2,1)} %w_ref.9) | copy-start | bytes 10616836
  0.0 16.0 %collective-permute-start = (bf16[2,4,128,256]{3,2,1,0:T(8,128)(2,1)}, bf16[2,4,128,256]{3,2,1,0:T(8,128)(2,1)S(1)}, u32[]{:S(2)}, u32[]{:S(2)}) collective-permute-start(bf16[2,4,128,256]{3,2,1,0:T(8,128)(2,1)} %x_ref.1), channel_id=1, source_target_pairs={{0,1},{1,2},{2,3},{3,0},{4,5},{5,6},{6,7},{7,4},{8,9},{9,10},{10,1... | collective-permute-start | bytes 1572872 | tf_op jit(solution)/shard_map/ppermute | solution.py:283
  3.2 16.3 %collective-permute-start.2 = (bf16[2,2,128,256]{3,2,1,0:T(8,128)(2,1)S(1)}, bf16[2,2,128,256]{3,2,1,0:T(8,128)(2,1)S(1)}, u32[]{:S(2)}, u32[]{:S(2)}) collective-permute-start(bf16[2,2,128,256]{3,2,1,0:T(8,128)(2,1)S(1)} %get-tuple-element.21), channel_id=1, source_target_pairs={{4,8},{8,4},{20,24},{24,20},{0,16},{12,28},{16,0},{28,12},{5,9},{9... | collective-permute-start | bytes 786440 | tf_op jit(solution)/shard_map/ppermute | solution.py:293
  5.4 15.3 %collective-permute-start.4 = (bf16[2,2,128,256]{3,2,1,0:T(8,128)(2,1)S(1)}, bf16[2,2,128,256]{3,2,1,0:T(8,128)(2,1)S(1)}, u32[]{:S(2)}, u32[]{:S(2)}) collective-permute-start(bf16[2,2,128,256]{3,2,1,0:T(8,128)(2,1)S(1)} %get-tuple-element.24), channel_id=1, source_target_pairs={{0,4},{8,12},{4,0},{12,8},{1,5},{9,13},{5,1},{13,9},{2,6},{10,14},... | collective-permute-start | bytes 786440 | tf_op jit(solution)/shard_map/ppermute | solution.py:292
  16.0 6.9 %collective-permute-start.3 = (bf16[2,2,128,256]{3,2,1,0:T(8,128)(2,1)S(1)}, bf16[2,2,128,256]{3,2,1,0:T(8,128)(2,1)S(1)}, u32[]{:S(2)}, u32[]{:S(2)}) collective-permute-start(bf16[2,2,128,256]{3,2,1,0:T(8,128)(2,1)S(1)} %shard_map.57), channel_id=1, source_target_pairs={{0,4},{8,12},{4,0},{12,8},{1,5},{9,13},{5,1},{13,9},{2,6},{10,14},... | collective-permute-start | bytes 786440 | tf_op jit(solution)/shard_map/ppermute | solution.py:313
  17.3 6.6 %collective-permute-start.1 = (bf16[2,2,128,256]{3,2,1,0:T(8,128)(2,1)S(1)}, bf16[2,2,128,256]{3,2,1,0:T(8,128)(2,1)S(1)}, u32[]{:S(2)}, u32[]{:S(2)}) collective-permute-start(bf16[2,2,128,256]{3,2,1,0:T(8,128)(2,1)S(1)} %get-tuple-element.21), channel_id=1, source_target_pairs={{4,9},{5,10},{6,11},{8,5},{9,6},{10,7},{20,25},{21,26},{22,27},{24... | collective-permute-start | bytes 786440 | tf_op jit(solution)/shard_map/ppermute | solution.py:294
  20.7 2.0 %copy-start.1 = (bf16[3,3,3,256,256]{4,3,2,1,0:T(8,128)(2,1)S(1)}, bf16[3,3,3,256,256]{4,3,2,1,0:T(8,128)(2,1)}, u32[]{:S(2)}) copy-start(bf16[3,3,3,256,256]{4,3,2,1,0:T(8,128)(2,1)} %v_ref.5) | copy-start | bytes 10616836
  23.9 8.8 %copy-start.3 = (f32[256]{0:T(256)S(1)}, f32[256]{0:T(256)}, u32[]{:S(2)}) copy-start(f32[256]{0:T(256)} %param.9) | copy-start | bytes 3076
  25.0 9.7 %collective-permute-start.6 = (bf16[2,128,256]{2,1,0:T(8,128)(2,1)S(1)}, bf16[2,128,256]{2,1,0:T(8,128)(2,1)S(1)}, u32[]{:S(2)}, u32[]{:S(2)}) collective-permute-start(bf16[2,128,256]{2,1,0:T(8,128)(2,1)S(1)} %get-tuple-element.34), channel_id=1, source_target_pairs={{0,1},{1,2},{2,3},{4,5},{5,6},{6,7},{8,9},{9,10},{10,11},{12,13},{... | collective-permute-start | bytes 393224 | tf_op jit(solution)/shard_map/ppermute | solution.py:340
  31.3 5.7 %collective-permute-start.5 = (bf16[2,128,256]{2,1,0:T(8,128)(2,1)S(1)}, bf16[2,128,256]{2,1,0:T(8,128)(2,1)S(1)}, u32[]{:S(2)}, u32[]{:S(2)}) collective-permute-start(bf16[2,128,256]{2,1,0:T(8,128)(2,1)S(1)} %get-tuple-element.33), channel_id=1, source_target_pairs={{0,1},{1,2},{2,3},{3,0},{4,5},{5,6},{6,7},{7,4},{8,9},{9,10},{10,1... | collective-permute-start | bytes 393224 | tf_op jit(solution)/shard_map/ppermute | solution.py:332

commit v9 on v8

--- a/solution.py
+++ b/solution.py
@@ -12,13 +12,14 @@
 HBM = pl.BlockSpec(memory_space=pltpu.HBM)
 
 
-def call(body, outs, args, flops, in_specs=None, scratch=()):
+def call(body, outs, args, flops, in_specs=None, out_specs=None, scratch=(), aliases=None):
     return pl.pallas_call(
         body,
         out_shape=outs,
         in_specs=in_specs or [VMEM] * len(args),
-        out_specs=[VMEM] * len(outs),
+        out_specs=out_specs or [VMEM] * len(outs),
         scratch_shapes=scratch,
+        input_output_aliases=aliases or {},
         compiler_params=pltpu.CompilerParams(vmem_limit_bytes=16 << 20),
         cost_estimate=pl.CostEstimate(flops=flops, bytes_accessed=0, transcendentals=0),
     )(*args)
@@ -225,40 +226,51 @@
 ):
     rows, cols = m_ref.shape[1:3]
     odd = parity()
-    far = places(rows)[2]
-    near = pl.ds(2 * (1 - odd), rows)
 
     def slab(f):
         return outer_slab(outer_ref[f], m_ref.at[f], tiles)
 
+    def beside(h_ref, near_ref):
+        near = near_ref[pl.ds(odd * (rows - 2), 2)]
+        return either([h_ref[...], near], [near, h_ref[...]])
+
     bases = [lambda: acc0_ref[...], lambda: acc1_ref[...]]
+    place = places(rows)[2]
+    hidden(slab, bases, place, w_ref, tiles, rows, h0_ref, h1_ref, sum0_ref, sum1_ref)
+    h0, h1 = beside(h0_ref, near0_ref), beside(h1_ref, near1_ref)
+    partial_rows(times, h0, h1, v_ref, 2, cols, send_ref)
+
+
+def rest_body(
+    x_ref, near0_ref, near1_ref, far0_ref, far1_ref, v_ref, b_ref, out_ref, h0_ref, h1_ref
+):
+    rows, cols = x_ref.shape[1:3]
+    near, far = pl.ds(2 * (1 - parity()), rows), places(rows)[2]
     h0_ref[near], h1_ref[near] = near0_ref[...], near1_ref[...]
-    hidden(
-        slab, bases, far, w_ref, tiles, rows, h0_ref.at[far], h1_ref.at[far], sum0_ref, sum1_ref
-    )
-    side = pl.ds(odd * (rows - 2), 4)
-    partial_rows(times, h0_ref[side], h1_ref[side], v_ref, 2, cols, send_ref)
-
-
-def rest_body(x_ref, h0_ref, h1_ref, v_ref, b_ref, out_ref):
-    rows, cols = x_ref.shape[1:3]
-    h0, h1 = h0_ref[...], h1_ref[...]
-    taps = row_taps(h0, rows) + row_taps(h0, rows) + row_taps(h1, rows)
+    h0_ref[far], h1_ref[far] = far0_ref[...], far1_ref[...]
+    h0, h1 = row_taps(h0_ref[...], rows), row_taps(h1_ref[...], rows)
     weights = weight_rows(v_ref, 1) + 2 * weight_rows(v_ref, 2)
-    part = convolved(taps, weights, rows, cols)
+    part = convolved(h0 + h0 + h1, weights, rows, cols)
     total = x_ref[0].astype(jnp.float32) + x_ref[1].astype(jnp.float32) + part
     out_ref[0] = total * 0.5 + b_ref[...]
 
 
-def join_body(rest_ref, near_ref, far_ref, out_ref):
-    rows = rest_ref.shape[1]
-    odd = parity()
-    first = lax.axis_index("tm") == 0
-    for part_ref, start in ((near_ref, 2 * (1 - odd)), (far_ref, odd * (rows - 2))):
-        part = part_ref[...].astype(jnp.float32)
-        part = jnp.where(first, jnp.zeros_like(part), part)
-        place = pl.ds(start, part.shape[0])
-        out_ref[0, place] = (rest_ref[0, place] + 0.5 * part).astype(jnp.bfloat16)
+def join(rest_ref, part_ref, out_ref, start, made_ref, sem):
+    part = part_ref[...].astype(jnp.float32)
+    part = jnp.where(lax.axis_index("tm") == 0, jnp.zeros_like(part), part)
+    place = pl.ds(start, part.shape[0])
+    made_ref[...] = (rest_ref[0, place] + 0.5 * part).astype(jnp.bfloat16)
+    copy = pltpu.make_async_copy(made_ref, out_ref.at[0, place], sem)
+    copy.start()
+    copy.wait()
+
+
+def join_near_body(rest_ref, part_ref, out_ref, made_ref, sem):
+    join(rest_ref, part_ref, out_ref, 2 * (1 - parity()), made_ref, sem)
+
+
+def join_far_body(rest_ref, part_ref, _, out_ref, made_ref, sem):
+    join(rest_ref, part_ref, out_ref, parity() * (rest_ref.shape[1] - 2), made_ref, sem)
 
 
 def block(x, weight_first, bias_first, weight_second, bias_second):
@@ -330,9 +342,9 @@
         scratch=sums(2),
     )
     near_part = lax.ppermute(near_send, "tm", ring)
-    far_send, h0, h1 = call(
+    far_send, last0, last1 = call(
         functools.partial(far_body, tiles, times),
-        [frames(2), frames(wide), frames(wide)],
+        [frames(2), frames(2), frames(2)],
         (earlier, corner, weight_first, weight_second, far0, far1, near0, near1),
         0,
         scratch=sums(2),
@@ -341,10 +353,28 @@
     (rest,) = call(
         rest_body,
         [frames(1, rows, dtype=f32)],
-        (x, h0, h1, weight_second, bias_second),
+        (x, near0, near1, last0, last1, weight_second, bias_second),
         3 * unit * rows,
-    )
-    (pooled,) = call(join_body, [frames(1, rows)], (rest, near_part, far_part), 0)
+        scratch=[pltpu.VMEM((wide, cols, channels), jnp.bfloat16)] * 2,
+    )
+    (pooled,) = call(
+        join_near_body,
+        [frames(1, rows)],
+        (rest, near_part),
+        0,
+        out_specs=[HBM],
+        scratch=[pltpu.VMEM((rows - 2, cols, channels), jnp.bfloat16), pltpu.SemaphoreType.DMA(())],
+    )
+    (pooled,) = call(
+        join_far_body,
+        [frames(1, rows)],
+        (rest, far_part, pooled),
+        0,
+        in_specs=[VMEM, VMEM, HBM],
+        out_specs=[HBM],
+        scratch=[pltpu.VMEM((2, cols, channels), jnp.bfloat16), pltpu.SemaphoreType.DMA(())],
+        aliases={2: 0},
+    )
     return pooled
 
 

time: 38 us -> 36.4 us (0.958)
  waiting for transfers between devices: 12.5 us -> 10.2 us
  Pallas kernels: 9.22 us -> 9.85 us
    ppermute x1, waiting for transfers between devices: 2.3 us -> 0.01 us  [block(): near_part = lax.ppermute(near_send, 'tm', ring)]
    ppermute x1, starting transfers between devices: 1.35 us -> 3.5 us  [block(): near_part = lax.ppermute(near_send, 'tm', ring)]
    ppermute x1, starting transfers between devices: 6.36 us -> 4.28 us  [block(): far_part = lax.ppermute(far_send, 'tm', forward)]
    pallas_call x9 -> x10, Pallas kernels: 9.22 us -> 9.85 us  [call(): pl.pallas_call(body, out_shape=outs, in_specs=in_specs or [VMEM] * len(ar...]
  transfers between devices with their start and end apart: 7 -> 7, of which waited for: 2 -> 1; matrix products, arithmetic and copies ran while one was open for 0% -> 0% of each run, Pallas kernels for 20% -> 25%
where the time goes in v9:
time: 36.4 us; the launch traced here: 36.2 us
  starting transfers between devices  15.9 us (44%)
  waiting for transfers between devices  10.2 us (28%)
  Pallas kernels  9.85 us (27%)
    ppermute x1, waiting for transfers between devices, block(): earlier = lax.ppermute(x, 'tm', ring)  10.2 us
    pallas_call x10, Pallas kernels, call(): pl.pallas_call(body, out_shape=outs, in_specs=in_specs or [VMEM] * len(ar...  9.85 us
    ppermute x1, starting transfers between devices, block(): far_part = lax.ppermute(far_send, 'tm', forward)  4.28 us
    ppermute x1, starting transfers between devices, block(): near_part = lax.ppermute(near_send, 'tm', ring)  3.5 us
    ppermute x1, starting transfers between devices, block(): corner = lax.ppermute(outer_edge, ('tile', 'tm'), diagonal)  2.21 us
    ppermute x1, starting transfers between devices, block(): outer = lax.ppermute(outer_edge, ('clips', 'tile'), outer_full)  2.14 us
    ppermute x1, starting transfers between devices, block(): earlier = lax.ppermute(x, 'tm', ring)  2.11 us
    ppermute x1, starting transfers between devices, block(): inner_corner = lax.ppermute(inner_edge, 'tile', inner_pairs)  1.32 us
  transfers between devices with their start and end apart: 7, of which 1 were waited for; matrix products, arithmetic and copies ran while one was open for 0% of the time, Pallas kernels for 25%

profile of v9, /device:TPU:1, one launch (start us, length us, event | category | flops | bytes accessed | tf_op | source)
XLA Modules:
  0.0 36.2 jit_solution(8299201972982132524)
XLA Ops:
  0.0 0.0 copy-start.2
  0.0 0.0 copy-start
  0.0 2.1 %collective-permute-start = (bf16[2,4,128,256]{3,2,1,0:T(8,128)(2,1)}, bf16[2,4,128,256]{3,2,1,0:T(8,128)(2,1)S(1)}, u32[]{:S(2)}, u32[]{:S(2)}) collective-permute-start(bf16[2,4,128,256]{3,2,1,0:T(8,128)(2,1)} %x_ref.1), channel_id=1, source_target_pairs={{0,1},{1,2},{2,3},{3,0},{4,5},{5,6},{6,7},{7,4},{8,9},{9,10},{10,1... | collective-permute-start | bytes 1572872 | tf_op jit(solution)/shard_map/ppermute | solution.py:295
  2.1 1.1 %shard_map.55 = (bf16[2,4,128,256]{3,2,1,0:T(8,128)(2,1)S(1)}, bf16[2,2,128,256]{3,2,1,0:T(8,128)(2,1)S(1)}, bf16[2,2,128,256]{3,2,1,0:T(8,128)(2,1)S(1)}) custom-call(bf16[2,4,128,256]{3,2,1,0:T(8,128)(2,1)} %x_ref.1), custom_call_target="tpu_custom_call" | custom-call | flops 10000000000 | tf_op jit(solution)/shard_map/pallas_call | solution.py:16
  3.2 2.1 %collective-permute-start.4 = (bf16[2,2,128,256]{3,2,1,0:T(8,128)(2,1)S(1)}, bf16[2,2,128,256]{3,2,1,0:T(8,128)(2,1)S(1)}, u32[]{:S(2)}, u32[]{:S(2)}) collective-permute-start(bf16[2,2,128,256]{3,2,1,0:T(8,128)(2,1)S(1)} %get-tuple-element.28), channel_id=1, source_target_pairs={{4,8},{8,4},{20,24},{24,20},{0,16},{12,28},{16,0},{28,12},{5,9},{9... | collective-permute-start | bytes 786440 | tf_op jit(solution)/shard_map/ppermute | solution.py:305
  5.4 0.4 %collective-permute-start.2 = (bf16[2,2,128,256]{3,2,1,0:T(8,128)(2,1)S(1)}, bf16[2,2,128,256]{3,2,1,0:T(8,128)(2,1)S(1)}, u32[]{:S(2)}, u32[]{:S(2)}) collective-permute-start(bf16[2,2,128,256]{3,2,1,0:T(8,128)(2,1)S(1)} %get-tuple-element.21), channel_id=1, source_target_pairs={{0,4},{8,12},{4,0},{12,8},{1,5},{9,13},{5,1},{13,9},{2,6},{10,14},... | collective-permute-start | bytes 786440 | tf_op jit(solution)/shard_map/ppermute | solution.py:304
  5.8 10.2 %collective-permute-done.m_ref = bf16[2,4,128,256]{3,2,1,0:T(8,128)(2,1)S(1)} collective-permute-done((bf16[2,4,128,256]{3,2,1,0:T(8,128)(2,1)}, bf16[2,4,128,256]{3,2,1,0:T(8,128)(2,1)S(1)}, u32[]{:S(2)}, u32[]{:S(2)}) %collective-permute-start) | collective-permute-done | bytes 524320 | tf_op jit(solution)/shard_map/ppermute | solution.py:295
  16.0 1.3 %collective-permute-start.1 = (bf16[2,2,128,256]{3,2,1,0:T(8,128)(2,1)S(1)}, bf16[2,2,128,256]{3,2,1,0:T(8,128)(2,1)S(1)}, u32[]{:S(2)}, u32[]{:S(2)}) collective-permute-start(bf16[2,2,128,256]{3,2,1,0:T(8,128)(2,1)S(1)} %shard_map.56), channel_id=1, source_target_pairs={{0,4},{8,12},{4,0},{12,8},{1,5},{9,13},{5,1},{13,9},{2,6},{10,14},... | collective-permute-start | bytes 786440 | tf_op jit(solution)/shard_map/ppermute | solution.py:325
  17.3 2.2 %collective-permute-start.3 = (bf16[2,2,128,256]{3,2,1,0:T(8,128)(2,1)S(1)}, bf16[2,2,128,256]{3,2,1,0:T(8,128)(2,1)S(1)}, u32[]{:S(2)}, u32[]{:S(2)}) collective-permute-start(bf16[2,2,128,256]{3,2,1,0:T(8,128)(2,1)S(1)} %get-tuple-element.28), channel_id=1, source_target_pairs={{4,9},{5,10},{6,11},{8,5},{9,6},{10,7},{20,25},{21,26},{22,27},{24... | collective-permute-start | bytes 786440 | tf_op jit(solution)/shard_map/ppermute | solution.py:306
  19.5 0.0 collective-permute-done.4.outer_ref
  19.5 0.0 copy-done.2
  19.6 0.0 copy-done
  19.6 1.1 %shard_map.60 = (f32[2,128,256]{2,1,0:T(8,128)S(1)}, f32[2,128,256]{2,1,0:T(8,128)S(1)}) custom-call(bf16[2,4,128,256]{3,2,1,0:T(8,128)(2,1)S(1)} %get-tuple-element.20.x_ref, bf16[2,2,128,256]{3,2,1,0:T(8,128)(2,1)S(1)} %collective-permute-done.4.outer_ref, bf16[3,3,3,256,256]{4,3,2,1,0:T(8,128)(2,1)S(1)} %copy-done, f32[1,1,256]{2,1,0:T(1,128)S(1)} %bitcast.2), custom_call_target="tpu_custom_call" | custom-call | tf_op jit(solution)/shard_map/pallas_call | solution.py:16
  20.7 0.0 copy-start.1
  20.7 0.0 collective-permute-done.2.inner_ref
  20.7 2.0 %shard_map.57 = (f32[4,128,256]{2,1,0:T(8,128)S(1)}, f32[4,128,256]{2,1,0:T(8,128)S(1)}) custom-call(bf16[2,4,128,256]{3,2,1,0:T(8,128)(2,1)S(1)} %get-tuple-element.20.x_ref, bf16[2,2,128,256]{3,2,1,0:T(8,128)(2,1)S(1)} %collective-permute-done.2.inner_ref, bf16[3,3,3,256,256]{4,3,2,1,0:T(8,128)(2,1)S(1)} %copy-done, f32[1,1,256]{2,1,0:T(1,128)S(1)} %bitcast.3), custom_call_target="tpu_custom_call" | custom-call | flops 1811939328 | tf_op jit(solution)/shard_map/pallas_call | solution.py:16
  22.7 0.0 copy-done.1
  22.7 0.2 shard_map.58
  22.9 0.0 collective-permute-done.1.inner_ref
  22.9 1.0 %shard_map.59 = (bf16[2,128,256]{2,1,0:T(8,128)(2,1)S(1)}, bf16[4,128,256]{2,1,0:T(8,128)(2,1)S(1)}, bf16[4,128,256]{2,1,0:T(8,128)(2,1)S(1)}) custom-call(bf16[2,4,128,256]{3,2,1,0:T(8,128)(2,1)S(1)} %collective-permute-done.m_ref, bf16[2,2,128,256]{3,2,1,0:T(8,128)(2,1)S(1)} %collective-permute-done.1.inner_ref, bf16[3,3,3,256,256]{4,3,2,1,0:T(8,128)(2,1)S(1)} %copy-done, ...), custom_call_target="tpu_custom_call" | custom-call | tf_op jit(solution)/shard_map/pallas_call | solution.py:16
  23.9 3.5 %collective-permute-start.6 = (bf16[2,128,256]{2,1,0:T(8,128)(2,1)S(1)}, bf16[2,128,256]{2,1,0:T(8,128)(2,1)S(1)}, u32[]{:S(2)}, u32[]{:S(2)}) collective-permute-start(bf16[2,128,256]{2,1,0:T(8,128)(2,1)S(1)} %get-tuple-element.34), channel_id=1, source_target_pairs={{0,1},{1,2},{2,3},{3,0},{4,5},{5,6},{6,7},{7,4},{8,9},{9,10},{10,1... | collective-permute-start | bytes 393224 | tf_op jit(solution)/shard_map/ppermute | solution.py:344
  27.4 0.0 collective-permute-done.3.outer_ref
  27.4 0.0 copy-start.3
  27.4 1.0 %shard_map.61 = (bf16[2,128,256]{2,1,0:T(8,128)(2,1)S(1)}, bf16[2,128,256]{2,1,0:T(8,128)(2,1)S(1)}, bf16[2,128,256]{2,1,0:T(8,128)(2,1)S(1)}) custom-call(bf16[2,4,128,256]{3,2,1,0:T(8,128)(2,1)S(1)} %collective-permute-done.m_ref, bf16[2,2,128,256]{3,2,1,0:T(8,128)(2,1)S(1)} %collective-permute-done.3.outer_ref, bf16[3,3,3,256,256]{4,3,2,1,0:T(8,128)(2,1)S(1)} %copy-done, ...), custom_call_target="tpu_custom_call" | custom-call | tf_op jit(solution)/shard_map/pallas_call | solution.py:16
  28.4 4.3 %collective-permute-start.5 = (bf16[2,128,256]{2,1,0:T(8,128)(2,1)S(1)}, bf16[2,128,256]{2,1,0:T(8,128)(2,1)S(1)}, u32[]{:S(2)}, u32[]{:S(2)}) collective-permute-start(bf16[2,128,256]{2,1,0:T(8,128)(2,1)S(1)} %get-tuple-element.33), channel_id=1, source_target_pairs={{0,1},{1,2},{2,3},{4,5},{5,6},{6,7},{8,9},{9,10},{10,11},{12,13},{... | collective-permute-start | bytes 393224 | tf_op jit(solution)/shard_map/ppermute | solution.py:352
  32.7 0.0 copy-done.3
  32.7 2.0 %shard_map.62.rest_ref = f32[1,4,128,256]{3,2,1,0:T(8,128)S(1)} custom-call(bf16[2,4,128,256]{3,2,1,0:T(8,128)(2,1)S(1)} %get-tuple-element.20.x_ref, bf16[4,128,256]{2,1,0:T(8,128)(2,1)S(1)} %get-tuple-element.26.near0_ref, bf16[4,128,256]{2,1,0:T(8,128)(2,1)S(1)} %get-tuple-element.27.near1_ref, bf16[2,128,256]{2,1,0:T(8,128)(2,1)S(1)} %get-tuple-element.31.far0_ref, ...), custom_call_target="tpu_custom_call" | custom-call | flops 1811939328 | tf_op jit(solution)/shard_map/pallas_call | solution.py:16
  34.7 0.0 collective-permute-done.6.part_ref
  34.8 0.7 %shard_map.63._ = bf16[1,4,128,256]{3,2,1,0:T(8,128)(2,1)} custom-call(f32[1,4,128,256]{3,2,1,0:T(8,128)S(1)} %shard_map.62.rest_ref, bf16[2,128,256]{2,1,0:T(8,128)(2,1)S(1)} %collective-permute-done.6.part_ref), custom_call_target="tpu_custom_call" | custom-call | tf_op jit(solution)/shard_map/pallas_call | solution.py:16
  35.5 0.0 collective-permute-done.5.part_ref
  35.5 0.7 %shard_map.64 = bf16[1,4,128,256]{3,2,1,0:T(8,128)(2,1)} custom-call(f32[1,4,128,256]{3,2,1,0:T(8,128)S(1)} %shard_map.62.rest_ref, bf16[2,128,256]{2,1,0:T(8,128)(2,1)S(1)} %collective-permute-done.5.part_ref, bf16[1,4,128,256]{3,2,1,0:T(8,128)(2,1)} %shard_map.63._), custom_call_target="tpu_custom_call", output_to_operand_aliasing={{}: (2, {})} | custom-call | tf_op jit(solution)/shard_map/pallas_call | solution.py:16
  (1 shorter events, 0.0 us)
Async XLA Ops:
  0.0 19.6 %copy-start.2 = (f32[256]{0:T(256)S(1)}, f32[256]{0:T(256)}, u32[]{:S(2)}) copy-start(f32[256]{0:T(256)} %param.7) | copy-start | bytes 3076
  0.0 19.6 %copy-start = (bf16[3,3,3,256,256]{4,3,2,1,0:T(8,128)(2,1)S(1)}, bf16[3,3,3,256,256]{4,3,2,1,0:T(8,128)(2,1)}, u32[]{:S(2)}) copy-start(bf16[3,3,3,256,256]{4,3,2,1,0:T(8,128)(2,1)} %w_ref.9) | copy-start | bytes 10616836
  0.0 16.0 %collective-permute-start = (bf16[2,4,128,256]{3,2,1,0:T(8,128)(2,1)}, bf16[2,4,128,256]{3,2,1,0:T(8,128)(2,1)S(1)}, u32[]{:S(2)}, u32[]{:S(2)}) collective-permute-start(bf16[2,4,128,256]{3,2,1,0:T(8,128)(2,1)} %x_ref.1), channel_id=1, source_target_pairs={{0,1},{1,2},{2,3},{3,0},{4,5},{5,6},{6,7},{7,4},{8,9},{9,10},{10,1... | collective-permute-start | bytes 1572872 | tf_op jit(solution)/shard_map/ppermute | solution.py:295
  3.2 16.3 %collective-permute-start.4 = (bf16[2,2,128,256]{3,2,1,0:T(8,128)(2,1)S(1)}, bf16[2,2,128,256]{3,2,1,0:T(8,128)(2,1)S(1)}, u32[]{:S(2)}, u32[]{:S(2)}) collective-permute-start(bf16[2,2,128,256]{3,2,1,0:T(8,128)(2,1)S(1)} %get-tuple-element.28), channel_id=1, source_target_pairs={{4,8},{8,4},{20,24},{24,20},{0,16},{12,28},{16,0},{28,12},{5,9},{9... | collective-permute-start | bytes 786440 | tf_op jit(solution)/shard_map/ppermute | solution.py:305
  5.4 15.3 %collective-permute-start.2 = (bf16[2,2,128,256]{3,2,1,0:T(8,128)(2,1)S(1)}, bf16[2,2,128,256]{3,2,1,0:T(8,128)(2,1)S(1)}, u32[]{:S(2)}, u32[]{:S(2)}) collective-permute-start(bf16[2,2,128,256]{3,2,1,0:T(8,128)(2,1)S(1)} %get-tuple-element.21), channel_id=1, source_target_pairs={{0,4},{8,12},{4,0},{12,8},{1,5},{9,13},{5,1},{13,9},{2,6},{10,14},... | collective-permute-start | bytes 786440 | tf_op jit(solution)/shard_map/ppermute | solution.py:304
  16.0 6.9 %collective-permute-start.1 = (bf16[2,2,128,256]{3,2,1,0:T(8,128)(2,1)S(1)}, bf16[2,2,128,256]{3,2,1,0:T(8,128)(2,1)S(1)}, u32[]{:S(2)}, u32[]{:S(2)}) collective-permute-start(bf16[2,2,128,256]{3,2,1,0:T(8,128)(2,1)S(1)} %shard_map.56), channel_id=1, source_target_pairs={{0,4},{8,12},{4,0},{12,8},{1,5},{9,13},{5,1},{13,9},{2,6},{10,14},... | collective-permute-start | bytes 786440 | tf_op jit(solution)/shard_map/ppermute | solution.py:325
  17.3 10.1 %collective-permute-start.3 = (bf16[2,2,128,256]{3,2,1,0:T(8,128)(2,1)S(1)}, bf16[2,2,128,256]{3,2,1,0:T(8,128)(2,1)S(1)}, u32[]{:S(2)}, u32[]{:S(2)}) collective-permute-start(bf16[2,2,128,256]{3,2,1,0:T(8,128)(2,1)S(1)} %get-tuple-element.28), channel_id=1, source_target_pairs={{4,9},{5,10},{6,11},{8,5},{9,6},{10,7},{20,25},{21,26},{22,27},{24... | collective-permute-start | bytes 786440 | tf_op jit(solution)/shard_map/ppermute | solution.py:306
  20.7 2.0 %copy-start.1 = (bf16[3,3,3,256,256]{4,3,2,1,0:T(8,128)(2,1)S(1)}, bf16[3,3,3,256,256]{4,3,2,1,0:T(8,128)(2,1)}, u32[]{:S(2)}) copy-start(bf16[3,3,3,256,256]{4,3,2,1,0:T(8,128)(2,1)} %v_ref.5) | copy-start | bytes 10616836
  23.9 10.8 %collective-permute-start.6 = (bf16[2,128,256]{2,1,0:T(8,128)(2,1)S(1)}, bf16[2,128,256]{2,1,0:T(8,128)(2,1)S(1)}, u32[]{:S(2)}, u32[]{:S(2)}) collective-permute-start(bf16[2,128,256]{2,1,0:T(8,128)(2,1)S(1)} %get-tuple-element.34), channel_id=1, source_target_pairs={{0,1},{1,2},{2,3},{3,0},{4,5},{5,6},{6,7},{7,4},{8,9},{9,10},{10,1... | collective-permute-start | bytes 393224 | tf_op jit(solution)/shard_map/ppermute | solution.py:344
  27.4 5.3 %copy-start.3 = (f32[256]{0:T(256)S(1)}, f32[256]{0:T(256)}, u32[]{:S(2)}) copy-start(f32[256]{0:T(256)} %param.9) | copy-start | bytes 3076
  28.4 7.1 %collective-permute-start.5 = (bf16[2,128,256]{2,1,0:T(8,128)(2,1)S(1)}, bf16[2,128,256]{2,1,0:T(8,128)(2,1)S(1)}, u32[]{:S(2)}, u32[]{:S(2)}) collective-permute-start(bf16[2,128,256]{2,1,0:T(8,128)(2,1)S(1)} %get-tuple-element.33), channel_id=1, source_target_pairs={{0,1},{1,2},{2,3},{4,5},{5,6},{6,7},{8,9},{9,10},{10,11},{12,13},{... | collective-permute-start | bytes 393224 | tf_op jit(solution)/shard_map/ppermute | solution.py:352
